TPU v7x, 512 devices: a whole 4x4x16 slice. The times are simulated.
512 devices in a mesh: wide: 64 (over y_lo, z, core), narrow: 8 (over y_hi, x).
Axes of the slice: x: 4, y: 4 (y_hi: 2, y_lo: 2; y = y_hi * 2 + y_lo), z: 16, core: 2. Of those that a mesh axis runs over, the one named last changes fastest.
Arguments:
- tokens: bfloat16 [8192, 2048], P('wide', 'narrow'), may hold values from -6 to 6
- expert_ids: int32 [8192, 6], P('wide'), may hold values from 0 to 63, all different within a row; in each aligned block of 128 rows (0 to 127, 128 to 255, ...) at most 14 rows name the same one
- route_weights: bfloat16 [8192, 6], P('wide'), may hold values from 0.049804688 to 0.5
- w_gate: bfloat16 [64, 1408, 2048], P('wide', 'narrow'), may hold values from -0.125 to 0.125
- w_up: bfloat16 [64, 1408, 2048], P('wide', 'narrow'), may hold values from -0.125 to 0.125
- w_down: bfloat16 [64, 1408, 2048], P('wide', 'narrow'), may hold values from -0.15625 to 0.15625
Outputs:
- mixed: bfloat16 [8192, 2048], P('wide', 'narrow')
Inputs may be any that keep to these rules, and one draw needn't show every extreme that they name: `expert_ids`: within a row the 6 experts differ. Among the 128 tokens of one aligned block, no expert is named more than 14 times, a bound that some block reaches.
All inputs are finite; a program needn't handle non-finite values.
Results may differ from a plain program's by a relative error of at most 0.017.
Values may be sent and summed in bfloat16 or wider, within the bound.
A program may use at most 64 MiB of HBM per device.

v0:
```python
import jax
import jax.numpy as jnp
from jax import lax
from jax.sharding import PartitionSpec as P


def local(tokens, expert_ids, route_weights, w_gate, w_up, w_down):
    tok_rows = expert_ids.shape[0]
    top_count = expert_ids.shape[1]
    local_experts = w_gate.shape[0]
    groups_wide = lax.axis_size("wide")
    experts_all = local_experts * groups_wide
    capacity = 7 * tok_rows * top_count // (6 * experts_all)
    slots_all = experts_all * capacity
    width = w_down.shape[2]
    flat_ids = expert_ids.reshape(-1)
    onehot = (flat_ids[:, None] == jnp.arange(experts_all, dtype=jnp.int32)[None, :]).astype(
        jnp.int32
    )
    running = jnp.cumsum(onehot, axis=0)
    slot_index = jnp.sum(running * onehot, axis=1) - 1
    destination = (flat_ids * capacity + slot_index).reshape(tok_rows, top_count)
    slot_table = (
        destination[:, :, None] == jnp.arange(slots_all, dtype=jnp.int32)[None, None, :]
    ).astype(jnp.float32)
    dispatch = jnp.sum(slot_table, axis=1).astype(jnp.bfloat16)
    whole = lax.all_gather(tokens, "narrow", axis=1, tiled=True)
    outgoing = jnp.einsum("ts,td->sd", dispatch, whole, preferred_element_type=jnp.float32).astype(
        jnp.bfloat16
    )
    received = lax.all_to_all(outgoing, "wide", split_axis=0, concat_axis=0, tiled=True)
    slot_rows = received.reshape(groups_wide, local_experts, capacity, width)
    gate_proj = jnp.einsum("secd,efd->secf", slot_rows, w_gate, preferred_element_type=jnp.float32)
    up_proj = jnp.einsum("secd,efd->secf", slot_rows, w_up, preferred_element_type=jnp.float32)
    hidden = (jax.nn.silu(gate_proj) * up_proj).astype(jnp.bfloat16)
    partial_value = jnp.einsum(
        "secf,efd->secd", hidden, w_down, preferred_element_type=jnp.float32
    ).astype(jnp.bfloat16)
    partial_value = partial_value.reshape(slots_all, width)
    summed = lax.psum_scatter(partial_value, "narrow", scatter_dimension=1, tiled=True).astype(
        jnp.float32
    )
    returned = lax.all_to_all(
        summed.astype(jnp.bfloat16), "wide", split_axis=0, concat_axis=0, tiled=True
    ).astype(summed.dtype)
    picked = returned[destination.reshape(-1)].reshape(tok_rows, top_count, -1)
    mixed = jnp.sum(route_weights.astype(jnp.float32)[:, :, None] * picked, axis=1)
    return mixed.astype(jnp.bfloat16)


def solution(mesh):
    in_specs = (
        P("wide", "narrow"),
        P("wide", None),
        P("wide", None),
        P("wide", "narrow", None),
        P("wide", "narrow", None),
        P("wide", "narrow", None),
    )
    out_specs = P("wide", "narrow")
    return jax.shard_map(local, mesh=mesh, in_specs=in_specs, out_specs=out_specs, check_vma=False)
```

profile of v0, /device:TPU:1, one launch (start us, length us, event | category | flops | bytes accessed | tf_op | source)
XLA Modules:
  0.0 438.2 jit_solution(4259593260769932684)
XLA Ops:
  6.5 0.0 copy-start
  6.5 0.0 reduce-scatter.2.cloned.1.call-start
  6.5 0.9 copy.26
  7.4 0.1 eq.42
  7.5 0.1 eq.38
  7.7 1.8 reduce-window.6
  9.5 0.3 slice_reduce_fusion
  9.8 0.1 fusion.28
  10.0 0.1 sub.9
  10.1 0.1 copy.30
  10.2 0.4 convert_reduce_fusion
  10.6 31.0 %all_gather.3 = bf16[128,2048]{1,0:T(8,128)(2,1)S(1)} all-gather(bf16[128,256]{1,0:T(8,128)(2,1)} %param.6), channel_id=1, replica_groups=mesh['wide'=64,'narrow'=8] {'narrow'}, dimensions={1}, use_global_device_ids=true | all-gather | bytes 589824 | tf_op jit(solution)/shard_map/all_gather | solution.py:27
  41.6 3.0 convolution_convert_fusion
  44.6 6.0 %all_to_all.12 = bf16[64,14,2048]{2,1,0:T(8,128)(2,1)} reshape(bf16[896,2048]{1,0:T(8,128)(2,1)} %convolution_convert_fusion) | data formatting | bytes 7340032 | tf_op jit(solution)/shard_map/all_to_all | solution.py:31
  50.6 0.0 copy-start.3
  50.6 207.4 %all_to_all.18 = bf16[64,14,2048]{2,1,0:T(8,128)(2,1)S(1)} all-to-all(bf16[64,14,2048]{2,1,0:T(8,128)(2,1)} %all_to_all.12), channel_id=1, replica_groups=mesh['wide'=64,'narrow'=8] {'wide'}, dimensions={0} | all-to-all | bytes 7340032 | tf_op jit(solution)/shard_map/all_to_all | solution.py:31
  258.0 0.0 copy-start.1
  258.0 1.9 copy-done.1
  259.9 0.0 copy-done.3
  259.9 0.0 copy-start.4
  259.9 5.1 %fusion.4 = f32[64,1,14,176]{3,0,2,1:T(8,128)} fusion(bf16[64,14,2048]{2,1,0:T(8,128)(2,1)S(1)} %all_to_all.18, bf16[1,176,2048]{2,1,0:T(8,128)(2,1)S(1)} %copy-done.3), kind=kOutput, calls=%fused_computation.9 | convolution fusion | flops 645922816 | bytes 5021696 | tf_op jit(solution)/shard_map/secd,efd->secf/dot_general | solution.py:33
  265.0 0.0 copy-done
  265.0 0.0 copy-done.4
  265.0 8.3 %convert_bitcast_fusion = bf16[64,1,14,2048]{3,0,2,1:T(8,128)(2,1)} fusion(bf16[64,14,2048]{2,1,0:T(8,128)(2,1)} %copy-done.1, f32[64,1,14,176]{3,0,2,1:T(8,128)} %fusion.4, bf16[1,176,2048]{2,1,0:T(8,128)(2,1)S(1)} %copy-done, bf16[1,176,2048]{2,1,0:T(8,128)(2,1)S(1)} %copy-done.4), kind=kOutput, calls=%fused_computation.1 | convolution fusion | flops 1294626816 | bytes 9412608 | tf_op jit(solution)/shard_map/secf,efd->secd/dot_general | solution.py:36
  273.2 6.0 %copy.33 = bf16[64,1,14,2048]{3,2,0,1:T(8,128)(2,1)} copy(bf16[64,1,14,2048]{3,0,2,1:T(8,128)(2,1)} %convert_bitcast_fusion) | data formatting | bytes 7340032 | tf_op jit(solution)/shard_map/convert_element_type | solution.py:38
  279.2 6.0 %reshape.100 = bf16[896,2048]{1,0:T(8,128)(2,1)} reshape(bf16[64,1,14,2048]{3,2,0,1:T(8,128)(2,1)} %copy.33) | data formatting | bytes 7340032 | tf_op jit(solution)/shard_map/reshape | solution.py:39
  285.2 0.0 copy-start.2
  285.2 0.0 reduce-scatter.2.cloned.1.call-update
  285.2 94.2 %reduce-scatter.2.cloned.1.call-done = bf16[896,256]{1,0:T(8,128)(2,1)} async-done(((bf16[896,2048]{1,0:T(8,128)(2,1)}), bf16[896,256]{1,0:T(8,128)(2,1)}) %reduce-scatter.2.cloned.1.call-update) | async-done | bytes 458768 | tf_op jit(solution)/shard_map/reduce_scatter | solution.py:40
  379.5 1.9 all_to_all.14
  381.4 14.9 %all-to-all-start.1 = ((bf16[64,14,256]{2,1,0:T(8,128)(2,1)}), bf16[64,14,256]{2,1,0:T(8,128)(2,1)S(1)}, u32[]{:S(2)}, u32[]{:S(2)}) async-start(bf16[64,14,256]{2,1,0:T(8,128)(2,1)} %all_to_all.14), calls=%async_computation.2 | async-start | bytes 1048576 | tf_op jit(solution)/shard_map/all_to_all | solution.py:43
  396.3 0.0 copy-done.2
  396.4 0.1 copy.25
  396.5 0.1 mul.42
  396.7 31.4 %all-to-all-done.1 = bf16[64,14,256]{2,1,0:T(8,128)(2,1)S(1)} async-done(((bf16[64,14,256]{2,1,0:T(8,128)(2,1)}), bf16[64,14,256]{2,1,0:T(8,128)(2,1)S(1)}, u32[]{:S(2)}, u32[]{:S(2)}) %all-to-all-start.1) | async-done | bytes 458784 | tf_op jit(solution)/shard_map/all_to_all | solution.py:43
  428.0 0.1 reshape.102
  428.1 2.1 gather_fusion
  430.3 0.1 reshape.101
  430.4 1.0 multiply_reduce_fusion
  (6 shorter events, 0.1 us)
Async XLA Ops:
  6.5 258.4 %copy-start = (bf16[1,176,2048]{2,1,0:T(8,128)(2,1)S(1)}, bf16[1,176,2048]{2,1,0:T(8,128)(2,1)}, u32[]{:S(2)}) copy-start(bf16[1,176,2048]{2,1,0:T(8,128)(2,1)} %param.11) | copy-start | bytes 2162692
  6.5 372.9 %reduce-scatter.2.cloned.1.call-start = ((), (), s32[]{:S(2)}) async-start(), calls=%async_computation.3 | async-start | bytes 4128768 | tf_op jit(solution)/shard_map/reduce_scatter | solution.py:40
  50.6 209.3 %copy-start.3 = (bf16[1,176,2048]{2,1,0:T(8,128)(2,1)S(1)}, bf16[1,176,2048]{2,1,0:T(8,128)(2,1)}, u32[]{:S(2)}) copy-start(bf16[1,176,2048]{2,1,0:T(8,128)(2,1)} %param.9) | copy-start | bytes 2162692
  258.0 1.9 copy-start.1
  259.9 5.1 %copy-start.4 = (bf16[1,176,2048]{2,1,0:T(8,128)(2,1)S(1)}, bf16[1,176,2048]{2,1,0:T(8,128)(2,1)}, u32[]{:S(2)}) copy-start(bf16[1,176,2048]{2,1,0:T(8,128)(2,1)} %param.10) | copy-start | bytes 2162692
  285.2 111.2 %copy-start.2 = (bf16[128,6]{0,1:T(8,128)(2,1)S(1)}, bf16[128,6]{0,1:T(8,128)(2,1)}, u32[]{:S(2)}) copy-start(bf16[128,6]{0,1:T(8,128)(2,1)} %param.8) | copy-start | bytes 4612
  381.4 46.6 %all-to-all-start.1 = ((bf16[64,14,256]{2,1,0:T(8,128)(2,1)}), bf16[64,14,256]{2,1,0:T(8,128)(2,1)S(1)}, u32[]{:S(2)}, u32[]{:S(2)}) async-start(bf16[64,14,256]{2,1,0:T(8,128)(2,1)} %all_to_all.14), calls=%async_computation.2 | async-start | bytes 1048576 | tf_op jit(solution)/shard_map/all_to_all | solution.py:43
Sparse Core Ops, SparseCore 0:
  285.3 94.0 reduce-scatter.1
where the time goes:
time: 439 us; the launch traced here: 438 us
  blocking collectives  238 us (54%)
  waiting for transfers between devices  126 us (29%)
  local copies, waits for them, and re-layouts  26 us (6%)
  matrix products  16.3 us (4%)
  starting transfers between devices  14.9 us (3%)
  between operations  13.5 us (3%)
    all_to_all x1, blocking collectives, local(): lax.all_to_all(outgoing, 'wide', split_axis=0, concat_axis=0, tiled=True)  207 us
    reduce_scatter x1, waiting for transfers between devices, local(): lax.psum_scatter(partial_value, 'narrow', scatter_dimension=1, tiled=True)  94.2 us
    all_to_all x1, waiting for transfers between devices, local(): lax.all_to_all(summed.astype(jnp.bfloat16), 'wide', split_axis=0, concat_...  31.4 us
    all_gather x1, blocking collectives, local(): whole = lax.all_gather(tokens, 'narrow', axis=1, tiled=True)  31 us
    all_to_all x1, starting transfers between devices, local(): lax.all_to_all(summed.astype(jnp.bfloat16), 'wide', split_axis=0, concat_...  14.9 us
  transfers between devices with their start and end apart: 2, of which 2 were waited for; matrix products, arithmetic and copies ran while one was open for 0% of the time, Pallas kernels for 0%

commit v1 on v0

v1 whole, which is shorter than its diff:
```python
import jax
import jax.numpy as jnp
from jax import lax
from jax.sharding import PartitionSpec as P


def local(tokens, expert_ids, route_weights, w_gate, w_up, w_down):
    tok_rows = expert_ids.shape[0]
    top_count = expert_ids.shape[1]
    local_experts = w_gate.shape[0]
    groups_wide = lax.axis_size("wide")
    experts_all = local_experts * groups_wide
    capacity = 7 * tok_rows * top_count // (6 * experts_all)
    slots_all = experts_all * capacity
    flat_ids = expert_ids.reshape(-1)
    onehot = (flat_ids[:, None] == jnp.arange(experts_all, dtype=jnp.int32)[None, :]).astype(
        jnp.int32
    )
    running = jnp.cumsum(onehot, axis=0)
    slot_index = jnp.sum(running * onehot, axis=1) - 1
    destination = (flat_ids * capacity + slot_index).reshape(tok_rows, top_count)
    hit = destination[:, :, None] == jnp.arange(slots_all, dtype=jnp.int32)[None, None, :]
    dispatch = jnp.any(hit, axis=1).astype(jnp.bfloat16)
    combine = jnp.sum(
        jnp.where(hit, route_weights.astype(jnp.float32)[:, :, None], 0.0), axis=1
    ).astype(jnp.bfloat16)
    outgoing = jnp.einsum("ts,td->sd", dispatch, tokens, preferred_element_type=jnp.float32).astype(
        jnp.bfloat16
    )
    received = lax.all_to_all(outgoing, "wide", split_axis=0, concat_axis=0, tiled=True)
    slot_rows = lax.all_gather(received, "narrow", axis=1, tiled=True)
    gate_proj = jnp.einsum("sd,fd->sf", slot_rows, w_gate[0], preferred_element_type=jnp.float32)
    up_proj = jnp.einsum("sd,fd->sf", slot_rows, w_up[0], preferred_element_type=jnp.float32)
    hidden = (jax.nn.silu(gate_proj) * up_proj).astype(jnp.bfloat16)
    partial_value = jnp.einsum(
        "sf,fd->sd", hidden, w_down[0], preferred_element_type=jnp.float32
    ).astype(jnp.bfloat16)
    summed = lax.psum_scatter(partial_value, "narrow", scatter_dimension=1, tiled=True)
    returned = lax.all_to_all(summed, "wide", split_axis=0, concat_axis=0, tiled=True)
    mixed = jnp.einsum("ts,sd->td", combine, returned, preferred_element_type=jnp.float32)
    return mixed.astype(jnp.bfloat16)


def solution(mesh):
    in_specs = (
        P("wide", "narrow"),
        P("wide", None),
        P("wide", None),
        P("wide", "narrow", None),
        P("wide", "narrow", None),
        P("wide", "narrow", None),
    )
    out_specs = P("wide", "narrow")
    return jax.shard_map(local, mesh=mesh, in_specs=in_specs, out_specs=out_specs, check_vma=False)
```

time: 439 us -> 308 us (0.70)
  blocking collectives: 238 us -> 49.6 us
  waiting for transfers between devices: 126 us -> 209 us
  local copies, waits for them, and re-layouts: 26 us -> 4.76 us
  matrix products: 16.3 us -> 11.9 us
    all_to_all x1, blocking collectives: 207 us -> 49.6 us  [local(): lax.all_to_all(outgoing, 'wide', split_axis=0, concat_axis=0, tiled=True)]
    all_gather x0 -> x1, waiting for transfers between devices: none -> 81.2 us  [local(): slot_rows = lax.all_gather(received, 'narrow', axis=1, tiled=True)]
    all_gather x1 -> x0, blocking collectives: 31 us -> none  [local(): whole = lax.all_gather(tokens, 'narrow', axis=1, tiled=True)]
    convert_element_type x3 -> x0, local copies, waits for them, and re-layouts: 6.22 us -> none  [the longest x1 5.99 us: local(): partial_value = jnp.einsum('secf,efd->secd', hidden, w_down, preferred_el...]
    reshape x2 -> x0, local copies, waits for them, and re-layouts: 6.06 us -> none  [the longest x1 5.95 us: local(): partial_value = partial_value.reshape(slots_all, width)]
    all_to_all x1 -> x2, local copies, waits for them, and re-layouts: 6 us -> 1.04 us  [local(): lax.all_to_all(outgoing, 'wide', split_axis=0, concat_axis=0, tiled=True)]
    dot_general x3 -> x4, matrix products: 16.3 us -> 11.9 us  [the longest x1 6.47 us: local(): jnp.einsum('sf,fd->sd', hidden, w_down[0], preferred_element_type=jnp.flo...]
  transfers between devices with their start and end apart: 2 -> 3, of which waited for: 2 -> 3; matrix products, arithmetic and copies ran while one was open for 0% -> 0% of each run, Pallas kernels for 0% -> 0%
where the time goes in v1:
time: 308 us; the launch traced here: 307 us
  waiting for transfers between devices  209 us (68%)
  blocking collectives  49.6 us (16%)
  starting transfers between devices  15 us (5%)
  between operations  13.5 us (4%)
  matrix products  11.9 us (4%)
  local copies, waits for them, and re-layouts  4.76 us (2%)
  other arithmetic  3.48 us (1%)
    reduce_scatter x1, waiting for transfers between devices, local(): lax.psum_scatter(partial_value, 'narrow', scatter_dimension=1, tiled=True)  96.4 us
    all_gather x1, waiting for transfers between devices, local(): slot_rows = lax.all_gather(received, 'narrow', axis=1, tiled=True)  81.2 us
    all_to_all x1, blocking collectives, local(): lax.all_to_all(outgoing, 'wide', split_axis=0, concat_axis=0, tiled=True)  49.6 us
    all_to_all x1, waiting for transfers between devices, local(): lax.all_to_all(summed, 'wide', split_axis=0, concat_axis=0, tiled=True)  31.3 us
    all_to_all x1, starting transfers between devices, local(): lax.all_to_all(summed, 'wide', split_axis=0, concat_axis=0, tiled=True)  14.9 us
    dot_general x1, matrix products, local(): jnp.einsum('sf,fd->sd', hidden, w_down[0], preferred_element_type=jnp.flo...  6.47 us
  transfers between devices with their start and end apart: 3, of which 3 were waited for; matrix products, arithmetic and copies ran while one was open for 0% of the time, Pallas kernels for 0%

profile of v1, /device:TPU:1, one launch (start us, length us, event | category | flops | bytes accessed | tf_op | source)
XLA Modules:
  0.0 307.2 jit_solution(4234591035933541755)
XLA Ops:
  6.5 0.0 copy-start
  6.5 0.0 copy-start.2
  6.5 0.0 all-gather.2.cloned.1.call-start
  6.5 0.9 copy.21
  7.4 0.1 eq.42
  7.6 0.1 eq.38
  7.7 1.8 reduce-window.6
  9.5 0.3 slice_reduce_fusion
  9.8 0.1 fusion.15
  10.0 0.1 sub.7
  10.1 0.1 copy.24
  10.2 0.7 multiply_add_fusion
  10.9 0.4 fusion
  11.4 1.2 convolution_convert_fusion.1
  12.5 0.1 all_to_all.16
  12.7 49.6 %all_to_all.24 = bf16[64,14,256]{2,1,0:T(8,128)(2,1)S(1)} all-to-all(bf16[64,14,256]{2,1,0:T(8,128)(2,1)S(1)} %all_to_all.16), channel_id=1, replica_groups=mesh['wide'=64,'narrow'=8] {'wide'}, dimensions={0} | all-to-all | bytes 917504 | tf_op jit(solution)/shard_map/all_to_all | solution.py:30
  62.3 0.0 copy-start.3
  62.3 0.9 all_to_all.18
  63.2 0.0 all-gather.2.cloned.1.call-update
  63.3 0.0 reduce-scatter.2.cloned.1.call-start
  63.3 81.2 %all-gather.2.cloned.1.call-done = bf16[896,2048]{1,0:T(8,128)(2,1)} async-done(((bf16[896,256]{1,0:T(8,128)(2,1)}), bf16[896,2048]{1,0:T(8,128)(2,1)}) %all-gather.2.cloned.1.call-update) | async-done | bytes 3670032 | tf_op jit(solution)/shard_map/all_gather | solution.py:31
  144.5 0.0 copy-done.2
  144.5 3.4 %fusion.5 = f32[896,176]{0,1:T(8,128)S(1)} fusion(bf16[896,2048]{1,0:T(8,128)(2,1)} %all-gather.2.cloned.1.call-done, bf16[1,176,2048]{2,1,0:T(8,128)(2,1)S(1)} %copy-done.2), kind=kOutput, calls=%fused_computation.10 | convolution fusion | flops 645922816 | bytes 5021696 | tf_op jit(solution)/shard_map/sd,fd->sf/dot_general | solution.py:32
  147.9 0.0 copy-done
  147.9 0.0 copy-done.3
  147.9 6.5 %convolution_convert_fusion = bf16[896,2048]{1,0:T(8,128)(2,1)} fusion(bf16[896,2048]{1,0:T(8,128)(2,1)} %all-gather.2.cloned.1.call-done, bf16[1,176,2048]{2,1,0:T(8,128)(2,1)S(1)} %copy-done, bf16[1,176,2048]{2,1,0:T(8,128)(2,1)S(1)} %copy-done.3, f32[896,176]{0,1:T(8,128)S(1)} %fusion.5), kind=kOutput, calls=%fused_computation | convolution fusion | flops 1294626816 | bytes 9412608 | tf_op jit(solution)/shard_map/sf,fd->sd/dot_general | solution.py:35
  154.4 0.0 copy-start.1
  154.4 0.0 reduce-scatter.2.cloned.1.call-update
  154.4 96.4 %reduce-scatter.2.cloned.1.call-done = bf16[896,256]{1,0:T(8,128)(2,1)} async-done(((bf16[896,2048]{1,0:T(8,128)(2,1)}), bf16[896,256]{1,0:T(8,128)(2,1)}) %reduce-scatter.2.cloned.1.call-update) | async-done | bytes 458768 | tf_op jit(solution)/shard_map/reduce_scatter | solution.py:38
  250.8 1.9 all_to_all.19
  252.7 14.9 %all-to-all-start.1 = ((bf16[64,14,256]{2,1,0:T(8,128)(2,1)}), bf16[64,14,256]{2,1,0:T(8,128)(2,1)S(1)}, u32[]{:S(2)}, u32[]{:S(2)}) async-start(bf16[64,14,256]{2,1,0:T(8,128)(2,1)} %all_to_all.19), calls=%async_computation.2 | async-start | bytes 1048576 | tf_op jit(solution)/shard_map/all_to_all | solution.py:39
  267.7 0.0 copy-done.1
  267.7 0.3 select_reduce_fusion
  268.1 31.3 %all-to-all-done.1 = bf16[64,14,256]{2,1,0:T(8,128)(2,1)S(1)} async-done(((bf16[64,14,256]{2,1,0:T(8,128)(2,1)}), bf16[64,14,256]{2,1,0:T(8,128)(2,1)S(1)}, u32[]{:S(2)}, u32[]{:S(2)}) %all-to-all-start.1) | async-done | bytes 458784 | tf_op jit(solution)/shard_map/all_to_all | solution.py:39
  299.4 0.1 all_to_all.21
  299.5 0.9 convolution_convert_fusion.2
  (4 shorter events, 0.0 us)
Async XLA Ops:
  6.5 141.4 %copy-start = (bf16[1,176,2048]{2,1,0:T(8,128)(2,1)S(1)}, bf16[1,176,2048]{2,1,0:T(8,128)(2,1)}, u32[]{:S(2)}) copy-start(bf16[1,176,2048]{2,1,0:T(8,128)(2,1)} %param.11) | copy-start | bytes 2162692
  6.5 138.0 %copy-start.2 = (bf16[1,176,2048]{2,1,0:T(8,128)(2,1)S(1)}, bf16[1,176,2048]{2,1,0:T(8,128)(2,1)}, u32[]{:S(2)}) copy-start(bf16[1,176,2048]{2,1,0:T(8,128)(2,1)} %param.9) | copy-start | bytes 2162692
  6.5 138.0 %all-gather.2.cloned.1.call-start = ((), (), s32[]{:S(2)}) async-start(), calls=%async_computation.3 | async-start | bytes 4128768 | tf_op jit(solution)/shard_map/all_gather | solution.py:31
  62.3 85.6 %copy-start.3 = (bf16[1,176,2048]{2,1,0:T(8,128)(2,1)S(1)}, bf16[1,176,2048]{2,1,0:T(8,128)(2,1)}, u32[]{:S(2)}) copy-start(bf16[1,176,2048]{2,1,0:T(8,128)(2,1)} %param.10) | copy-start | bytes 2162692
  63.3 187.5 %reduce-scatter.2.cloned.1.call-start = ((), (), s32[]{:S(2)}) async-start(), calls=%async_computation.4 | async-start | bytes 4128768 | tf_op jit(solution)/shard_map/reduce_scatter | solution.py:38
  154.4 113.3 %copy-start.1 = (bf16[128,6]{0,1:T(8,128)(2,1)S(1)}, bf16[128,6]{0,1:T(8,128)(2,1)}, u32[]{:S(2)}) copy-start(bf16[128,6]{0,1:T(8,128)(2,1)} %param.8) | copy-start | bytes 4612
  252.7 46.6 %all-to-all-start.1 = ((bf16[64,14,256]{2,1,0:T(8,128)(2,1)}), bf16[64,14,256]{2,1,0:T(8,128)(2,1)S(1)}, u32[]{:S(2)}, u32[]{:S(2)}) async-start(bf16[64,14,256]{2,1,0:T(8,128)(2,1)} %all_to_all.19), calls=%async_computation.2 | async-start | bytes 1048576 | tf_op jit(solution)/shard_map/all_to_all | solution.py:39
Sparse Core Ops, SparseCore 0:
  63.4 81.0 all-gather.1
  154.5 96.2 reduce-scatter.1

commit v2 on v1

--- a/solution.py
+++ b/solution.py
@@ -1,7 +1,72 @@
 import jax
 import jax.numpy as jnp
 from jax import lax
+from jax.experimental import pallas as pl
+from jax.experimental.pallas import tpu as pltpu
 from jax.sharding import PartitionSpec as P
+
+MESH = pl.DeviceIdType.MESH
+
+
+def _exchange_kernel(n_peers, pick_src, x_ref, y_ref, send_sem, recv_sem, own_sem):
+    me = lax.axis_index("narrow")
+    w = lax.axis_index("wide")
+    barrier = pltpu.get_barrier_semaphore()
+    for k in range(1, n_peers):
+        peer = lax.rem(me + k, n_peers)
+        pl.semaphore_signal(barrier, inc=1, device_id=(w, peer), device_id_type=MESH)
+    pl.semaphore_wait(barrier, n_peers - 1)
+    own = pltpu.make_async_copy(pick_src(x_ref, me), y_ref.at[me], own_sem)
+    own.start()
+    copies = []
+    for k in range(1, n_peers):
+        peer = lax.rem(me + k, n_peers)
+        c = pltpu.make_async_remote_copy(
+            src_ref=pick_src(x_ref, peer),
+            dst_ref=y_ref.at[me],
+            send_sem=send_sem.at[k - 1],
+            recv_sem=recv_sem.at[k - 1],
+            device_id=(w, peer),
+            device_id_type=MESH,
+        )
+        c.start()
+        copies.append(c)
+    for k in range(1, n_peers):
+        src = lax.rem(me + n_peers - k, n_peers)
+        pltpu.make_async_remote_copy(
+            src_ref=pick_src(x_ref, src),
+            dst_ref=y_ref.at[src],
+            send_sem=send_sem.at[k - 1],
+            recv_sem=recv_sem.at[k - 1],
+            device_id=(w, src),
+            device_id_type=MESH,
+        ).wait_recv()
+    for c in copies:
+        c.wait_send()
+    own.wait()
+
+
+def _exchange(x, n_peers, gather, collective_id):
+    if gather:
+        out_shape = (n_peers,) + x.shape
+        pick_src = lambda ref, i: ref
+    else:
+        out_shape = x.shape
+        pick_src = lambda ref, i: ref.at[i]
+    nbytes = x.size * x.dtype.itemsize
+    return pl.pallas_call(
+        lambda *refs: _exchange_kernel(n_peers, pick_src, *refs),
+        out_shape=jax.ShapeDtypeStruct(out_shape, x.dtype),
+        in_specs=[pl.BlockSpec(memory_space=pl.ANY)],
+        out_specs=pl.BlockSpec(memory_space=pl.ANY),
+        scratch_shapes=[
+            pltpu.SemaphoreType.DMA((n_peers - 1,)),
+            pltpu.SemaphoreType.DMA((n_peers - 1,)),
+            pltpu.SemaphoreType.DMA(()),
+        ],
+        compiler_params=pltpu.CompilerParams(collective_id=collective_id, has_side_effects=True),
+        cost_estimate=pl.CostEstimate(flops=0, bytes_accessed=2 * nbytes, transcendentals=0),
+    )(x)
 
 
 def local(tokens, expert_ids, route_weights, w_gate, w_up, w_down):
@@ -28,14 +93,20 @@
         jnp.bfloat16
     )
     received = lax.all_to_all(outgoing, "wide", split_axis=0, concat_axis=0, tiled=True)
-    slot_rows = lax.all_gather(received, "narrow", axis=1, tiled=True)
-    gate_proj = jnp.einsum("sd,fd->sf", slot_rows, w_gate[0], preferred_element_type=jnp.float32)
-    up_proj = jnp.einsum("sd,fd->sf", slot_rows, w_up[0], preferred_element_type=jnp.float32)
+    n_narrow = lax.axis_size("narrow")
+    width = tokens.shape[1]
+    slot_rows = _exchange(received, n_narrow, True, 0)
+    wg = w_gate[0].reshape(-1, n_narrow, width)
+    wu = w_up[0].reshape(-1, n_narrow, width)
+    wd = w_down[0].reshape(-1, n_narrow, width)
+    gate_proj = jnp.einsum("nsd,fnd->sf", slot_rows, wg, preferred_element_type=jnp.float32)
+    up_proj = jnp.einsum("nsd,fnd->sf", slot_rows, wu, preferred_element_type=jnp.float32)
     hidden = (jax.nn.silu(gate_proj) * up_proj).astype(jnp.bfloat16)
     partial_value = jnp.einsum(
-        "sf,fd->sd", hidden, w_down[0], preferred_element_type=jnp.float32
+        "sf,fnd->nsd", hidden, wd, preferred_element_type=jnp.float32
     ).astype(jnp.bfloat16)
-    summed = lax.psum_scatter(partial_value, "narrow", scatter_dimension=1, tiled=True)
+    parts = _exchange(partial_value, n_narrow, False, 1)
+    summed = jnp.sum(parts.astype(jnp.float32), axis=0).astype(jnp.bfloat16)
     returned = lax.all_to_all(summed, "wide", split_axis=0, concat_axis=0, tiled=True)
     mixed = jnp.einsum("ts,sd->td", combine, returned, preferred_element_type=jnp.float32)
     return mixed.astype(jnp.bfloat16)

time: 308 us -> 237 us (0.77)
  waiting for transfers between devices: 209 us -> 62.4 us
  Pallas kernels: 0 us -> 126 us
  blocking collectives: 49.6 us -> 0 us
  between operations: 13.5 us -> 0.21 us
  starting transfers between devices: 15 us -> 25.7 us
    pallas_call x0 -> x2, Pallas kernels: none -> 126 us  [_exchange(): pl.pallas_call(lambda *refs: _exchange_kernel(n_peers, pick_src, *refs),...]
    reduce_scatter x1 -> x0, waiting for transfers between devices: 96.4 us -> none  [local(): lax.psum_scatter(partial_value, 'narrow', scatter_dimension=1, tiled=True)]
    all_gather x1 -> x0, waiting for transfers between devices: 81.2 us -> none  [local(): slot_rows = lax.all_gather(received, 'narrow', axis=1, tiled=True)]
    all_to_all x1 -> x0, blocking collectives: 49.6 us -> none  [local(): lax.all_to_all(outgoing, 'wide', split_axis=0, concat_axis=0, tiled=True)]
    all_to_all x0 -> x1, waiting for transfers between devices: none -> 31.1 us  [local(): lax.all_to_all(outgoing, 'wide', split_axis=0, concat_axis=0, tiled=True)]
    all_to_all x0 -> x1, starting transfers between devices: none -> 18.2 us  [local(): lax.all_to_all(outgoing, 'wide', split_axis=0, concat_axis=0, tiled=True)]
    all_to_all x1, starting transfers between devices: 14.9 us -> 7.56 us  [local(): lax.all_to_all(summed, 'wide', split_axis=0, concat_axis=0, tiled=True)]
  transfers between devices with their start and end apart: 3 -> 2, of which waited for: 3 -> 2; matrix products, arithmetic and copies ran while one was open for 0% -> 0% of each run, Pallas kernels for 0% -> 0%
where the time goes in v2:
time: 237 us
  Pallas kernels  126 us (53%)
  waiting for transfers between devices  62.4 us (26%)
  starting transfers between devices  25.7 us (11%)
  matrix products  11 us (5%)
  other arithmetic  6.26 us (3%)
  local copies, waits for them, and re-layouts  5.1 us (2%)
    pallas_call x2, Pallas kernels, _exchange(): pl.pallas_call(lambda *refs: _exchange_kernel(n_peers, pick_src, *refs),...  126 us
    all_to_all x1, waiting for transfers between devices, local(): lax.all_to_all(summed, 'wide', split_axis=0, concat_axis=0, tiled=True)  31.3 us
    all_to_all x1, waiting for transfers between devices, local(): lax.all_to_all(outgoing, 'wide', split_axis=0, concat_axis=0, tiled=True)  31.1 us
    all_to_all x1, starting transfers between devices, local(): lax.all_to_all(outgoing, 'wide', split_axis=0, concat_axis=0, tiled=True)  18.2 us
    all_to_all x1, starting transfers between devices, local(): lax.all_to_all(summed, 'wide', split_axis=0, concat_axis=0, tiled=True)  7.56 us
    dot_general x1, matrix products, local(): jnp.einsum('sf,fnd->nsd', hidden, wd, preferred_element_type=jnp.float32)  6.44 us
  transfers between devices with their start and end apart: 2, of which 2 were waited for; matrix products, arithmetic and copies ran while one was open for 0% of the time, Pallas kernels for 0%

profile of v2, /device:TPU:1, one launch (start us, length us, event | category | flops | bytes accessed | tf_op | source)
XLA Modules:
  0.0 236.8 jit_solution(4020877763756662456)
XLA Ops:
  0.0 0.0 copy-start
  0.0 0.0 copy-start.1
  0.0 0.0 copy-start.2
  0.0 0.0 copy-start.3
  0.0 0.9 copy.28
  1.0 0.1 eq.42
  1.1 0.1 eq.38
  1.3 1.8 reduce-window.6
  3.1 0.3 slice_reduce_fusion
  3.4 0.1 fusion.16
  3.5 0.1 sub.7
  3.7 0.1 copy.31
  3.7 0.7 multiply_add_fusion
  4.4 0.4 fusion
  4.9 0.0 copy-done
  4.9 0.3 convolution_convert_fusion
  5.2 0.9 all_to_all.15
  6.1 18.2 %all-to-all-start = ((bf16[64,14,256]{2,1,0:T(8,128)(2,1)}), bf16[64,14,256]{2,1,0:T(8,128)(2,1)S(1)}, u32[]{:S(2)}, u32[]{:S(2)}) async-start(bf16[64,14,256]{2,1,0:T(8,128)(2,1)} %all_to_all.15), calls=%async_computation | async-start | bytes 1048576 | tf_op jit(solution)/shard_map/all_to_all | solution.py:95
  24.3 0.0 copy-done.1
  24.3 0.2 copy.36
  24.5 0.0 copy-done.2
  24.5 0.2 copy.37
  24.7 0.0 copy-done.3
  24.7 0.2 copy.38
  24.9 31.1 %all-to-all-done = bf16[64,14,256]{2,1,0:T(8,128)(2,1)S(1)} async-done(((bf16[64,14,256]{2,1,0:T(8,128)(2,1)}), bf16[64,14,256]{2,1,0:T(8,128)(2,1)S(1)}, u32[]{:S(2)}, u32[]{:S(2)}) %all-to-all-start) | async-done | bytes 458784 | tf_op jit(solution)/shard_map/all_to_all | solution.py:95
  56.0 0.9 all_to_all.17.refs_0_
  56.9 63.2 %shard_map.64 = bf16[8,896,256]{2,1,0:T(8,128)(2,1)} custom-call(bf16[896,256]{1,0:T(8,128)(2,1)} %all_to_all.17.refs_0_), custom_call_target="tpu_custom_call" | custom-call | bytes 917504 | tf_op jit(solution)/shard_map/pallas_call | solution.py:57
  120.1 3.4 %convolution_bitcast_fusion.1 = f32[896,176]{0,1:T(8,128)S(1)} fusion(bf16[8,896,256]{2,1,0:T(8,128)(2,1)} %shard_map.64, bf16[176,8,256]{2,1,0:T(8,128)(2,1)S(1)} %bitcast.54), kind=kOutput, calls=%fused_computation.7 | convolution fusion | flops 645922816 | bytes 5021696 | tf_op jit(solution)/shard_map/nsd,fnd->sf/dot_general | solution.py:102
  123.5 6.4 %convert_bitcast_fusion.refs_0_ = bf16[8,896,256]{2,1,0:T(8,128)(2,1)} fusion(bf16[8,896,256]{2,1,0:T(8,128)(2,1)} %shard_map.64, bf16[176,8,256]{2,1,0:T(8,128)(2,1)S(1)} %bitcast.53, bf16[176,8,256]{2,1,0:T(8,128)(2,1)S(1)} %bitcast.52, f32[896,176]{0,1:T(8,128)S(1)} %convolution_bitcast_fusion.1), kind=kOutput, calls=%fused_computation | convolution fusion | flops 1294626816 | bytes 9412608 | tf_op jit(solution)/shard_map/sf,fnd->nsd/dot_general | solution.py:105
  129.9 62.8 %shard_map.65 = bf16[8,896,256]{2,1,0:T(8,128)(2,1)} custom-call(bf16[8,896,256]{2,1,0:T(8,128)(2,1)} %convert_bitcast_fusion.refs_0_), custom_call_target="tpu_custom_call" | custom-call | bytes 7340032 | tf_op jit(solution)/shard_map/pallas_call | solution.py:57
  192.8 0.0 copy-start.4
  192.8 2.8 %reduce_sum.32 = bf16[896,256]{1,0:T(8,128)(2,1)S(1)} reduce(bf16[8,896,256]{2,1,0:T(8,128)(2,1)} %shard_map.65, bf16[]{:T(256)} %constant.19.clone.1), dimensions={0}, to_apply=%region_5.6 | reduce | flops 1605632 | bytes 4128770 | tf_op jit(solution)/shard_map/reduce_sum | solution.py:109
  195.6 0.9 all_to_all.18
  196.5 7.6 %all-to-all-start.1 = ((bf16[64,14,256]{2,1,0:T(8,128)(2,1)}), bf16[64,14,256]{2,1,0:T(8,128)(2,1)S(1)}, u32[]{:S(2)}, u32[]{:S(2)}) async-start(bf16[64,14,256]{2,1,0:T(8,128)(2,1)} %all_to_all.18), calls=%async_computation.1 | async-start | bytes 1048576 | tf_op jit(solution)/shard_map/all_to_all | solution.py:110
  204.1 0.0 copy-done.4
  204.1 0.3 select_reduce_fusion
  204.4 31.3 %all-to-all-done.1 = bf16[64,14,256]{2,1,0:T(8,128)(2,1)S(1)} async-done(((bf16[64,14,256]{2,1,0:T(8,128)(2,1)}), bf16[64,14,256]{2,1,0:T(8,128)(2,1)S(1)}, u32[]{:S(2)}, u32[]{:S(2)}) %all-to-all-start.1) | async-done | bytes 458784 | tf_op jit(solution)/shard_map/all_to_all | solution.py:110
  235.8 0.1 all_to_all.20
  235.9 0.9 convolution_convert_fusion.1
  (4 shorter events, 0.0 us)
Async XLA Ops:
  0.0 4.9 %copy-start = (bf16[128,256]{1,0:T(8,128)(2,1)S(1)}, bf16[128,256]{1,0:T(8,128)(2,1)}, u32[]{:S(2)}) copy-start(bf16[128,256]{1,0:T(8,128)(2,1)} %param.6) | copy-start | bytes 196612
  0.0 24.3 %copy-start.1 = (bf16[1,176,2048]{2,1,0:T(8,128)(2,1)S(1)}, bf16[1,176,2048]{2,1,0:T(8,128)(2,1)}, u32[]{:S(2)}) copy-start(bf16[1,176,2048]{2,1,0:T(8,128)(2,1)} %param.9) | copy-start | bytes 2162692
  0.0 24.5 %copy-start.2 = (bf16[1,176,2048]{2,1,0:T(8,128)(2,1)S(1)}, bf16[1,176,2048]{2,1,0:T(8,128)(2,1)}, u32[]{:S(2)}) copy-start(bf16[1,176,2048]{2,1,0:T(8,128)(2,1)} %param.10) | copy-start | bytes 2162692
  0.0 24.7 %copy-start.3 = (bf16[1,176,2048]{2,1,0:T(8,128)(2,1)S(1)}, bf16[1,176,2048]{2,1,0:T(8,128)(2,1)}, u32[]{:S(2)}) copy-start(bf16[1,176,2048]{2,1,0:T(8,128)(2,1)} %param.11) | copy-start | bytes 2162692
  6.1 49.8 %all-to-all-start = ((bf16[64,14,256]{2,1,0:T(8,128)(2,1)}), bf16[64,14,256]{2,1,0:T(8,128)(2,1)S(1)}, u32[]{:S(2)}, u32[]{:S(2)}) async-start(bf16[64,14,256]{2,1,0:T(8,128)(2,1)} %all_to_all.15), calls=%async_computation | async-start | bytes 1048576 | tf_op jit(solution)/shard_map/all_to_all | solution.py:95
  192.8 11.3 %copy-start.4 = (bf16[128,6]{0,1:T(8,128)(2,1)S(1)}, bf16[128,6]{0,1:T(8,128)(2,1)}, u32[]{:S(2)}) copy-start(bf16[128,6]{0,1:T(8,128)(2,1)} %param.8) | copy-start | bytes 4612
  196.5 39.2 %all-to-all-start.1 = ((bf16[64,14,256]{2,1,0:T(8,128)(2,1)}), bf16[64,14,256]{2,1,0:T(8,128)(2,1)S(1)}, u32[]{:S(2)}, u32[]{:S(2)}) async-start(bf16[64,14,256]{2,1,0:T(8,128)(2,1)} %all_to_all.18), calls=%async_computation.1 | async-start | bytes 1048576 | tf_op jit(solution)/shard_map/all_to_all | solution.py:110

commit v3 on v2

--- a/solution.py
+++ b/solution.py
@@ -8,13 +8,17 @@
 MESH = pl.DeviceIdType.MESH
 
 
-def _exchange_kernel(n_peers, pick_src, x_ref, y_ref, send_sem, recv_sem, own_sem):
-    me = lax.axis_index("narrow")
-    w = lax.axis_index("wide")
+def _exchange_kernel(n_peers, pick_src, axis, x_ref, y_ref, send_sem, recv_sem, own_sem):
+    me = lax.axis_index(axis)
+    other = lax.axis_index("wide" if axis == "narrow" else "narrow")
+    if axis == "narrow":
+        dev = lambda p: (other, p)
+    else:
+        dev = lambda p: (p, other)
     barrier = pltpu.get_barrier_semaphore()
     for k in range(1, n_peers):
         peer = lax.rem(me + k, n_peers)
-        pl.semaphore_signal(barrier, inc=1, device_id=(w, peer), device_id_type=MESH)
+        pl.semaphore_signal(barrier, inc=1, device_id=dev(peer), device_id_type=MESH)
     pl.semaphore_wait(barrier, n_peers - 1)
     own = pltpu.make_async_copy(pick_src(x_ref, me), y_ref.at[me], own_sem)
     own.start()
@@ -26,7 +30,7 @@
             dst_ref=y_ref.at[me],
             send_sem=send_sem.at[k - 1],
             recv_sem=recv_sem.at[k - 1],
-            device_id=(w, peer),
+            device_id=dev(peer),
             device_id_type=MESH,
         )
         c.start()
@@ -38,7 +42,7 @@
             dst_ref=y_ref.at[src],
             send_sem=send_sem.at[k - 1],
             recv_sem=recv_sem.at[k - 1],
-            device_id=(w, src),
+            device_id=dev(src),
             device_id_type=MESH,
         ).wait_recv()
     for c in copies:
@@ -46,7 +50,7 @@
     own.wait()
 
 
-def _exchange(x, n_peers, gather, collective_id):
+def _exchange(x, n_peers, gather, collective_id, axis="narrow"):
     if gather:
         out_shape = (n_peers,) + x.shape
         pick_src = lambda ref, i: ref
@@ -55,7 +59,7 @@
         pick_src = lambda ref, i: ref.at[i]
     nbytes = x.size * x.dtype.itemsize
     return pl.pallas_call(
-        lambda *refs: _exchange_kernel(n_peers, pick_src, *refs),
+        lambda *refs: _exchange_kernel(n_peers, pick_src, axis, *refs),
         out_shape=jax.ShapeDtypeStruct(out_shape, x.dtype),
         in_specs=[pl.BlockSpec(memory_space=pl.ANY)],
         out_specs=pl.BlockSpec(memory_space=pl.ANY),
@@ -92,7 +96,8 @@
     outgoing = jnp.einsum("ts,td->sd", dispatch, tokens, preferred_element_type=jnp.float32).astype(
         jnp.bfloat16
     )
-    received = lax.all_to_all(outgoing, "wide", split_axis=0, concat_axis=0, tiled=True)
+    received = _exchange(outgoing.reshape(groups_wide, capacity, -1), groups_wide, False, 2, "wide")
+    received = received.reshape(slots_all, -1)
     n_narrow = lax.axis_size("narrow")
     width = tokens.shape[1]
     slot_rows = _exchange(received, n_narrow, True, 0)
@@ -107,7 +112,8 @@
     ).astype(jnp.bfloat16)
     parts = _exchange(partial_value, n_narrow, False, 1)
     summed = jnp.sum(parts.astype(jnp.float32), axis=0).astype(jnp.bfloat16)
-    returned = lax.all_to_all(summed, "wide", split_axis=0, concat_axis=0, tiled=True)
+    returned = _exchange(summed.reshape(groups_wide, capacity, -1), groups_wide, False, 3, "wide")
+    returned = returned.reshape(slots_all, -1)
     mixed = jnp.einsum("ts,sd->td", combine, returned, preferred_element_type=jnp.float32)
     return mixed.astype(jnp.bfloat16)
 

time: 237 us -> 228 us (0.962)
  Pallas kernels: 126 us -> 203 us
  waiting for transfers between devices: 62.4 us -> 0 us
  starting transfers between devices: 25.7 us -> 0 us
    pallas_call x2 -> x4, Pallas kernels: 126 us -> 203 us  [_exchange(): pl.pallas_call(lambda *refs: _exchange_kernel(n_peers, pick_src, axis, *r...]
    all_to_all x2 -> x0, waiting for transfers between devices: 62.4 us -> none  [the longest x1 31.3 us: local(): lax.all_to_all(summed, 'wide', split_axis=0, concat_axis=0, tiled=True)]
    all_to_all x2 -> x0, starting transfers between devices: 25.7 us -> none  [the longest x1 18.2 us: local(): lax.all_to_all(outgoing, 'wide', split_axis=0, concat_axis=0, tiled=True)]
    reshape x0 -> x4, local copies, waits for them, and re-layouts: none -> 4.99 us  [the longest x1 1.95 us: local(): received = received.reshape(slots_all, -1)]
    all_to_all x4 -> x0, local copies, waits for them, and re-layouts: 2.89 us -> none  [the longest x2 1.83 us: local(): lax.all_to_all(outgoing, 'wide', split_axis=0, concat_axis=0, tiled=True)]
  transfers between devices with their start and end apart: 2 -> 0, of which waited for: 2 -> 0; matrix products, arithmetic and copies ran while one was open for 0% -> 0% of each run, Pallas kernels for 0% -> 0%
where the time goes in v3:
time: 228 us; the launch traced here: 227 us
  Pallas kernels  203 us (89%)
  matrix products  11.1 us (5%)
  local copies, waits for them, and re-layouts  7.1 us (3%)
  other arithmetic  6.25 us (3%)
    pallas_call x4, Pallas kernels, _exchange(): pl.pallas_call(lambda *refs: _exchange_kernel(n_peers, pick_src, axis, *r...  203 us
    dot_general x1, matrix products, local(): jnp.einsum('sf,fnd->nsd', hidden, wd, preferred_element_type=jnp.float32)  6.44 us

profile of v3, /device:TPU:1, one launch (start us, length us, event | category | flops | bytes accessed | tf_op | source)
XLA Modules:
  0.0 227.4 jit_solution(5883626692067398354)
XLA Ops:
  0.0 0.0 copy-start
  0.0 0.8 copy.28
  0.8 0.1 eq.42
  1.0 1.8 reduce-window.6
  2.8 0.3 slice_reduce_fusion
  3.1 0.1 eq.38
  3.2 0.1 fusion.16
  3.4 0.1 sub.7
  3.5 0.1 copy.31
  3.6 0.7 multiply_add_fusion
  4.3 0.4 fusion
  4.7 0.0 copy-done
  4.7 0.3 convolution_convert_fusion
  5.1 0.0 copy-start.1
  5.1 0.9 reshape.41.refs_0_
  6.0 42.9 %shard_map.64 = bf16[64,14,256]{2,1,0:T(8,128)(2,1)} custom-call(bf16[64,14,256]{2,1,0:T(8,128)(2,1)} %reshape.41.refs_0_), custom_call_target="tpu_custom_call" | custom-call | bytes 917504 | tf_op jit(solution)/shard_map/pallas_call | solution.py:61
  49.0 2.0 reshape.42.refs_0_
  50.9 63.6 %shard_map.65 = bf16[8,896,256]{2,1,0:T(8,128)(2,1)} custom-call(bf16[896,256]{1,0:T(8,128)(2,1)} %reshape.42.refs_0_), custom_call_target="tpu_custom_call" | custom-call | bytes 917504 | tf_op jit(solution)/shard_map/pallas_call | solution.py:61
  114.5 0.0 copy-done.1
  114.5 0.0 copy-start.2
  114.5 0.2 copy.36
  114.7 0.0 copy-start.3
  114.7 3.5 %convolution_bitcast_fusion.1 = f32[896,176]{0,1:T(8,128)S(1)} fusion(bf16[8,896,256]{2,1,0:T(8,128)(2,1)} %shard_map.65, bf16[176,8,256]{2,1,0:T(8,128)(2,1)S(1)} %bitcast.54), kind=kOutput, calls=%fused_computation.7 | convolution fusion | flops 645922816 | bytes 5021696 | tf_op jit(solution)/shard_map/nsd,fnd->sf/dot_general | solution.py:107
  118.2 0.0 copy-done.2
  118.2 0.2 copy.37
  118.4 0.0 copy-done.3
  118.4 0.2 copy.38
  118.6 6.4 %convert_bitcast_fusion.refs_0_ = bf16[8,896,256]{2,1,0:T(8,128)(2,1)} fusion(bf16[8,896,256]{2,1,0:T(8,128)(2,1)} %shard_map.65, bf16[176,8,256]{2,1,0:T(8,128)(2,1)S(1)} %bitcast.53, bf16[176,8,256]{2,1,0:T(8,128)(2,1)S(1)} %bitcast.52, f32[896,176]{0,1:T(8,128)S(1)} %convolution_bitcast_fusion.1), kind=kOutput, calls=%fused_computation | convolution fusion | flops 1294626816 | bytes 9412608 | tf_op jit(solution)/shard_map/sf,fnd->nsd/dot_general | solution.py:110
  125.0 57.4 %shard_map.66 = bf16[8,896,256]{2,1,0:T(8,128)(2,1)} custom-call(bf16[8,896,256]{2,1,0:T(8,128)(2,1)} %convert_bitcast_fusion.refs_0_), custom_call_target="tpu_custom_call" | custom-call | bytes 7340032 | tf_op jit(solution)/shard_map/pallas_call | solution.py:61
  182.4 0.0 copy-start.4
  182.4 2.8 %reduce_sum.32 = bf16[896,256]{1,0:T(8,128)(2,1)S(1)} reduce(bf16[8,896,256]{2,1,0:T(8,128)(2,1)} %shard_map.66, bf16[]{:T(256)} %constant.19.clone.1), dimensions={0}, to_apply=%region_5.6 | reduce | flops 1605632 | bytes 4128770 | tf_op jit(solution)/shard_map/reduce_sum | solution.py:114
  185.2 0.9 reshape.43.refs_0_
  186.1 38.8 %shard_map.67 = bf16[64,14,256]{2,1,0:T(8,128)(2,1)} custom-call(bf16[64,14,256]{2,1,0:T(8,128)(2,1)} %reshape.43.refs_0_), custom_call_target="tpu_custom_call" | custom-call | bytes 917504 | tf_op jit(solution)/shard_map/pallas_call | solution.py:61
  225.0 1.2 reshape.44
  226.2 0.0 copy-done.4
  226.2 0.3 select_reduce_fusion
  226.5 0.9 convolution_convert_fusion.1
  (4 shorter events, 0.0 us)
Async XLA Ops:
  0.0 4.7 %copy-start = (bf16[128,256]{1,0:T(8,128)(2,1)S(1)}, bf16[128,256]{1,0:T(8,128)(2,1)}, u32[]{:S(2)}) copy-start(bf16[128,256]{1,0:T(8,128)(2,1)} %param.6) | copy-start | bytes 196612
  5.1 109.4 %copy-start.1 = (bf16[1,176,2048]{2,1,0:T(8,128)(2,1)S(1)}, bf16[1,176,2048]{2,1,0:T(8,128)(2,1)}, u32[]{:S(2)}) copy-start(bf16[1,176,2048]{2,1,0:T(8,128)(2,1)} %param.9) | copy-start | bytes 2162692
  114.5 3.7 %copy-start.2 = (bf16[1,176,2048]{2,1,0:T(8,128)(2,1)S(1)}, bf16[1,176,2048]{2,1,0:T(8,128)(2,1)}, u32[]{:S(2)}) copy-start(bf16[1,176,2048]{2,1,0:T(8,128)(2,1)} %param.10) | copy-start | bytes 2162692
  114.7 3.7 %copy-start.3 = (bf16[1,176,2048]{2,1,0:T(8,128)(2,1)S(1)}, bf16[1,176,2048]{2,1,0:T(8,128)(2,1)}, u32[]{:S(2)}) copy-start(bf16[1,176,2048]{2,1,0:T(8,128)(2,1)} %param.11) | copy-start | bytes 2162692
  182.4 43.7 %copy-start.4 = (bf16[128,6]{0,1:T(8,128)(2,1)S(1)}, bf16[128,6]{0,1:T(8,128)(2,1)}, u32[]{:S(2)}) copy-start(bf16[128,6]{0,1:T(8,128)(2,1)} %param.8) | copy-start | bytes 4612

commit v4 on v3

--- a/solution.py
+++ b/solution.py
@@ -50,6 +50,85 @@
     own.wait()
 
 
+def _gather_kernel(x_ref, y_ref, sem_y, sem_x1, sem_x2, own_sem):
+    me = lax.axis_index("narrow")
+    w = lax.axis_index("wide")
+    yh = me // 4
+    xi = me % 4
+    partner = (1 - yh) * 4 + xi
+    right = yh * 4 + (xi + 1) % 4
+    left = yh * 4 + (xi + 3) % 4
+    barrier = pltpu.get_barrier_semaphore()
+    for peer in (partner, right, left):
+        pl.semaphore_signal(barrier, inc=1, device_id=(w, peer), device_id_type=MESH)
+    pl.semaphore_wait(barrier, 3)
+
+    def remote(src, slot, sem, peer):
+        return pltpu.make_async_remote_copy(
+            src_ref=src,
+            dst_ref=y_ref.at[slot],
+            send_sem=sem[0],
+            recv_sem=sem[1],
+            device_id=(w, peer),
+            device_id_type=MESH,
+        )
+
+    own = pltpu.make_async_copy(x_ref, y_ref.at[me], own_sem)
+    own.start()
+    cy = remote(x_ref, me, (sem_y.at[0], sem_y.at[1]), partner)
+    cy.start()
+    c1 = [
+        remote(x_ref, me, (sem_x1.at[0, 0], sem_x1.at[0, 1]), right),
+        remote(x_ref, me, (sem_x1.at[1, 0], sem_x1.at[1, 1]), left),
+    ]
+    for c in c1:
+        c.start()
+    remote(x_ref, partner, (sem_y.at[0], sem_y.at[1]), partner).wait_recv()
+    c2 = [
+        remote(y_ref.at[partner], partner, (sem_x1.at[2, 0], sem_x1.at[2, 1]), right),
+        remote(y_ref.at[partner], partner, (sem_x1.at[3, 0], sem_x1.at[3, 1]), left),
+    ]
+    for c in c2:
+        c.start()
+    lp = (1 - yh) * 4 + (xi + 3) % 4
+    rp = (1 - yh) * 4 + (xi + 1) % 4
+    remote(x_ref, left, (sem_x1.at[0, 0], sem_x1.at[0, 1]), left).wait_recv()
+    remote(x_ref, right, (sem_x1.at[1, 0], sem_x1.at[1, 1]), right).wait_recv()
+    c3 = [
+        remote(y_ref.at[left], left, (sem_x2.at[0, 0], sem_x2.at[0, 1]), right),
+    ]
+    c3[0].start()
+    remote(x_ref, rp, (sem_x1.at[3, 0], sem_x1.at[3, 1]), right).wait_recv()
+    c4 = remote(y_ref.at[rp], rp, (sem_x2.at[1, 0], sem_x2.at[1, 1]), left)
+    c4.start()
+    remote(x_ref, lp, (sem_x1.at[2, 0], sem_x1.at[2, 1]), left).wait_recv()
+    far = yh * 4 + (xi + 2) % 4
+    far_p = (1 - yh) * 4 + (xi + 2) % 4
+    remote(x_ref, far, (sem_x2.at[0, 0], sem_x2.at[0, 1]), left).wait_recv()
+    remote(x_ref, far_p, (sem_x2.at[1, 0], sem_x2.at[1, 1]), right).wait_recv()
+    for c in [cy] + c1 + c2 + c3 + [c4]:
+        c.wait_send()
+    own.wait()
+
+
+def _gather(x, n_peers, collective_id):
+    nbytes = x.size * x.dtype.itemsize
+    return pl.pallas_call(
+        _gather_kernel,
+        out_shape=jax.ShapeDtypeStruct((n_peers,) + x.shape, x.dtype),
+        in_specs=[pl.BlockSpec(memory_space=pl.ANY)],
+        out_specs=pl.BlockSpec(memory_space=pl.ANY),
+        scratch_shapes=[
+            pltpu.SemaphoreType.DMA((2,)),
+            pltpu.SemaphoreType.DMA((4, 2)),
+            pltpu.SemaphoreType.DMA((2, 2)),
+            pltpu.SemaphoreType.DMA(()),
+        ],
+        compiler_params=pltpu.CompilerParams(collective_id=collective_id, has_side_effects=True),
+        cost_estimate=pl.CostEstimate(flops=0, bytes_accessed=2 * n_peers * nbytes, transcendentals=0),
+    )(x)
+
+
 def _exchange(x, n_peers, gather, collective_id, axis="narrow"):
     if gather:
         out_shape = (n_peers,) + x.shape
@@ -100,7 +179,7 @@
     received = received.reshape(slots_all, -1)
     n_narrow = lax.axis_size("narrow")
     width = tokens.shape[1]
-    slot_rows = _exchange(received, n_narrow, True, 0)
+    slot_rows = _gather(received, n_narrow, 0)
     wg = w_gate[0].reshape(-1, n_narrow, width)
     wu = w_up[0].reshape(-1, n_narrow, width)
     wd = w_down[0].reshape(-1, n_narrow, width)

time: 228 us -> 200 us (0.88)
  Pallas kernels: 203 us -> 175 us
    pallas_call x4 -> x3, Pallas kernels: 203 us -> 138 us  [_exchange(): pl.pallas_call(lambda *refs: _exchange_kernel(n_peers, pick_src, axis, *r...]
    pallas_call x0 -> x1, Pallas kernels: none -> 36.8 us  [_gather(): pl.pallas_call(_gather_kernel, out_shape=jax.ShapeDtypeStruct((n_peers,)...]
where the time goes in v4:
time: 200 us
  Pallas kernels  175 us (88%)
  matrix products  11.1 us (6%)
  local copies, waits for them, and re-layouts  7.1 us (4%)
  other arithmetic  6.25 us (3%)
    pallas_call x3, Pallas kernels, _exchange(): pl.pallas_call(lambda *refs: _exchange_kernel(n_peers, pick_src, axis, *r...  138 us
    pallas_call x1, Pallas kernels, _gather(): pl.pallas_call(_gather_kernel, out_shape=jax.ShapeDtypeStruct((n_peers,)...  36.8 us
    dot_general x1, matrix products, local(): jnp.einsum('sf,fnd->nsd', hidden, wd, preferred_element_type=jnp.float32)  6.45 us

profile of v4, /device:TPU:1, one launch (start us, length us, event | category | flops | bytes accessed | tf_op | source)
XLA Modules:
  0.0 199.5 jit_solution(2544342091027666917)
XLA Ops:
  0.0 0.0 copy-start
  0.0 0.8 copy.28
  0.8 0.1 eq.42
  1.0 1.8 reduce-window.6
  2.8 0.3 slice_reduce_fusion
  3.1 0.1 eq.38
  3.2 0.1 fusion.16
  3.4 0.1 sub.7
  3.5 0.1 copy.31
  3.6 0.7 multiply_add_fusion
  4.3 0.4 fusion
  4.7 0.0 copy-done
  4.7 0.3 convolution_convert_fusion
  5.1 0.0 copy-start.1
  5.1 0.9 reshape.41.refs_0_
  6.0 42.9 %shard_map.64 = bf16[64,14,256]{2,1,0:T(8,128)(2,1)} custom-call(bf16[64,14,256]{2,1,0:T(8,128)(2,1)} %reshape.41.refs_0_), custom_call_target="tpu_custom_call" | custom-call | bytes 917504 | tf_op jit(solution)/shard_map/pallas_call | solution.py:140
  49.0 2.0 reshape.42.x_ref
  50.9 36.8 %shard_map.65 = bf16[8,896,256]{2,1,0:T(8,128)(2,1)} custom-call(bf16[896,256]{1,0:T(8,128)(2,1)} %reshape.42.x_ref), custom_call_target="tpu_custom_call" | custom-call | bytes 7340032 | tf_op jit(solution)/shard_map/pallas_call | solution.py:116
  87.8 0.0 copy-done.1
  87.8 0.0 copy-start.2
  87.8 0.2 copy.36
  88.0 0.0 copy-start.3
  88.0 3.5 %convolution_bitcast_fusion.1 = f32[896,176]{0,1:T(8,128)S(1)} fusion(bf16[8,896,256]{2,1,0:T(8,128)(2,1)} %shard_map.65, bf16[176,8,256]{2,1,0:T(8,128)(2,1)S(1)} %bitcast.54), kind=kOutput, calls=%fused_computation.7 | convolution fusion | flops 645922816 | bytes 5021696 | tf_op jit(solution)/shard_map/nsd,fnd->sf/dot_general | solution.py:186
  91.4 0.0 copy-done.2
  91.4 0.2 copy.37
  91.6 0.0 copy-done.3
  91.6 0.2 copy.38
  91.8 6.4 %convert_bitcast_fusion.refs_0_ = bf16[8,896,256]{2,1,0:T(8,128)(2,1)} fusion(bf16[8,896,256]{2,1,0:T(8,128)(2,1)} %shard_map.65, bf16[176,8,256]{2,1,0:T(8,128)(2,1)S(1)} %bitcast.53, bf16[176,8,256]{2,1,0:T(8,128)(2,1)S(1)} %bitcast.52, f32[896,176]{0,1:T(8,128)S(1)} %convolution_bitcast_fusion.1), kind=kOutput, calls=%fused_computation | convolution fusion | flops 1294626816 | bytes 9412608 | tf_op jit(solution)/shard_map/sf,fnd->nsd/dot_general | solution.py:189
  98.3 56.0 %shard_map.66 = bf16[8,896,256]{2,1,0:T(8,128)(2,1)} custom-call(bf16[8,896,256]{2,1,0:T(8,128)(2,1)} %convert_bitcast_fusion.refs_0_), custom_call_target="tpu_custom_call" | custom-call | bytes 7340032 | tf_op jit(solution)/shard_map/pallas_call | solution.py:140
  154.3 0.0 copy-start.4
  154.3 2.8 %reduce_sum.32 = bf16[896,256]{1,0:T(8,128)(2,1)S(1)} reduce(bf16[8,896,256]{2,1,0:T(8,128)(2,1)} %shard_map.66, bf16[]{:T(256)} %constant.19.clone.1), dimensions={0}, to_apply=%region_5.6 | reduce | flops 1605632 | bytes 4128770 | tf_op jit(solution)/shard_map/reduce_sum | solution.py:193
  157.1 0.9 reshape.43.refs_0_
  158.0 39.1 %shard_map.67 = bf16[64,14,256]{2,1,0:T(8,128)(2,1)} custom-call(bf16[64,14,256]{2,1,0:T(8,128)(2,1)} %reshape.43.refs_0_), custom_call_target="tpu_custom_call" | custom-call | bytes 917504 | tf_op jit(solution)/shard_map/pallas_call | solution.py:140
  197.1 1.2 reshape.44
  198.3 0.0 copy-done.4
  198.3 0.3 select_reduce_fusion
  198.7 0.9 convolution_convert_fusion.1
  (4 shorter events, 0.0 us)
Async XLA Ops:
  0.0 4.7 %copy-start = (bf16[128,256]{1,0:T(8,128)(2,1)S(1)}, bf16[128,256]{1,0:T(8,128)(2,1)}, u32[]{:S(2)}) copy-start(bf16[128,256]{1,0:T(8,128)(2,1)} %param.6) | copy-start | bytes 196612
  5.1 82.7 %copy-start.1 = (bf16[1,176,2048]{2,1,0:T(8,128)(2,1)S(1)}, bf16[1,176,2048]{2,1,0:T(8,128)(2,1)}, u32[]{:S(2)}) copy-start(bf16[1,176,2048]{2,1,0:T(8,128)(2,1)} %param.9) | copy-start | bytes 2162692
  87.8 3.7 %copy-start.2 = (bf16[1,176,2048]{2,1,0:T(8,128)(2,1)S(1)}, bf16[1,176,2048]{2,1,0:T(8,128)(2,1)}, u32[]{:S(2)}) copy-start(bf16[1,176,2048]{2,1,0:T(8,128)(2,1)} %param.10) | copy-start | bytes 2162692
  88.0 3.7 %copy-start.3 = (bf16[1,176,2048]{2,1,0:T(8,128)(2,1)S(1)}, bf16[1,176,2048]{2,1,0:T(8,128)(2,1)}, u32[]{:S(2)}) copy-start(bf16[1,176,2048]{2,1,0:T(8,128)(2,1)} %param.11) | copy-start | bytes 2162692
  154.3 44.0 %copy-start.4 = (bf16[128,6]{0,1:T(8,128)(2,1)S(1)}, bf16[128,6]{0,1:T(8,128)(2,1)}, u32[]{:S(2)}) copy-start(bf16[128,6]{0,1:T(8,128)(2,1)} %param.8) | copy-start | bytes 4612

commit v5 on v4

--- a/solution.py
+++ b/solution.py
@@ -127,6 +127,102 @@
         compiler_params=pltpu.CompilerParams(collective_id=collective_id, has_side_effects=True),
         cost_estimate=pl.CostEstimate(flops=0, bytes_accessed=2 * n_peers * nbytes, transcendentals=0),
     )(x)
+
+
+def _add_into(dst, *srcs):
+    rows_all = dst.shape[0]
+    step = 128 if rows_all % 128 == 0 else rows_all
+
+    def body(i, carry):
+        rows = pl.ds(pl.multiple_of(i * step, step), step)
+        total = srcs[0][rows, :].astype(jnp.float32)
+        for src in srcs[1:]:
+            total = total + src[rows, :].astype(jnp.float32)
+        dst[rows, :] = total.astype(dst.dtype)
+        return carry
+
+    lax.fori_loop(0, rows_all // step, body, 0)
+
+
+def _reduce_kernel(p_ref, o_ref, rp, rm, sp, sm, qy, ry, sem_p, sem_m, sem_y):
+    me = lax.axis_index("narrow")
+    w = lax.axis_index("wide")
+    yh = me // 4
+    xi = me % 4
+    other = 1 - yh
+    partner = other * 4 + xi
+    right = yh * 4 + (xi + 1) % 4
+    left = yh * 4 + (xi + 3) % 4
+    barrier = pltpu.get_barrier_semaphore()
+    for peer in (partner, right, left):
+        pl.semaphore_signal(barrier, inc=1, device_id=(w, peer), device_id_type=MESH)
+    pl.semaphore_wait(barrier, 3)
+
+    def remote(src, dst, sem, peer):
+        return pltpu.make_async_remote_copy(
+            src_ref=src,
+            dst_ref=dst,
+            send_sem=sem.at[0],
+            recv_sem=sem.at[1],
+            device_id=(w, peer),
+            device_id_type=MESH,
+        )
+
+    mine = lambda h, k: p_ref.at[h * 4 + (xi + k) % 4]
+    sends = []
+    c = remote(mine(other, 3), rp.at[0], sem_p.at[0], right)
+    c.start()
+    sends.append(c)
+    c = remote(mine(yh, 1), rm.at[0], sem_m.at[0], left)
+    c.start()
+    sends.append(c)
+    for step, (kp, km) in enumerate(((2, 2), (1, 3))):
+        remote(sp.at[step], rp.at[step], sem_p.at[step], left).wait_recv()
+        _add_into(sp.at[step], rp.at[step], mine(other, kp))
+        c = remote(sp.at[step], rp.at[step + 1], sem_p.at[step + 1], right)
+        c.start()
+        sends.append(c)
+        remote(sm.at[step], rm.at[step], sem_m.at[step], right).wait_recv()
+        _add_into(sm.at[step], rm.at[step], mine(yh, km))
+        c = remote(sm.at[step], rm.at[step + 1], sem_m.at[step + 1], left)
+        c.start()
+        sends.append(c)
+    remote(qy, rp.at[2], sem_p.at[2], left).wait_recv()
+    _add_into(qy, rp.at[2], mine(other, 0))
+    c = remote(qy, ry, sem_y, partner)
+    c.start()
+    sends.append(c)
+    remote(sm.at[1], rm.at[2], sem_m.at[2], right).wait_recv()
+    remote(qy, ry, sem_y, partner).wait_recv()
+    _add_into(o_ref, rm.at[2], mine(yh, 0), ry)
+    for c in sends:
+        c.wait_send()
+
+
+def _reduce(p, collective_id):
+    n_peers, rows, cols = p.shape
+    block = pltpu.VMEM((rows, cols), p.dtype)
+    return pl.pallas_call(
+        _reduce_kernel,
+        out_shape=jax.ShapeDtypeStruct((rows, cols), p.dtype),
+        in_specs=[pl.BlockSpec(memory_space=pltpu.VMEM)],
+        out_specs=pl.BlockSpec(memory_space=pltpu.VMEM),
+        scratch_shapes=[
+            pltpu.VMEM((3, rows, cols), p.dtype),
+            pltpu.VMEM((3, rows, cols), p.dtype),
+            pltpu.VMEM((2, rows, cols), p.dtype),
+            pltpu.VMEM((2, rows, cols), p.dtype),
+            block,
+            block,
+            pltpu.SemaphoreType.DMA((3, 2)),
+            pltpu.SemaphoreType.DMA((3, 2)),
+            pltpu.SemaphoreType.DMA((2,)),
+        ],
+        compiler_params=pltpu.CompilerParams(collective_id=collective_id, has_side_effects=True),
+        cost_estimate=pl.CostEstimate(
+            flops=2 * p.size, bytes_accessed=2 * p.size * p.dtype.itemsize, transcendentals=0
+        ),
+    )(p)
 
 
 def _exchange(x, n_peers, gather, collective_id, axis="narrow"):
@@ -189,8 +285,7 @@
     partial_value = jnp.einsum(
         "sf,fnd->nsd", hidden, wd, preferred_element_type=jnp.float32
     ).astype(jnp.bfloat16)
-    parts = _exchange(partial_value, n_narrow, False, 1)
-    summed = jnp.sum(parts.astype(jnp.float32), axis=0).astype(jnp.bfloat16)
+    summed = _reduce(partial_value, 1)
     returned = _exchange(summed.reshape(groups_wide, capacity, -1), groups_wide, False, 3, "wide")
     returned = returned.reshape(slots_all, -1)
     mixed = jnp.einsum("ts,sd->td", combine, returned, preferred_element_type=jnp.float32)

time: 200 us -> 187 us (0.935)
  Pallas kernels: 175 us -> 164 us
  other arithmetic: 6.25 us -> 3.47 us
    pallas_call x3 -> x2, Pallas kernels: 138 us -> 85.9 us  [_exchange(): pl.pallas_call(lambda *refs: _exchange_kernel(n_peers, pick_src, axis, *r...]
    pallas_call x0 -> x1, Pallas kernels: none -> 41.3 us  [_reduce(): pl.pallas_call(_reduce_kernel, out_shape=jax.ShapeDtypeStruct((rows, cols...]
    reduce_sum x1 -> x0, other arithmetic: 2.78 us -> none  [local(): summed = jnp.sum(parts.astype(jnp.float32), axis=0).astype(jnp.bfloat16)]
where the time goes in v5:
time: 187 us
  Pallas kernels  164 us (88%)
  matrix products  11.1 us (6%)
  local copies, waits for them, and re-layouts  8.12 us (4%)
  other arithmetic  3.47 us (2%)
    pallas_call x2, Pallas kernels, _exchange(): pl.pallas_call(lambda *refs: _exchange_kernel(n_peers, pick_src, axis, *r...  85.9 us
    pallas_call x1, Pallas kernels, _reduce(): pl.pallas_call(_reduce_kernel, out_shape=jax.ShapeDtypeStruct((rows, cols...  41.3 us
    pallas_call x1, Pallas kernels, _gather(): pl.pallas_call(_gather_kernel, out_shape=jax.ShapeDtypeStruct((n_peers,)...  36.8 us
    dot_general x1, matrix products, local(): jnp.einsum('sf,fnd->nsd', hidden, wd, preferred_element_type=jnp.float32)  6.45 us

profile of v5, /device:TPU:1, one launch (start us, length us, event | category | flops | bytes accessed | tf_op | source)
XLA Modules:
  0.0 186.9 jit_solution(8091462049726296747)
XLA Ops:
  0.0 0.0 copy-start
  0.0 0.8 copy.28
  0.8 0.1 eq.42
  1.0 1.8 reduce-window.6
  2.8 0.3 slice_reduce_fusion
  3.1 0.1 eq.38
  3.2 0.1 fusion.16
  3.4 0.1 sub.7
  3.5 0.1 copy.31
  3.6 0.7 multiply_add_fusion
  4.3 0.4 fusion
  4.7 0.0 copy-done
  4.7 0.3 convolution_convert_fusion
  5.1 0.0 copy-start.1
  5.1 0.9 reshape.41.refs_0_
  6.0 42.9 %shard_map.64 = bf16[64,14,256]{2,1,0:T(8,128)(2,1)} custom-call(bf16[64,14,256]{2,1,0:T(8,128)(2,1)} %reshape.41.refs_0_), custom_call_target="tpu_custom_call" | custom-call | bytes 917504 | tf_op jit(solution)/shard_map/pallas_call | solution.py:236
  49.0 2.0 %reshape.42.x_ref = bf16[896,256]{1,0:T(8,128)(2,1)} reshape(bf16[64,14,256]{2,1,0:T(8,128)(2,1)} %shard_map.64) | data formatting | bytes 917504 | tf_op jit(solution)/shard_map/reshape | solution.py:275
  50.9 36.8 %shard_map.65 = bf16[8,896,256]{2,1,0:T(8,128)(2,1)} custom-call(bf16[896,256]{1,0:T(8,128)(2,1)} %reshape.42.x_ref), custom_call_target="tpu_custom_call" | custom-call | bytes 7340032 | tf_op jit(solution)/shard_map/pallas_call | solution.py:116
  87.8 0.0 copy-done.1
  87.8 0.0 copy-start.2
  87.8 0.2 copy.36
  88.0 0.0 copy-start.3
  88.0 3.5 %convolution_bitcast_fusion.1 = f32[896,176]{0,1:T(8,128)S(1)} fusion(bf16[8,896,256]{2,1,0:T(8,128)(2,1)} %shard_map.65, bf16[176,8,256]{2,1,0:T(8,128)(2,1)S(1)} %bitcast.54), kind=kOutput, calls=%fused_computation.7 | convolution fusion | flops 645922816 | bytes 5021696 | tf_op jit(solution)/shard_map/nsd,fnd->sf/dot_general | solution.py:282
  91.4 0.0 copy-done.2
  91.4 0.2 copy.37
  91.6 0.0 copy-done.3
  91.6 0.2 copy.38
  91.8 6.4 %convert_bitcast_fusion.p_ref = bf16[8,896,256]{2,1,0:T(8,128)(2,1)} fusion(bf16[8,896,256]{2,1,0:T(8,128)(2,1)} %shard_map.65, bf16[176,8,256]{2,1,0:T(8,128)(2,1)S(1)} %bitcast.53, bf16[176,8,256]{2,1,0:T(8,128)(2,1)S(1)} %bitcast.52, f32[896,176]{0,1:T(8,128)S(1)} %convolution_bitcast_fusion.1), kind=kOutput, calls=%fused_computation | convolution fusion | flops 1294626816 | bytes 9412608 | tf_op jit(solution)/shard_map/sf,fnd->nsd/dot_general | solution.py:285
  98.3 0.0 copy-start.4
  98.3 41.3 %shard_map.66 = bf16[896,256]{1,0:T(8,128)(2,1)} custom-call(bf16[8,896,256]{2,1,0:T(8,128)(2,1)} %convert_bitcast_fusion.p_ref), custom_call_target="tpu_custom_call" | custom-call | flops 3670016 | bytes 7340032 | tf_op jit(solution)/shard_map/pallas_call | solution.py:205
  139.5 1.9 %reshape.43.refs_0_ = bf16[64,14,256]{2,1,0:T(8,128)(2,1)} reshape(bf16[896,256]{1,0:T(8,128)(2,1)} %shard_map.66) | data formatting | bytes 917504 | tf_op jit(solution)/shard_map/reshape | solution.py:289
  141.5 43.0 %shard_map.67 = bf16[64,14,256]{2,1,0:T(8,128)(2,1)} custom-call(bf16[64,14,256]{2,1,0:T(8,128)(2,1)} %reshape.43.refs_0_), custom_call_target="tpu_custom_call" | custom-call | bytes 917504 | tf_op jit(solution)/shard_map/pallas_call | solution.py:236
  184.5 1.2 reshape.44
  185.7 0.0 copy-done.4
  185.7 0.3 select_reduce_fusion
  186.0 0.9 convolution_convert_fusion.1
  (4 shorter events, 0.0 us)
Async XLA Ops:
  0.0 4.7 %copy-start = (bf16[128,256]{1,0:T(8,128)(2,1)S(1)}, bf16[128,256]{1,0:T(8,128)(2,1)}, u32[]{:S(2)}) copy-start(bf16[128,256]{1,0:T(8,128)(2,1)} %param.6) | copy-start | bytes 196612
  5.1 82.7 %copy-start.1 = (bf16[1,176,2048]{2,1,0:T(8,128)(2,1)S(1)}, bf16[1,176,2048]{2,1,0:T(8,128)(2,1)}, u32[]{:S(2)}) copy-start(bf16[1,176,2048]{2,1,0:T(8,128)(2,1)} %param.9) | copy-start | bytes 2162692
  87.8 3.7 %copy-start.2 = (bf16[1,176,2048]{2,1,0:T(8,128)(2,1)S(1)}, bf16[1,176,2048]{2,1,0:T(8,128)(2,1)}, u32[]{:S(2)}) copy-start(bf16[1,176,2048]{2,1,0:T(8,128)(2,1)} %param.10) | copy-start | bytes 2162692
  88.0 3.7 %copy-start.3 = (bf16[1,176,2048]{2,1,0:T(8,128)(2,1)S(1)}, bf16[1,176,2048]{2,1,0:T(8,128)(2,1)}, u32[]{:S(2)}) copy-start(bf16[1,176,2048]{2,1,0:T(8,128)(2,1)} %param.11) | copy-start | bytes 2162692
  98.3 87.4 %copy-start.4 = (bf16[128,6]{0,1:T(8,128)(2,1)S(1)}, bf16[128,6]{0,1:T(8,128)(2,1)}, u32[]{:S(2)}) copy-start(bf16[128,6]{0,1:T(8,128)(2,1)} %param.8) | copy-start | bytes 4612

commit v6 on v5

--- a/solution.py
+++ b/solution.py
@@ -225,6 +225,79 @@
     )(p)
 
 
+def _wide_kernel(x_ref, y_ref, t_ref, sem_z, sem_g, own_z, own_g):
+    nz = x_ref.shape[1]
+    me = lax.axis_index("wide")
+    n = lax.axis_index("narrow")
+    yl = me // (2 * nz)
+    zi = (me // 2) % nz
+    co = me % 2
+    dev = lambda a, z, c: ((a * nz + z) * 2 + c, n)
+    groups = [((yl + j // 2) % 2, (co + j % 2) % 2) for j in range(1, 4)]
+    barrier = pltpu.get_barrier_semaphore()
+    for k in range(1, nz):
+        pl.semaphore_signal(barrier, inc=1, device_id=dev(yl, (zi + k) % nz, co), device_id_type=MESH)
+    for a, c in groups:
+        pl.semaphore_signal(barrier, inc=1, device_id=dev(a, zi, c), device_id_type=MESH)
+    pl.semaphore_wait(barrier, nz - 1 + 3)
+
+    def remote(src, dst, sem, peer):
+        return pltpu.make_async_remote_copy(
+            src_ref=src,
+            dst_ref=dst,
+            send_sem=sem.at[0],
+            recv_sem=sem.at[1],
+            device_id=peer,
+            device_id_type=MESH,
+        )
+
+    own = pltpu.make_async_copy(x_ref.at[:, zi], t_ref.at[zi], own_z)
+    own.start()
+    sends = []
+    for k in range(1, nz):
+        zp = (zi + k) % nz
+        c = remote(x_ref.at[:, zp], t_ref.at[zi], sem_z.at[k - 1], dev(yl, zp, co))
+        c.start()
+        sends.append(c)
+    for k in range(1, nz):
+        zs = (zi + nz - k) % nz
+        remote(x_ref.at[:, zs], t_ref.at[zs], sem_z.at[k - 1], dev(yl, zs, co)).wait_recv()
+    own.wait()
+    own = pltpu.make_async_copy(t_ref.at[:, yl, co], y_ref.at[yl, :, co], own_g)
+    own.start()
+    for j, (a, c) in enumerate(groups):
+        cp = remote(t_ref.at[:, a, c], y_ref.at[yl, :, co], sem_g.at[j], dev(a, zi, c))
+        cp.start()
+        sends.append(cp)
+    for j, (a, c) in enumerate(groups):
+        remote(t_ref.at[:, yl, co], y_ref.at[a, :, c], sem_g.at[j], dev(a, zi, c)).wait_recv()
+    for c in sends:
+        c.wait_send()
+    own.wait()
+
+
+def _wide(x, collective_id):
+    n_dev, rows, cols = x.shape
+    nz = n_dev // 4
+    x = x.reshape(2, nz, 2, rows, cols)
+    y = pl.pallas_call(
+        _wide_kernel,
+        out_shape=jax.ShapeDtypeStruct(x.shape, x.dtype),
+        in_specs=[pl.BlockSpec(memory_space=pl.ANY)],
+        out_specs=pl.BlockSpec(memory_space=pl.ANY),
+        scratch_shapes=[
+            pltpu.VMEM((nz, 2, 2, rows, cols), x.dtype),
+            pltpu.SemaphoreType.DMA((nz - 1, 2)),
+            pltpu.SemaphoreType.DMA((3, 2)),
+            pltpu.SemaphoreType.DMA(()),
+            pltpu.SemaphoreType.DMA(()),
+        ],
+        compiler_params=pltpu.CompilerParams(collective_id=collective_id, has_side_effects=True),
+        cost_estimate=pl.CostEstimate(flops=0, bytes_accessed=4 * x.size * x.dtype.itemsize, transcendentals=0),
+    )(x)
+    return y.reshape(n_dev, rows, cols)
+
+
 def _exchange(x, n_peers, gather, collective_id, axis="narrow"):
     if gather:
         out_shape = (n_peers,) + x.shape
@@ -271,7 +344,7 @@
     outgoing = jnp.einsum("ts,td->sd", dispatch, tokens, preferred_element_type=jnp.float32).astype(
         jnp.bfloat16
     )
-    received = _exchange(outgoing.reshape(groups_wide, capacity, -1), groups_wide, False, 2, "wide")
+    received = _wide(outgoing.reshape(groups_wide, capacity, -1), 2)
     received = received.reshape(slots_all, -1)
     n_narrow = lax.axis_size("narrow")
     width = tokens.shape[1]
@@ -286,7 +359,7 @@
         "sf,fnd->nsd", hidden, wd, preferred_element_type=jnp.float32
     ).astype(jnp.bfloat16)
     summed = _reduce(partial_value, 1)
-    returned = _exchange(summed.reshape(groups_wide, capacity, -1), groups_wide, False, 3, "wide")
+    returned = _wide(summed.reshape(groups_wide, capacity, -1), 3)
     returned = returned.reshape(slots_all, -1)
     mixed = jnp.einsum("ts,sd->td", combine, returned, preferred_element_type=jnp.float32)
     return mixed.astype(jnp.bfloat16)

time: 187 us -> 196 us (1.048); the launches traced: 187 us -> 194 us
  Pallas kernels: 164 us -> 171 us
    another operation x0 -> x4, local copies, waits for them, and re-layouts: none -> 6.01 us  [the longest x2 2.88 us: _wide(): x = x.reshape(2, nz, 2, rows, cols)]
    reshape x4 -> x0, local copies, waits for them, and re-layouts: 6.01 us -> none  [the longest x1 1.95 us: local(): received = received.reshape(slots_all, -1)]
    pallas_call x1, Pallas kernels: 41.3 us -> 45.4 us  [_reduce(): pl.pallas_call(_reduce_kernel, out_shape=jax.ShapeDtypeStruct((rows, cols...]
    pallas_call x1, Pallas kernels: 36.8 us -> 38.9 us  [_gather(): pl.pallas_call(_gather_kernel, out_shape=jax.ShapeDtypeStruct((n_peers,)...]
where the time goes in v6:
time: 196 us; the launch traced here: 194 us
  Pallas kernels  171 us (87%)
  matrix products  11.1 us (6%)
  local copies, waits for them, and re-layouts  8.12 us (4%)
  other arithmetic  3.47 us (2%)
    pallas_call x2, Pallas kernels, _wide(): pl.pallas_call(_wide_kernel, out_shape=jax.ShapeDtypeStruct(x.shape, x.dt...  86.3 us
    pallas_call x1, Pallas kernels, _reduce(): pl.pallas_call(_reduce_kernel, out_shape=jax.ShapeDtypeStruct((rows, cols...  45.4 us
    pallas_call x1, Pallas kernels, _gather(): pl.pallas_call(_gather_kernel, out_shape=jax.ShapeDtypeStruct((n_peers,)...  38.9 us
    dot_general x1, matrix products, local(): jnp.einsum('sf,fnd->nsd', hidden, wd, preferred_element_type=jnp.float32)  6.45 us

profile of v6, /device:TPU:1, one launch (start us, length us, event | category | flops | bytes accessed | tf_op | source)
XLA Modules:
  0.0 193.6 jit_solution(8144983350888140699)
XLA Ops:
  0.0 0.0 copy-start
  0.0 0.8 copy.28
  0.8 0.1 eq.42
  1.0 1.8 reduce-window.6
  2.8 0.3 slice_reduce_fusion
  3.1 0.1 eq.38
  3.2 0.1 fusion.16
  3.4 0.1 sub.7
  3.5 0.1 copy.31
  3.6 0.7 multiply_add_fusion
  4.3 0.4 fusion
  4.7 0.0 copy-done
  4.7 0.3 convolution_convert_fusion
  5.1 0.0 copy-start.1
  5.1 0.9 reshape_reshape.12.x_ref
  6.0 47.4 %shard_map.64 = bf16[2,16,2,14,256]{4,3,2,1,0:T(8,128)(2,1)} custom-call(bf16[2,16,2,14,256]{4,3,2,1,0:T(8,128)(2,1)} %reshape_reshape.12.x_ref), custom_call_target="tpu_custom_call" | custom-call | bytes 1835008 | tf_op jit(solution)/shard_map/pallas_call | solution.py:283
  53.4 2.0 %reshape_reshape.13.x_ref = bf16[896,256]{1,0:T(8,128)(2,1)} reshape(bf16[2,16,2,14,256]{4,3,2,1,0:T(8,128)(2,1)} %shard_map.64) | data formatting | bytes 917504 | tf_op jit(solution)/shard_map/reshape;reshape | solution.py:348
  55.4 38.9 %shard_map.65 = bf16[8,896,256]{2,1,0:T(8,128)(2,1)} custom-call(bf16[896,256]{1,0:T(8,128)(2,1)} %reshape_reshape.13.x_ref), custom_call_target="tpu_custom_call" | custom-call | bytes 7340032 | tf_op jit(solution)/shard_map/pallas_call | solution.py:116
  94.3 0.0 copy-done.1
  94.3 0.0 copy-start.2
  94.3 0.2 copy.36
  94.5 0.0 copy-start.3
  94.5 3.5 %convolution_bitcast_fusion.1 = f32[896,176]{0,1:T(8,128)S(1)} fusion(bf16[8,896,256]{2,1,0:T(8,128)(2,1)} %shard_map.65, bf16[176,8,256]{2,1,0:T(8,128)(2,1)S(1)} %bitcast.54), kind=kOutput, calls=%fused_computation.7 | convolution fusion | flops 645922816 | bytes 5021696 | tf_op jit(solution)/shard_map/nsd,fnd->sf/dot_general | solution.py:355
  97.9 0.0 copy-done.2
  97.9 0.2 copy.37
  98.1 0.0 copy-done.3
  98.1 0.2 copy.38
  98.3 6.4 %convert_bitcast_fusion.p_ref = bf16[8,896,256]{2,1,0:T(8,128)(2,1)} fusion(bf16[8,896,256]{2,1,0:T(8,128)(2,1)} %shard_map.65, bf16[176,8,256]{2,1,0:T(8,128)(2,1)S(1)} %bitcast.53, bf16[176,8,256]{2,1,0:T(8,128)(2,1)S(1)} %bitcast.52, f32[896,176]{0,1:T(8,128)S(1)} %convolution_bitcast_fusion.1), kind=kOutput, calls=%fused_computation | convolution fusion | flops 1294626816 | bytes 9412608 | tf_op jit(solution)/shard_map/sf,fnd->nsd/dot_general | solution.py:358
  104.8 0.0 copy-start.4
  104.8 45.4 %shard_map.66 = bf16[896,256]{1,0:T(8,128)(2,1)} custom-call(bf16[8,896,256]{2,1,0:T(8,128)(2,1)} %convert_bitcast_fusion.p_ref), custom_call_target="tpu_custom_call" | custom-call | flops 3670016 | bytes 7340032 | tf_op jit(solution)/shard_map/pallas_call | solution.py:205
  150.2 1.9 %reshape_reshape.14.x_ref = bf16[2,16,2,14,256]{4,3,2,1,0:T(8,128)(2,1)} reshape(bf16[896,256]{1,0:T(8,128)(2,1)} %shard_map.66) | data formatting | bytes 917504 | tf_op jit(solution)/shard_map/reshape;reshape | solution.py:282
  152.1 39.0 %shard_map.67 = bf16[2,16,2,14,256]{4,3,2,1,0:T(8,128)(2,1)} custom-call(bf16[2,16,2,14,256]{4,3,2,1,0:T(8,128)(2,1)} %reshape_reshape.14.x_ref), custom_call_target="tpu_custom_call" | custom-call | bytes 1835008 | tf_op jit(solution)/shard_map/pallas_call | solution.py:283
  191.1 1.2 reshape_reshape.15
  192.3 0.0 copy-done.4
  192.3 0.3 select_reduce_fusion
  192.7 0.9 convolution_convert_fusion.1
  (4 shorter events, 0.0 us)
Async XLA Ops:
  0.0 4.7 %copy-start = (bf16[128,256]{1,0:T(8,128)(2,1)S(1)}, bf16[128,256]{1,0:T(8,128)(2,1)}, u32[]{:S(2)}) copy-start(bf16[128,256]{1,0:T(8,128)(2,1)} %param.6) | copy-start | bytes 196612
  5.1 89.2 %copy-start.1 = (bf16[1,176,2048]{2,1,0:T(8,128)(2,1)S(1)}, bf16[1,176,2048]{2,1,0:T(8,128)(2,1)}, u32[]{:S(2)}) copy-start(bf16[1,176,2048]{2,1,0:T(8,128)(2,1)} %param.9) | copy-start | bytes 2162692
  94.3 3.7 %copy-start.2 = (bf16[1,176,2048]{2,1,0:T(8,128)(2,1)S(1)}, bf16[1,176,2048]{2,1,0:T(8,128)(2,1)}, u32[]{:S(2)}) copy-start(bf16[1,176,2048]{2,1,0:T(8,128)(2,1)} %param.10) | copy-start | bytes 2162692
  94.5 3.7 %copy-start.3 = (bf16[1,176,2048]{2,1,0:T(8,128)(2,1)S(1)}, bf16[1,176,2048]{2,1,0:T(8,128)(2,1)}, u32[]{:S(2)}) copy-start(bf16[1,176,2048]{2,1,0:T(8,128)(2,1)} %param.11) | copy-start | bytes 2162692
  104.8 87.5 %copy-start.4 = (bf16[128,6]{0,1:T(8,128)(2,1)S(1)}, bf16[128,6]{0,1:T(8,128)(2,1)}, u32[]{:S(2)}) copy-start(bf16[128,6]{0,1:T(8,128)(2,1)} %param.8) | copy-start | bytes 4612

commit v7 on v5

--- a/solution.py
+++ b/solution.py
@@ -1,3 +1,5 @@
+import types
+
 import jax
 import jax.numpy as jnp
 from jax import lax
@@ -50,7 +52,7 @@
     own.wait()
 
 
-def _gather_kernel(x_ref, y_ref, sem_y, sem_x1, sem_x2, own_sem):
+def _gather_chain(x_ref, slot_of, sem_y, sem_x1, sem_x2, own_sem):
     me = lax.axis_index("narrow")
     w = lax.axis_index("wide")
     yh = me // 4
@@ -58,10 +60,8 @@
     partner = (1 - yh) * 4 + xi
     right = yh * 4 + (xi + 1) % 4
     left = yh * 4 + (xi + 3) % 4
-    barrier = pltpu.get_barrier_semaphore()
-    for peer in (partner, right, left):
-        pl.semaphore_signal(barrier, inc=1, device_id=(w, peer), device_id_type=MESH)
-    pl.semaphore_wait(barrier, 3)
+
+    y_ref = types.SimpleNamespace(at=_Slots(slot_of))
 
     def remote(src, slot, sem, peer):
         return pltpu.make_async_remote_copy(
@@ -106,26 +106,132 @@
     far_p = (1 - yh) * 4 + (xi + 2) % 4
     remote(x_ref, far, (sem_x2.at[0, 0], sem_x2.at[0, 1]), left).wait_recv()
     remote(x_ref, far_p, (sem_x2.at[1, 0], sem_x2.at[1, 1]), right).wait_recv()
-    for c in [cy] + c1 + c2 + c3 + [c4]:
-        c.wait_send()
-    own.wait()
-
-
-def _gather(x, n_peers, collective_id):
-    nbytes = x.size * x.dtype.itemsize
+    return [cy] + c1 + c2 + c3 + [c4], own
+
+
+class _Slots:
+    def __init__(self, fn):
+        self.fn = fn
+
+    def __getitem__(self, k):
+        return self.fn(k)
+
+
+def _narrow_peers():
+    me = lax.axis_index("narrow")
+    yh = me // 4
+    xi = me % 4
+    return ((1 - yh) * 4 + xi, yh * 4 + (xi + 1) % 4, yh * 4 + (xi + 3) % 4)
+
+
+def _dispatch_kernel(x_ref, y_ref, r_ref, sem_w, own_w, sem_y, sem_x1, sem_x2, own_g):
+    nw, _, cols = x_ref.shape
+    halves = 2
+    cw = cols // halves
+    me_w = lax.axis_index("wide")
+    me = lax.axis_index("narrow")
+    barrier = pltpu.get_barrier_semaphore()
+
+    def greet(k, carry):
+        pl.semaphore_signal(barrier, inc=1, device_id=((me_w + k) % nw, me), device_id_type=MESH)
+        return carry
+
+    lax.fori_loop(1, nw, greet, 0)
+    for peer in _narrow_peers():
+        pl.semaphore_signal(barrier, inc=1, device_id=(me_w, peer), device_id_type=MESH)
+    pl.semaphore_wait(barrier, nw - 1 + 3)
+
+    def wide_copy(h, k, peer_of_copy, target):
+        cs = pl.ds(h * cw, cw)
+        return pltpu.make_async_remote_copy(
+            src_ref=x_ref.at[peer_of_copy, :, cs],
+            dst_ref=r_ref.at[target, :, cs],
+            send_sem=sem_w.at[h, k, 0],
+            recv_sem=sem_w.at[h, k, 1],
+            device_id=(peer_of_copy, me),
+            device_id_type=MESH,
+        )
+
+    def wide_start(h):
+        cs = pl.ds(h * cw, cw)
+        own = pltpu.make_async_copy(x_ref.at[me_w, :, cs], r_ref.at[me_w, :, cs], own_w.at[h])
+        own.start()
+
+        def body(k, carry):
+            wide_copy(h, k, (me_w + k) % nw, me_w).start()
+            return carry
+
+        lax.fori_loop(1, nw, body, 0)
+        return own
+
+    def wide_wait(h, own):
+        def body(k, carry):
+            src = (me_w + nw - k) % nw
+            pltpu.make_async_remote_copy(
+                src_ref=x_ref.at[src, :, pl.ds(h * cw, cw)],
+                dst_ref=r_ref.at[src, :, pl.ds(h * cw, cw)],
+                send_sem=sem_w.at[h, k, 0],
+                recv_sem=sem_w.at[h, k, 1],
+                device_id=(src, me),
+                device_id_type=MESH,
+            ).wait_recv()
+            return carry
+
+        lax.fori_loop(1, nw, body, 0)
+        own.wait()
+
+    def wide_sent(h):
+        def body(k, carry):
+            wide_copy(h, k, (me_w + k) % nw, me_w).wait_send()
+            return carry
+
+        lax.fori_loop(1, nw, body, 0)
+
+    pending = []
+    own0 = wide_start(0)
+    wide_wait(0, own0)
+    own1 = wide_start(1)
+    for h in range(halves):
+        if h == 1:
+            wide_wait(1, own1)
+        cs = pl.ds(h * cw, cw)
+        sends, own = _gather_chain(
+            r_ref.at[:, :, cs],
+            lambda k, cs=cs: y_ref.at[k, :, :, cs],
+            sem_y.at[h],
+            sem_x1.at[h],
+            sem_x2.at[h],
+            own_g.at[h],
+        )
+        pending.append((sends, own))
+    for h in range(halves):
+        wide_sent(h)
+        sends, own = pending[h]
+        for c in sends:
+            c.wait_send()
+        own.wait()
+
+
+def _dispatch(x, n_narrow, collective_id):
+    nw, rows, cols = x.shape
     return pl.pallas_call(
-        _gather_kernel,
-        out_shape=jax.ShapeDtypeStruct((n_peers,) + x.shape, x.dtype),
+        _dispatch_kernel,
+        out_shape=jax.ShapeDtypeStruct((n_narrow, nw, rows, cols), x.dtype),
         in_specs=[pl.BlockSpec(memory_space=pl.ANY)],
         out_specs=pl.BlockSpec(memory_space=pl.ANY),
         scratch_shapes=[
+            pltpu.VMEM((nw, rows, cols), x.dtype),
+            pltpu.SemaphoreType.DMA((2, nw, 2)),
             pltpu.SemaphoreType.DMA((2,)),
-            pltpu.SemaphoreType.DMA((4, 2)),
             pltpu.SemaphoreType.DMA((2, 2)),
-            pltpu.SemaphoreType.DMA(()),
+            pltpu.SemaphoreType.DMA((2, 4, 2)),
+            pltpu.SemaphoreType.DMA((2, 2, 2)),
+            pltpu.SemaphoreType.DMA((2,)),
         ],
         compiler_params=pltpu.CompilerParams(collective_id=collective_id, has_side_effects=True),
-        cost_estimate=pl.CostEstimate(flops=0, bytes_accessed=2 * n_peers * nbytes, transcendentals=0),
+        cost_estimate=pl.CostEstimate(
+            flops=0, bytes_accessed=2 * (n_narrow + 1) * x.size * x.dtype.itemsize, transcendentals=0
+        ),
     )(x)
 
 
@@ -271,11 +377,10 @@
     outgoing = jnp.einsum("ts,td->sd", dispatch, tokens, preferred_element_type=jnp.float32).astype(
         jnp.bfloat16
     )
-    received = _exchange(outgoing.reshape(groups_wide, capacity, -1), groups_wide, False, 2, "wide")
-    received = received.reshape(slots_all, -1)
+    gathered = _dispatch(outgoing.reshape(groups_wide, capacity, -1), lax.axis_size("narrow"), 0)
     n_narrow = lax.axis_size("narrow")
     width = tokens.shape[1]
-    slot_rows = _gather(received, n_narrow, 0)
+    slot_rows = gathered.reshape(n_narrow, slots_all, width)
     wg = w_gate[0].reshape(-1, n_narrow, width)
     wu = w_up[0].reshape(-1, n_narrow, width)
     wd = w_down[0].reshape(-1, n_narrow, width)

time: 187 us -> 189 us (1.011)
  local copies, waits for them, and re-layouts: 8.12 us -> 13.1 us
  Pallas kernels: 164 us -> 162 us
    pallas_call x2 -> x1, Pallas kernels: 85.9 us -> 43.5 us  [_exchange(): pl.pallas_call(lambda *refs: _exchange_kernel(n_peers, pick_src, axis, *r...]
    pallas_call x1, Pallas kernels: 36.8 us -> 78 us  [_dispatch(): pl.pallas_call(_dispatch_kernel, out_shape=jax.ShapeDtypeStruct((n_narrow...]
    pallas_call x0 -> x1, local copies, waits for them, and re-layouts: none -> 6.23 us  [_dispatch(): pl.pallas_call(_dispatch_kernel, out_shape=jax.ShapeDtypeStruct((n_narrow...]
    dot_general x1, matrix products: 3.45 us -> 1.48 us  [local(): jnp.einsum('nsd,fnd->sf', slot_rows, wg, preferred_element_type=jnp.float32)]
    reshape x1 -> x0, local copies, waits for them, and re-layouts: 1.95 us -> none  [local(): received = received.reshape(slots_all, -1)]
where the time goes in v7:
time: 189 us; the launch traced here: 188 us
  Pallas kernels  162 us (86%)
  local copies, waits for them, and re-layouts  13.1 us (7%)
  matrix products  9.34 us (5%)
  other arithmetic  3.47 us (2%)
    pallas_call x1, Pallas kernels, _dispatch(): pl.pallas_call(_dispatch_kernel, out_shape=jax.ShapeDtypeStruct((n_narrow...  78 us
    pallas_call x1, Pallas kernels, _exchange(): pl.pallas_call(lambda *refs: _exchange_kernel(n_peers, pick_src, axis, *r...  43.5 us
    pallas_call x1, Pallas kernels, _reduce(): pl.pallas_call(_reduce_kernel, out_shape=jax.ShapeDtypeStruct((rows, cols...  40.6 us
    dot_general x1, matrix products, local(): jnp.einsum('sf,fnd->nsd', hidden, wd, preferred_element_type=jnp.float32)  6.66 us
    pallas_call x1, local copies, waits for them, and re-layouts, _dispatch(): pl.pallas_call(_dispatch_kernel, out_shape=jax.ShapeDtypeStruct((n_narrow...  6.23 us

profile of v7, /device:TPU:1, one launch (start us, length us, event | category | flops | bytes accessed | tf_op | source)
XLA Modules:
  0.0 188.2 jit_solution(13019206106717981799)
XLA Ops:
  0.0 0.0 copy-start
  0.0 0.8 copy.33
  0.8 0.1 eq.42
  1.0 1.8 reduce-window.6
  2.8 0.3 slice_reduce_fusion
  3.1 0.1 eq.38
  3.2 0.1 fusion.34
  3.4 0.1 sub.7
  3.5 0.1 copy.36
  3.6 0.7 multiply_add_fusion
  4.3 0.4 fusion.4
  4.7 0.0 copy-done
  4.7 0.3 convolution_convert_fusion
  5.1 0.9 reshape.41.x_ref
  6.0 78.0 %shard_map.64 = bf16[8,64,14,256]{3,2,1,0:T(8,128)(2,1)} custom-call(bf16[64,14,256]{2,1,0:T(8,128)(2,1)} %reshape.41.x_ref), custom_call_target="tpu_custom_call" | custom-call | bytes 8257536 | tf_op jit(solution)/shard_map/pallas_call | solution.py:217
  84.0 0.0 copy-start.2
  84.1 6.2 %copy.37 = bf16[8,64,14,256]{3,0,2,1:T(8,128)(2,1)S(1)} copy(bf16[8,64,14,256]{3,2,1,0:T(8,128)(2,1)} %shard_map.64) | data formatting | bytes 7340032 | tf_op jit(solution)/shard_map/pallas_call | solution.py:217
  90.3 0.0 copy-start.1
  90.3 0.0 copy-done.2
  90.3 0.2 copy.44
  90.5 0.0 copy-start.3
  90.5 0.0 copy-start.4
  90.5 1.5 fusion.5
  92.0 0.1 copy-done.1
  92.1 0.0 copy-done.3
  92.1 0.2 copy.45
  92.3 0.6 copy-done.4
  92.9 0.2 copy.46
  93.1 6.7 %convert_bitcast_fusion.p_ref = bf16[8,896,256]{2,1,0:T(8,128)(2,1)} fusion(bf16[8,896,256]{2,0,1:T(8,128)(2,1)} %bitcast.49, bf16[176,8,256]{2,1,0:T(8,128)(2,1)S(1)} %bitcast.54, bf16[176,8,256]{2,1,0:T(8,128)(2,1)S(1)} %bitcast.53, f32[896,176]{0,1:T(8,128)S(1)} %fusion.5), kind=kOutput, calls=%fused_computation | convolution fusion | flops 1294626816 | bytes 9412608 | tf_op jit(solution)/shard_map/sf,fnd->nsd/dot_general | solution.py:390
  99.7 0.0 copy-start.5
  99.7 40.6 %shard_map.65 = bf16[896,256]{1,0:T(8,128)(2,1)} custom-call(bf16[8,896,256]{2,1,0:T(8,128)(2,1)} %convert_bitcast_fusion.p_ref), custom_call_target="tpu_custom_call" | custom-call | flops 3670016 | bytes 7340032 | tf_op jit(solution)/shard_map/pallas_call | solution.py:311
  140.4 1.9 %reshape.43.refs_0_ = bf16[64,14,256]{2,1,0:T(8,128)(2,1)} reshape(bf16[896,256]{1,0:T(8,128)(2,1)} %shard_map.65) | data formatting | bytes 917504 | tf_op jit(solution)/shard_map/reshape | solution.py:394
  142.3 43.5 %shard_map.66 = bf16[64,14,256]{2,1,0:T(8,128)(2,1)} custom-call(bf16[64,14,256]{2,1,0:T(8,128)(2,1)} %reshape.43.refs_0_), custom_call_target="tpu_custom_call" | custom-call | bytes 917504 | tf_op jit(solution)/shard_map/pallas_call | solution.py:342
  185.8 1.2 reshape.44
  187.0 0.0 copy-done.5
  187.0 0.3 select_reduce_fusion
  187.4 0.9 convolution_convert_fusion.1
  (4 shorter events, 0.0 us)
Async XLA Ops:
  0.0 4.7 %copy-start = (bf16[128,256]{1,0:T(8,128)(2,1)S(1)}, bf16[128,256]{1,0:T(8,128)(2,1)}, u32[]{:S(2)}) copy-start(bf16[128,256]{1,0:T(8,128)(2,1)} %param.6) | copy-start | bytes 196612
  84.0 6.3 %copy-start.2 = (bf16[1,176,2048]{2,1,0:T(8,128)(2,1)S(1)}, bf16[1,176,2048]{2,1,0:T(8,128)(2,1)}, u32[]{:S(2)}) copy-start(bf16[1,176,2048]{2,1,0:T(8,128)(2,1)} %param.9) | copy-start | bytes 2162692
  90.3 1.8 copy-start.1
  90.5 1.6 copy-start.3
  90.5 2.4 %copy-start.4 = (bf16[1,176,2048]{2,1,0:T(8,128)(2,1)S(1)}, bf16[1,176,2048]{2,1,0:T(8,128)(2,1)}, u32[]{:S(2)}) copy-start(bf16[1,176,2048]{2,1,0:T(8,128)(2,1)} %param.11) | copy-start | bytes 2162692
  99.7 87.2 %copy-start.5 = (bf16[128,6]{0,1:T(8,128)(2,1)S(1)}, bf16[128,6]{0,1:T(8,128)(2,1)}, u32[]{:S(2)}) copy-start(bf16[128,6]{0,1:T(8,128)(2,1)} %param.8) | copy-start | bytes 4612

commit v8 on v7

--- a/solution.py
+++ b/solution.py
@@ -241,10 +241,10 @@
 
     def body(i, carry):
         rows = pl.ds(pl.multiple_of(i * step, step), step)
-        total = srcs[0][rows, :].astype(jnp.float32)
+        total = srcs[0][rows].astype(jnp.float32)
         for src in srcs[1:]:
-            total = total + src[rows, :].astype(jnp.float32)
-        dst[rows, :] = total.astype(dst.dtype)
+            total = total + src[rows].astype(jnp.float32)
+        dst[rows] = total.astype(dst.dtype)
         return carry
 
     lax.fori_loop(0, rows_all // step, body, 0)
@@ -306,18 +306,18 @@
 
 
 def _reduce(p, collective_id):
-    n_peers, rows, cols = p.shape
-    block = pltpu.VMEM((rows, cols), p.dtype)
+    one = p.shape[1:]
+    block = pltpu.VMEM(one, p.dtype)
     return pl.pallas_call(
         _reduce_kernel,
-        out_shape=jax.ShapeDtypeStruct((rows, cols), p.dtype),
+        out_shape=jax.ShapeDtypeStruct(one, p.dtype),
         in_specs=[pl.BlockSpec(memory_space=pltpu.VMEM)],
         out_specs=pl.BlockSpec(memory_space=pltpu.VMEM),
         scratch_shapes=[
-            pltpu.VMEM((3, rows, cols), p.dtype),
-            pltpu.VMEM((3, rows, cols), p.dtype),
-            pltpu.VMEM((2, rows, cols), p.dtype),
-            pltpu.VMEM((2, rows, cols), p.dtype),
+            pltpu.VMEM((3,) + one, p.dtype),
+            pltpu.VMEM((3,) + one, p.dtype),
+            pltpu.VMEM((2,) + one, p.dtype),
+            pltpu.VMEM((2,) + one, p.dtype),
             block,
             block,
             pltpu.SemaphoreType.DMA((3, 2)),
@@ -374,26 +374,26 @@
     combine = jnp.sum(
         jnp.where(hit, route_weights.astype(jnp.float32)[:, :, None], 0.0), axis=1
     ).astype(jnp.bfloat16)
-    outgoing = jnp.einsum("ts,td->sd", dispatch, tokens, preferred_element_type=jnp.float32).astype(
-        jnp.bfloat16
-    )
-    gathered = _dispatch(outgoing.reshape(groups_wide, capacity, -1), lax.axis_size("narrow"), 0)
+    dispatch = dispatch.reshape(tok_rows, groups_wide, capacity)
+    combine = combine.reshape(tok_rows, groups_wide, capacity)
+    outgoing = jnp.einsum(
+        "tbc,td->bcd", dispatch, tokens, preferred_element_type=jnp.float32
+    ).astype(jnp.bfloat16)
     n_narrow = lax.axis_size("narrow")
     width = tokens.shape[1]
-    slot_rows = gathered.reshape(n_narrow, slots_all, width)
+    slot_rows = _dispatch(outgoing, n_narrow, 0)
     wg = w_gate[0].reshape(-1, n_narrow, width)
     wu = w_up[0].reshape(-1, n_narrow, width)
     wd = w_down[0].reshape(-1, n_narrow, width)
-    gate_proj = jnp.einsum("nsd,fnd->sf", slot_rows, wg, preferred_element_type=jnp.float32)
-    up_proj = jnp.einsum("nsd,fnd->sf", slot_rows, wu, preferred_element_type=jnp.float32)
+    gate_proj = jnp.einsum("nbcd,fnd->bcf", slot_rows, wg, preferred_element_type=jnp.float32)
+    up_proj = jnp.einsum("nbcd,fnd->bcf", slot_rows, wu, preferred_element_type=jnp.float32)
     hidden = (jax.nn.silu(gate_proj) * up_proj).astype(jnp.bfloat16)
     partial_value = jnp.einsum(
-        "sf,fnd->nsd", hidden, wd, preferred_element_type=jnp.float32
+        "sf,fnd->nsd", hidden.reshape(slots_all, -1), wd, preferred_element_type=jnp.float32
     ).astype(jnp.bfloat16)
     summed = _reduce(partial_value, 1)
     returned = _exchange(summed.reshape(groups_wide, capacity, -1), groups_wide, False, 3, "wide")
-    returned = returned.reshape(slots_all, -1)
-    mixed = jnp.einsum("ts,sd->td", combine, returned, preferred_element_type=jnp.float32)
+    mixed = jnp.einsum("tbc,bcd->td", combine, returned, preferred_element_type=jnp.float32)
     return mixed.astype(jnp.bfloat16)
 
 

time: 189 us -> 184 us (0.974)
  local copies, waits for them, and re-layouts: 13.1 us -> 6.16 us
    pallas_call x1 -> x0, local copies, waits for them, and re-layouts: 6.23 us -> none  [_dispatch(): pl.pallas_call(_dispatch_kernel, out_shape=jax.ShapeDtypeStruct((n_narrow...]
    dot_general x4 -> x5, matrix products: 9.34 us -> 10.4 us  [the longest x1 3.73 us: local(): jnp.einsum('nbcd,fnd->bcf', slot_rows, wg, preferred_element_type=jnp.flo...]
where the time goes in v8:
time: 184 us; the launch traced here: 182 us
  Pallas kernels  162 us (88%)
  matrix products  10.4 us (6%)
  local copies, waits for them, and re-layouts  6.16 us (3%)
  other arithmetic  3.47 us (2%)
    pallas_call x1, Pallas kernels, _dispatch(): pl.pallas_call(_dispatch_kernel, out_shape=jax.ShapeDtypeStruct((n_narrow...  78.1 us
    pallas_call x1, Pallas kernels, _exchange(): pl.pallas_call(lambda *refs: _exchange_kernel(n_peers, pick_src, axis, *r...  43 us
    pallas_call x1, Pallas kernels, _reduce(): pl.pallas_call(_reduce_kernel, out_shape=jax.ShapeDtypeStruct(one, p.dtyp...  40.7 us
    dot_general x1, matrix products, local(): jnp.einsum('nbcd,fnd->bcf', slot_rows, wg, preferred_element_type=jnp.flo...  3.73 us

profile of v8, /device:TPU:1, one launch (start us, length us, event | category | flops | bytes accessed | tf_op | source)
XLA Modules:
  0.0 182.0 jit_solution(14535235080316466543)
XLA Ops:
  0.0 0.0 copy-start
  0.0 0.8 copy.52
  0.8 0.1 eq.42
  1.0 1.8 reduce-window.6
  2.8 0.3 slice_reduce_fusion
  3.1 0.0 copy-start.2
  3.1 0.1 eq.38
  3.2 0.1 fusion.28
  3.4 0.1 sub.7
  3.5 0.1 copy.55
  3.6 0.7 multiply_add_fusion
  4.3 0.4 fusion.4
  4.7 0.3 copy.57
  5.0 0.1 reshape.41
  5.1 0.0 copy-done
  5.1 0.3 convolution_convert_fusion
  5.4 1.1 copy.59.x_ref
  6.4 78.1 %shard_map.64 = bf16[8,64,14,256]{3,2,1,0:T(8,128)(2,1)} custom-call(bf16[64,14,256]{2,1,0:T(8,128)(2,1)} %copy.59.x_ref), custom_call_target="tpu_custom_call" | custom-call | bytes 8257536 | tf_op jit(solution)/shard_map/pallas_call | solution.py:217
  84.5 0.0 copy-done.2
  84.5 0.2 copy.74
  84.7 0.0 copy-start.3
  84.7 0.0 copy-start.1
  84.7 3.7 %fusion.5 = f32[64,14,176]{2,0,1:T(8,128)S(1)} fusion(bf16[8,64,14,256]{3,2,1,0:T(8,128)(2,1)} %shard_map.64, bf16[176,8,256]{2,1,0:T(8,128)(2,1)S(1)} %bitcast.62), kind=kOutput, calls=%fused_computation.8 | convolution fusion | flops 645922816 | bytes 5021696 | tf_op jit(solution)/shard_map/nbcd,fnd->bcf/dot_general | solution.py:388
  88.4 0.0 copy-done.3
  88.5 0.2 copy.75
  88.6 0.0 copy-done.1
  88.6 0.0 copy-start.4
  88.7 1.5 fusion.14
  90.2 0.3 copy.64
  90.4 0.2 reshape.42
  90.7 0.0 copy-done.4
  90.7 0.2 copy.76
  90.8 2.9 %convert_bitcast_fusion.p_ref = bf16[8,896,256]{2,1,0:T(8,128)(2,1)} fusion(bf16[176,8,256]{2,1,0:T(8,128)(2,1)S(1)} %bitcast.57, bf16[896,176]{1,0:T(8,128)(2,1)S(1)} %reshape.42), kind=kOutput, calls=%fused_computation | convolution fusion | flops 647757824 | bytes 4706304 | tf_op jit(solution)/shard_map/sf,fnd->nsd/dot_general | solution.py:391
  93.8 0.0 copy-start.5
  93.8 40.7 %shard_map.65 = bf16[896,256]{1,0:T(8,128)(2,1)} custom-call(bf16[8,896,256]{2,1,0:T(8,128)(2,1)} %convert_bitcast_fusion.p_ref), custom_call_target="tpu_custom_call" | custom-call | flops 3670016 | bytes 7340032 | tf_op jit(solution)/shard_map/pallas_call | solution.py:311
  134.5 1.9 %reshape.43.refs_0_ = bf16[64,14,256]{2,1,0:T(8,128)(2,1)} reshape(bf16[896,256]{1,0:T(8,128)(2,1)} %shard_map.65) | data formatting | bytes 917504 | tf_op jit(solution)/shard_map/reshape | solution.py:395
  136.4 43.0 %shard_map.66 = bf16[64,14,256]{2,1,0:T(8,128)(2,1)} custom-call(bf16[64,14,256]{2,1,0:T(8,128)(2,1)} %reshape.43.refs_0_), custom_call_target="tpu_custom_call" | custom-call | bytes 917504 | tf_op jit(solution)/shard_map/pallas_call | solution.py:342
  179.4 0.0 copy-done.5
  179.4 0.3 select_reduce_fusion
  179.8 0.2 copy.56
  180.0 0.1 convert_element_type.33
  180.0 2.0 %fusion.17 = bf16[128,256]{1,0:T(8,128)(2,1)} fusion(bf16[64,14,256]{2,1,0:T(8,128)(2,1)} %shard_map.66, bf16[128,64,14]{0,2,1:T(8,128)(2,1)S(1)} %convert_element_type.33), kind=kOutput, calls=%fused_computation.14 | convolution fusion | flops 58753024 | bytes 753664 | tf_op jit(solution)/shard_map/tbc,bcd->td/dot_general | solution.py:396
  (4 shorter events, 0.0 us)
Async XLA Ops:
  0.0 5.1 %copy-start = (bf16[128,256]{1,0:T(8,128)(2,1)S(1)}, bf16[128,256]{1,0:T(8,128)(2,1)}, u32[]{:S(2)}) copy-start(bf16[128,256]{1,0:T(8,128)(2,1)} %param.6) | copy-start | bytes 196612
  3.1 81.4 %copy-start.2 = (bf16[1,176,2048]{2,1,0:T(8,128)(2,1)S(1)}, bf16[1,176,2048]{2,1,0:T(8,128)(2,1)}, u32[]{:S(2)}) copy-start(bf16[1,176,2048]{2,1,0:T(8,128)(2,1)} %param.9) | copy-start | bytes 2162692
  84.7 3.8 %copy-start.3 = (bf16[1,176,2048]{2,1,0:T(8,128)(2,1)S(1)}, bf16[1,176,2048]{2,1,0:T(8,128)(2,1)}, u32[]{:S(2)}) copy-start(bf16[1,176,2048]{2,1,0:T(8,128)(2,1)} %param.10) | copy-start | bytes 2162692
  84.7 3.9 %copy-start.1 = (bf16[8,64,14,256]{3,2,1,0:T(8,128)(2,1)S(1)}, bf16[8,64,14,256]{3,2,1,0:T(8,128)(2,1)}, u32[]{:S(2)}) copy-start(bf16[8,64,14,256]{3,2,1,0:T(8,128)(2,1)} %shard_map.64) | copy-start | bytes 11010052
  88.6 2.0 %copy-start.4 = (bf16[1,176,2048]{2,1,0:T(8,128)(2,1)S(1)}, bf16[1,176,2048]{2,1,0:T(8,128)(2,1)}, u32[]{:S(2)}) copy-start(bf16[1,176,2048]{2,1,0:T(8,128)(2,1)} %param.11) | copy-start | bytes 2162692
  93.8 85.6 %copy-start.5 = (bf16[128,6]{0,1:T(8,128)(2,1)S(1)}, bf16[128,6]{0,1:T(8,128)(2,1)}, u32[]{:S(2)}) copy-start(bf16[128,6]{0,1:T(8,128)(2,1)} %param.8) | copy-start | bytes 4612

commit v9 on v8

--- a/solution.py
+++ b/solution.py
@@ -250,7 +250,7 @@
     lax.fori_loop(0, rows_all // step, body, 0)
 
 
-def _reduce_kernel(p_ref, o_ref, rp, rm, sp, sm, qy, ry, sem_p, sem_m, sem_y):
+def _reduce_kernel(p_ref, r_ref, rp, rm, sp, sm, qy, ry, o_ref, sem_p, sem_m, sem_y, sem_w, own_w):
     me = lax.axis_index("narrow")
     w = lax.axis_index("wide")
     yh = me // 4
@@ -259,10 +259,17 @@
     partner = other * 4 + xi
     right = yh * 4 + (xi + 1) % 4
     left = yh * 4 + (xi + 3) % 4
+    nw = r_ref.shape[0]
     barrier = pltpu.get_barrier_semaphore()
     for peer in (partner, right, left):
         pl.semaphore_signal(barrier, inc=1, device_id=(w, peer), device_id_type=MESH)
-    pl.semaphore_wait(barrier, 3)
+
+    def greet(k, carry):
+        pl.semaphore_signal(barrier, inc=1, device_id=((w + k) % nw, me), device_id_type=MESH)
+        return carry
+
+    lax.fori_loop(1, nw, greet, 0)
+    pl.semaphore_wait(barrier, 3 + nw - 1)
 
     def remote(src, dst, sem, peer):
         return pltpu.make_async_remote_copy(
@@ -300,19 +307,57 @@
     sends.append(c)
     remote(sm.at[1], rm.at[2], sem_m.at[2], right).wait_recv()
     remote(qy, ry, sem_y, partner).wait_recv()
-    _add_into(o_ref, rm.at[2], mine(yh, 0), ry)
+    own_p = mine(yh, 0)
+    cap = o_ref.shape[1]
+    for b in range(nw):
+        rows = pl.ds(b * cap, cap)
+        total = rm[2, rows].astype(jnp.float32) + own_p[rows].astype(jnp.float32)
+        o_ref[b] = (total + ry[rows].astype(jnp.float32)).astype(o_ref.dtype)
+    own = pltpu.make_async_copy(o_ref.at[w], r_ref.at[w], own_w)
+    own.start()
+
+    def wide_copy(k, peer, origin):
+        return pltpu.make_async_remote_copy(
+            src_ref=o_ref.at[peer],
+            dst_ref=r_ref.at[origin],
+            send_sem=sem_w.at[k, 0],
+            recv_sem=sem_w.at[k, 1],
+            device_id=(peer, me),
+            device_id_type=MESH,
+        )
+
+    def send_body(k, carry):
+        wide_copy(k, (w + k) % nw, w).start()
+        return carry
+
+    lax.fori_loop(1, nw, send_body, 0)
+
+    def recv_body(k, carry):
+        src = (w + nw - k) % nw
+        wide_copy(k, src, src).wait_recv()
+        return carry
+
+    lax.fori_loop(1, nw, recv_body, 0)
+
+    def sent_body(k, carry):
+        wide_copy(k, (w + k) % nw, w).wait_send()
+        return carry
+
+    lax.fori_loop(1, nw, sent_body, 0)
+    own.wait()
     for c in sends:
         c.wait_send()
 
 
-def _reduce(p, collective_id):
+def _reduce(p, nw, collective_id):
     one = p.shape[1:]
+    blocks = (nw, one[0] // nw, one[1])
     block = pltpu.VMEM(one, p.dtype)
     return pl.pallas_call(
         _reduce_kernel,
-        out_shape=jax.ShapeDtypeStruct(one, p.dtype),
+        out_shape=jax.ShapeDtypeStruct(blocks, p.dtype),
         in_specs=[pl.BlockSpec(memory_space=pltpu.VMEM)],
-        out_specs=pl.BlockSpec(memory_space=pltpu.VMEM),
+        out_specs=pl.BlockSpec(memory_space=pl.ANY),
         scratch_shapes=[
             pltpu.VMEM((3,) + one, p.dtype),
             pltpu.VMEM((3,) + one, p.dtype),
@@ -320,9 +365,12 @@
             pltpu.VMEM((2,) + one, p.dtype),
             block,
             block,
+            pltpu.VMEM(blocks, p.dtype),
             pltpu.SemaphoreType.DMA((3, 2)),
             pltpu.SemaphoreType.DMA((3, 2)),
             pltpu.SemaphoreType.DMA((2,)),
+            pltpu.SemaphoreType.DMA((nw, 2)),
+            pltpu.SemaphoreType.DMA(()),
         ],
         compiler_params=pltpu.CompilerParams(collective_id=collective_id, has_side_effects=True),
         cost_estimate=pl.CostEstimate(
@@ -391,8 +439,7 @@
     partial_value = jnp.einsum(
         "sf,fnd->nsd", hidden.reshape(slots_all, -1), wd, preferred_element_type=jnp.float32
     ).astype(jnp.bfloat16)
-    summed = _reduce(partial_value, 1)
-    returned = _exchange(summed.reshape(groups_wide, capacity, -1), groups_wide, False, 3, "wide")
+    returned = _reduce(partial_value, groups_wide, 1)
     mixed = jnp.einsum("tbc,bcd->td", combine, returned, preferred_element_type=jnp.float32)
     return mixed.astype(jnp.bfloat16)
 

time: 184 us -> 182 us (0.989); the launches traced: 182 us -> 182 us
  Pallas kernels: 162 us -> 164 us
  local copies, waits for them, and re-layouts: 6.16 us -> 4.22 us
    pallas_call x2 -> x1, Pallas kernels: 83.7 us -> 85.7 us  [_reduce(): pl.pallas_call(_reduce_kernel, out_shape=jax.ShapeDtypeStruct(blocks, p.d...]
    reshape x1 -> x0, local copies, waits for them, and re-layouts: 1.94 us -> none  [local(): summed.reshape(groups_wide, capacity, -1)]
where the time goes in v9:
time: 182 us
  Pallas kernels  164 us (90%)
  matrix products  10.4 us (6%)
  local copies, waits for them, and re-layouts  4.22 us (2%)
  other arithmetic  3.47 us (2%)
    pallas_call x1, Pallas kernels, _reduce(): pl.pallas_call(_reduce_kernel, out_shape=jax.ShapeDtypeStruct(blocks, p.d...  85.7 us
    pallas_call x1, Pallas kernels, _dispatch(): pl.pallas_call(_dispatch_kernel, out_shape=jax.ShapeDtypeStruct((n_narrow...  78.1 us
    dot_general x1, matrix products, local(): jnp.einsum('nbcd,fnd->bcf', slot_rows, wg, preferred_element_type=jnp.flo...  3.73 us

profile of v9, /device:TPU:1, one launch (start us, length us, event | category | flops | bytes accessed | tf_op | source)
XLA Modules:
  0.0 182.2 jit_solution(6831615911165642974)
XLA Ops:
  0.0 0.0 copy-start
  0.0 0.8 copy.49
  0.8 0.1 eq.42
  1.0 1.8 reduce-window.6
  2.8 0.3 slice_reduce_fusion
  3.1 0.0 copy-start.2
  3.1 0.1 eq.38
  3.2 0.1 fusion.28
  3.4 0.1 sub.7
  3.5 0.1 copy.52
  3.6 0.7 multiply_add_fusion
  4.3 0.4 fusion.4
  4.7 0.3 copy.54
  5.0 0.1 reshape.38
  5.1 0.0 copy-done
  5.1 0.3 convolution_convert_fusion
  5.4 1.1 copy.56.x_ref
  6.4 78.1 %shard_map.64 = bf16[8,64,14,256]{3,2,1,0:T(8,128)(2,1)} custom-call(bf16[64,14,256]{2,1,0:T(8,128)(2,1)} %copy.56.x_ref), custom_call_target="tpu_custom_call" | custom-call | bytes 8257536 | tf_op jit(solution)/shard_map/pallas_call | solution.py:217
  84.5 0.0 copy-done.2
  84.5 0.2 copy.71
  84.7 0.0 copy-start.3
  84.7 0.0 copy-start.1
  84.7 3.7 %fusion.5 = f32[64,14,176]{2,0,1:T(8,128)S(1)} fusion(bf16[8,64,14,256]{3,2,1,0:T(8,128)(2,1)} %shard_map.64, bf16[176,8,256]{2,1,0:T(8,128)(2,1)S(1)} %bitcast.62), kind=kOutput, calls=%fused_computation.8 | convolution fusion | flops 645922816 | bytes 5021696 | tf_op jit(solution)/shard_map/nbcd,fnd->bcf/dot_general | solution.py:436
  88.4 0.0 copy-done.3
  88.5 0.2 copy.72
  88.6 0.0 copy-done.1
  88.6 0.0 copy-start.4
  88.7 1.5 fusion.14
  90.2 0.3 copy.61
  90.4 0.2 reshape.39
  90.7 0.0 copy-done.4
  90.7 0.2 copy.73
  90.8 2.9 %convert_bitcast_fusion.p_ref = bf16[8,896,256]{2,1,0:T(8,128)(2,1)} fusion(bf16[176,8,256]{2,1,0:T(8,128)(2,1)S(1)} %bitcast.57, bf16[896,176]{1,0:T(8,128)(2,1)S(1)} %reshape.39), kind=kOutput, calls=%fused_computation | convolution fusion | flops 647757824 | bytes 4706304 | tf_op jit(solution)/shard_map/sf,fnd->nsd/dot_general | solution.py:439
  93.8 0.0 copy-start.5
  93.8 85.7 %shard_map.65 = bf16[64,14,256]{2,1,0:T(8,128)(2,1)} custom-call(bf16[8,896,256]{2,1,0:T(8,128)(2,1)} %convert_bitcast_fusion.p_ref), custom_call_target="tpu_custom_call" | custom-call | flops 3670016 | bytes 7340032 | tf_op jit(solution)/shard_map/pallas_call | solution.py:356
  179.5 0.0 copy-done.5
  179.5 0.3 select_reduce_fusion
  179.9 0.2 copy.53
  180.1 0.1 convert_element_type.33
  180.1 2.0 %fusion.17 = bf16[128,256]{1,0:T(8,128)(2,1)} fusion(bf16[64,14,256]{2,1,0:T(8,128)(2,1)} %shard_map.65, bf16[128,64,14]{0,2,1:T(8,128)(2,1)S(1)} %convert_element_type.33), kind=kOutput, calls=%fused_computation.14 | convolution fusion | flops 58753024 | bytes 753664 | tf_op jit(solution)/shard_map/tbc,bcd->td/dot_general | solution.py:443
  (4 shorter events, 0.0 us)
Async XLA Ops:
  0.0 5.1 %copy-start = (bf16[128,256]{1,0:T(8,128)(2,1)S(1)}, bf16[128,256]{1,0:T(8,128)(2,1)}, u32[]{:S(2)}) copy-start(bf16[128,256]{1,0:T(8,128)(2,1)} %param.6) | copy-start | bytes 196612
  3.1 81.4 %copy-start.2 = (bf16[1,176,2048]{2,1,0:T(8,128)(2,1)S(1)}, bf16[1,176,2048]{2,1,0:T(8,128)(2,1)}, u32[]{:S(2)}) copy-start(bf16[1,176,2048]{2,1,0:T(8,128)(2,1)} %param.9) | copy-start | bytes 2162692
  84.7 3.8 %copy-start.3 = (bf16[1,176,2048]{2,1,0:T(8,128)(2,1)S(1)}, bf16[1,176,2048]{2,1,0:T(8,128)(2,1)}, u32[]{:S(2)}) copy-start(bf16[1,176,2048]{2,1,0:T(8,128)(2,1)} %param.10) | copy-start | bytes 2162692
  84.7 3.9 %copy-start.1 = (bf16[8,64,14,256]{3,2,1,0:T(8,128)(2,1)S(1)}, bf16[8,64,14,256]{3,2,1,0:T(8,128)(2,1)}, u32[]{:S(2)}) copy-start(bf16[8,64,14,256]{3,2,1,0:T(8,128)(2,1)} %shard_map.64) | copy-start | bytes 11010052
  88.6 2.0 %copy-start.4 = (bf16[1,176,2048]{2,1,0:T(8,128)(2,1)S(1)}, bf16[1,176,2048]{2,1,0:T(8,128)(2,1)}, u32[]{:S(2)}) copy-start(bf16[1,176,2048]{2,1,0:T(8,128)(2,1)} %param.11) | copy-start | bytes 2162692
  93.8 85.8 %copy-start.5 = (bf16[128,6]{0,1:T(8,128)(2,1)S(1)}, bf16[128,6]{0,1:T(8,128)(2,1)}, u32[]{:S(2)}) copy-start(bf16[128,6]{0,1:T(8,128)(2,1)} %param.8) | copy-start | bytes 4612

commit v10 on v9

--- a/solution.py
+++ b/solution.py
@@ -281,38 +281,46 @@
             device_id_type=MESH,
         )
 
-    mine = lambda h, k: p_ref.at[h * 4 + (xi + k) % 4]
-    sends = []
-    c = remote(mine(other, 3), rp.at[0], sem_p.at[0], right)
-    c.start()
-    sends.append(c)
-    c = remote(mine(yh, 1), rm.at[0], sem_m.at[0], left)
-    c.start()
-    sends.append(c)
-    for step, (kp, km) in enumerate(((2, 2), (1, 3))):
-        remote(sp.at[step], rp.at[step], sem_p.at[step], left).wait_recv()
-        _add_into(sp.at[step], rp.at[step], mine(other, kp))
-        c = remote(sp.at[step], rp.at[step + 1], sem_p.at[step + 1], right)
-        c.start()
-        sends.append(c)
-        remote(sm.at[step], rm.at[step], sem_m.at[step], right).wait_recv()
-        _add_into(sm.at[step], rm.at[step], mine(yh, km))
-        c = remote(sm.at[step], rm.at[step + 1], sem_m.at[step + 1], left)
-        c.start()
-        sends.append(c)
-    remote(qy, rp.at[2], sem_p.at[2], left).wait_recv()
-    _add_into(qy, rp.at[2], mine(other, 0))
+    half = p_ref.shape[2] // 2
+    cols = (pl.ds(0, half), pl.ds(half, half))
+    peers = (right, left)
+    froms = (left, right)
+    offsets = ((3, 2, 1), (1, 2, 3))
+
+    def plane(h, rb, sb, sem):
+        sends = []
+        for d in (0, 1):
+            src = p_ref.at[h * 4 + (xi + offsets[d][0]) % 4, :, cols[d]]
+            c = remote(src, rb.at[d, 0], sem.at[d, 0], peers[d])
+            c.start()
+            sends.append(c)
+        for step in (1, 2):
+            for d in (0, 1):
+                remote(sb.at[d, step - 1], rb.at[d, step - 1], sem.at[d, step - 1], froms[d]).wait_recv()
+                term = p_ref.at[h * 4 + (xi + offsets[d][step]) % 4, :, cols[d]]
+                _add_into(sb.at[d, step - 1], rb.at[d, step - 1], term)
+                c = remote(sb.at[d, step - 1], rb.at[d, step], sem.at[d, step], peers[d])
+                c.start()
+                sends.append(c)
+        for d in (0, 1):
+            remote(sb.at[d, 1], rb.at[d, 2], sem.at[d, 2], froms[d]).wait_recv()
+        return sends
+
+    sends = plane(other, rp, sp, sem_p)
+    for d in (0, 1):
+        _add_into(qy.at[:, cols[d]], rp.at[d, 2], p_ref.at[other * 4 + xi, :, cols[d]])
     c = remote(qy, ry, sem_y, partner)
     c.start()
     sends.append(c)
-    remote(sm.at[1], rm.at[2], sem_m.at[2], right).wait_recv()
+    sends += plane(yh, rm, sm, sem_m)
     remote(qy, ry, sem_y, partner).wait_recv()
-    own_p = mine(yh, 0)
+    own_p = p_ref.at[yh * 4 + xi]
     cap = o_ref.shape[1]
     for b in range(nw):
         rows = pl.ds(b * cap, cap)
-        total = rm[2, rows].astype(jnp.float32) + own_p[rows].astype(jnp.float32)
-        o_ref[b] = (total + ry[rows].astype(jnp.float32)).astype(o_ref.dtype)
+        for d in (0, 1):
+            total = rm[d, 2, rows, :].astype(jnp.float32) + own_p[rows, cols[d]].astype(jnp.float32)
+            o_ref[b, :, cols[d]] = (total + ry[rows, cols[d]].astype(jnp.float32)).astype(o_ref.dtype)
     own = pltpu.make_async_copy(o_ref.at[w], r_ref.at[w], own_w)
     own.start()
 
@@ -359,15 +367,15 @@
         in_specs=[pl.BlockSpec(memory_space=pltpu.VMEM)],
         out_specs=pl.BlockSpec(memory_space=pl.ANY),
         scratch_shapes=[
-            pltpu.VMEM((3,) + one, p.dtype),
-            pltpu.VMEM((3,) + one, p.dtype),
-            pltpu.VMEM((2,) + one, p.dtype),
-            pltpu.VMEM((2,) + one, p.dtype),
+            pltpu.VMEM((2, 3, one[0], one[1] // 2), p.dtype),
+            pltpu.VMEM((2, 3, one[0], one[1] // 2), p.dtype),
+            pltpu.VMEM((2, 2, one[0], one[1] // 2), p.dtype),
+            pltpu.VMEM((2, 2, one[0], one[1] // 2), p.dtype),
             block,
             block,
             pltpu.VMEM(blocks, p.dtype),
-            pltpu.SemaphoreType.DMA((3, 2)),
-            pltpu.SemaphoreType.DMA((3, 2)),
+            pltpu.SemaphoreType.DMA((2, 3, 2)),
+            pltpu.SemaphoreType.DMA((2, 3, 2)),
             pltpu.SemaphoreType.DMA((2,)),
             pltpu.SemaphoreType.DMA((nw, 2)),
             pltpu.SemaphoreType.DMA(()),

time: 182 us -> 177 us (0.973)
  Pallas kernels: 164 us -> 158 us
    pallas_call x1, Pallas kernels: 85.7 us -> 80.2 us  [_reduce(): pl.pallas_call(_reduce_kernel, out_shape=jax.ShapeDtypeStruct(blocks, p.d...]
where the time goes in v10:
time: 177 us
  Pallas kernels  158 us (89%)
  matrix products  10.4 us (6%)
  local copies, waits for them, and re-layouts  4.22 us (2%)
  other arithmetic  3.47 us (2%)
    pallas_call x1, Pallas kernels, _reduce(): pl.pallas_call(_reduce_kernel, out_shape=jax.ShapeDtypeStruct(blocks, p.d...  80.2 us
    pallas_call x1, Pallas kernels, _dispatch(): pl.pallas_call(_dispatch_kernel, out_shape=jax.ShapeDtypeStruct((n_narrow...  78.1 us
    dot_general x1, matrix products, local(): jnp.einsum('nbcd,fnd->bcf', slot_rows, wg, preferred_element_type=jnp.flo...  3.73 us

profile of v10, /device:TPU:1, one launch (start us, length us, event | category | flops | bytes accessed | tf_op | source)
XLA Modules:
  0.0 176.6 jit_solution(14962690589675782891)
XLA Ops:
  0.0 0.0 copy-start
  0.0 0.8 copy.49
  0.8 0.1 eq.42
  1.0 1.8 %reduce-window.6 = s32[64,6,128]{2,0,1:T(8,128)S(1)} reduce-window(s32[64,6,128]{2,0,1:T(8,128)S(1)} %fusion.29, s32[]{:T(128)} %constant.7.clone.1), window={size=1x1x128 pad=0_0x0_0x127_0}, to_apply=%region_0.0 | reduce-window | flops 6242304 | bytes 393220 | tf_op jit(solution)/shard_map/reduce-window
  2.8 0.3 slice_reduce_fusion
  3.1 0.0 copy-start.2
  3.1 0.1 eq.38
  3.2 0.1 fusion.28
  3.4 0.1 sub.7
  3.5 0.1 copy.52
  3.6 0.7 multiply_add_fusion
  4.3 0.4 fusion.4
  4.7 0.3 copy.54
  5.0 0.1 reshape.38
  5.1 0.0 copy-done
  5.1 0.3 convolution_convert_fusion
  5.4 1.1 copy.56.x_ref
  6.4 78.1 %shard_map.64 = bf16[8,64,14,256]{3,2,1,0:T(8,128)(2,1)} custom-call(bf16[64,14,256]{2,1,0:T(8,128)(2,1)} %copy.56.x_ref), custom_call_target="tpu_custom_call" | custom-call | bytes 8257536 | tf_op jit(solution)/shard_map/pallas_call | solution.py:217
  84.5 0.0 copy-done.2
  84.5 0.2 copy.71
  84.7 0.0 copy-start.3
  84.7 0.0 copy-start.1
  84.7 3.7 %fusion.5 = f32[64,14,176]{2,0,1:T(8,128)S(1)} fusion(bf16[8,64,14,256]{3,2,1,0:T(8,128)(2,1)} %shard_map.64, bf16[176,8,256]{2,1,0:T(8,128)(2,1)S(1)} %bitcast.62), kind=kOutput, calls=%fused_computation.8 | convolution fusion | flops 645922816 | bytes 5021696 | tf_op jit(solution)/shard_map/nbcd,fnd->bcf/dot_general | solution.py:444
  88.4 0.0 copy-done.3
  88.5 0.2 copy.72
  88.6 0.0 copy-done.1
  88.6 0.0 copy-start.4
  88.7 1.5 fusion.14
  90.2 0.3 copy.61
  90.4 0.2 reshape.39
  90.7 0.0 copy-done.4
  90.7 0.2 copy.73
  90.8 2.9 %convert_bitcast_fusion.p_ref = bf16[8,896,256]{2,1,0:T(8,128)(2,1)} fusion(bf16[176,8,256]{2,1,0:T(8,128)(2,1)S(1)} %bitcast.57, bf16[896,176]{1,0:T(8,128)(2,1)S(1)} %reshape.39), kind=kOutput, calls=%fused_computation | convolution fusion | flops 647757824 | bytes 4706304 | tf_op jit(solution)/shard_map/sf,fnd->nsd/dot_general | solution.py:447
  93.8 0.0 copy-start.5
  93.8 80.2 %shard_map.65 = bf16[64,14,256]{2,1,0:T(8,128)(2,1)} custom-call(bf16[8,896,256]{2,1,0:T(8,128)(2,1)} %convert_bitcast_fusion.p_ref), custom_call_target="tpu_custom_call" | custom-call | flops 3670016 | bytes 7340032 | tf_op jit(solution)/shard_map/pallas_call | solution.py:364
  174.0 0.0 copy-done.5
  174.0 0.3 select_reduce_fusion
  174.4 0.2 copy.53
  174.6 0.1 convert_element_type.33
  174.6 2.0 %fusion.17 = bf16[128,256]{1,0:T(8,128)(2,1)} fusion(bf16[64,14,256]{2,1,0:T(8,128)(2,1)} %shard_map.65, bf16[128,64,14]{0,2,1:T(8,128)(2,1)S(1)} %convert_element_type.33), kind=kOutput, calls=%fused_computation.14 | convolution fusion | flops 58753024 | bytes 753664 | tf_op jit(solution)/shard_map/tbc,bcd->td/dot_general | solution.py:451
  (4 shorter events, 0.0 us)
Async XLA Ops:
  0.0 5.1 %copy-start = (bf16[128,256]{1,0:T(8,128)(2,1)S(1)}, bf16[128,256]{1,0:T(8,128)(2,1)}, u32[]{:S(2)}) copy-start(bf16[128,256]{1,0:T(8,128)(2,1)} %param.6) | copy-start | bytes 196612
  3.1 81.4 %copy-start.2 = (bf16[1,176,2048]{2,1,0:T(8,128)(2,1)S(1)}, bf16[1,176,2048]{2,1,0:T(8,128)(2,1)}, u32[]{:S(2)}) copy-start(bf16[1,176,2048]{2,1,0:T(8,128)(2,1)} %param.9) | copy-start | bytes 2162692
  84.7 3.8 %copy-start.3 = (bf16[1,176,2048]{2,1,0:T(8,128)(2,1)S(1)}, bf16[1,176,2048]{2,1,0:T(8,128)(2,1)}, u32[]{:S(2)}) copy-start(bf16[1,176,2048]{2,1,0:T(8,128)(2,1)} %param.10) | copy-start | bytes 2162692
  84.7 3.9 %copy-start.1 = (bf16[8,64,14,256]{3,2,1,0:T(8,128)(2,1)S(1)}, bf16[8,64,14,256]{3,2,1,0:T(8,128)(2,1)}, u32[]{:S(2)}) copy-start(bf16[8,64,14,256]{3,2,1,0:T(8,128)(2,1)} %shard_map.64) | copy-start | bytes 11010052
  88.6 2.0 %copy-start.4 = (bf16[1,176,2048]{2,1,0:T(8,128)(2,1)S(1)}, bf16[1,176,2048]{2,1,0:T(8,128)(2,1)}, u32[]{:S(2)}) copy-start(bf16[1,176,2048]{2,1,0:T(8,128)(2,1)} %param.11) | copy-start | bytes 2162692
  93.8 80.2 %copy-start.5 = (bf16[128,6]{0,1:T(8,128)(2,1)S(1)}, bf16[128,6]{0,1:T(8,128)(2,1)}, u32[]{:S(2)}) copy-start(bf16[128,6]{0,1:T(8,128)(2,1)} %param.8) | copy-start | bytes 4612

commit v11 on v10

--- a/solution.py
+++ b/solution.py
@@ -126,7 +126,7 @@
 
 def _dispatch_kernel(x_ref, y_ref, r_ref, sem_w, own_w, sem_y, sem_x1, sem_x2, own_g):
     nw, _, cols = x_ref.shape
-    halves = 2
+    halves = 1
     cw = cols // halves
     me_w = lax.axis_index("wide")
     me = lax.axis_index("narrow")
@@ -190,7 +190,8 @@
     pending = []
     own0 = wide_start(0)
     wide_wait(0, own0)
-    own1 = wide_start(1)
+    if halves > 1:
+        own1 = wide_start(1)
     for h in range(halves):
         if h == 1:
             wide_wait(1, own1)

time: 177 us -> 179 us (1.011)
  Pallas kernels: 158 us -> 160 us
    pallas_call x1, Pallas kernels: 78.1 us -> 84.7 us  [_dispatch(): pl.pallas_call(_dispatch_kernel, out_shape=jax.ShapeDtypeStruct((n_narrow...]
    pallas_call x1, Pallas kernels: 80.2 us -> 75.5 us  [_reduce(): pl.pallas_call(_reduce_kernel, out_shape=jax.ShapeDtypeStruct(blocks, p.d...]
where the time goes in v11:
time: 179 us; the launch traced here: 178 us
  Pallas kernels  160 us (89%)
  matrix products  10.4 us (6%)
  local copies, waits for them, and re-layouts  4.22 us (2%)
  other arithmetic  3.47 us (2%)
    pallas_call x1, Pallas kernels, _dispatch(): pl.pallas_call(_dispatch_kernel, out_shape=jax.ShapeDtypeStruct((n_narrow...  84.7 us
    pallas_call x1, Pallas kernels, _reduce(): pl.pallas_call(_reduce_kernel, out_shape=jax.ShapeDtypeStruct(blocks, p.d...  75.5 us
    dot_general x1, matrix products, local(): jnp.einsum('nbcd,fnd->bcf', slot_rows, wg, preferred_element_type=jnp.flo...  3.73 us

profile of v11, /device:TPU:1, one launch (start us, length us, event | category | flops | bytes accessed | tf_op | source)
XLA Modules:
  0.0 178.5 jit_solution(14531489850014870706)
XLA Ops:
  0.0 0.0 copy-start
  0.0 0.8 copy.49
  0.8 0.1 eq.42
  1.0 1.8 %reduce-window.6 = s32[64,6,128]{2,0,1:T(8,128)S(1)} reduce-window(s32[64,6,128]{2,0,1:T(8,128)S(1)} %fusion.29, s32[]{:T(128)} %constant.7.clone.1), window={size=1x1x128 pad=0_0x0_0x127_0}, to_apply=%region_0.0 | reduce-window | flops 6242304 | bytes 393220 | tf_op jit(solution)/shard_map/reduce-window
  2.8 0.3 slice_reduce_fusion
  3.1 0.0 copy-start.2
  3.1 0.1 eq.38
  3.2 0.1 fusion.28
  3.4 0.1 sub.7
  3.5 0.1 copy.52
  3.6 0.7 multiply_add_fusion
  4.3 0.4 fusion.4
  4.7 0.3 copy.54
  5.0 0.1 reshape.38
  5.1 0.0 copy-done
  5.1 0.3 convolution_convert_fusion
  5.4 1.1 copy.56.x_ref
  6.4 84.7 %shard_map.64 = bf16[8,64,14,256]{3,2,1,0:T(8,128)(2,1)} custom-call(bf16[64,14,256]{2,1,0:T(8,128)(2,1)} %copy.56.x_ref), custom_call_target="tpu_custom_call" | custom-call | bytes 8257536 | tf_op jit(solution)/shard_map/pallas_call | solution.py:218
  91.1 0.0 copy-done.2
  91.1 0.2 copy.71
  91.3 0.0 copy-start.3
  91.3 0.0 copy-start.1
  91.3 3.7 %fusion.5 = f32[64,14,176]{2,0,1:T(8,128)S(1)} fusion(bf16[8,64,14,256]{3,2,1,0:T(8,128)(2,1)} %shard_map.64, bf16[176,8,256]{2,1,0:T(8,128)(2,1)S(1)} %bitcast.62), kind=kOutput, calls=%fused_computation.8 | convolution fusion | flops 645922816 | bytes 5021696 | tf_op jit(solution)/shard_map/nbcd,fnd->bcf/dot_general | solution.py:445
  95.0 0.0 copy-done.3
  95.1 0.2 copy.72
  95.2 0.0 copy-done.1
  95.2 0.0 copy-start.4
  95.3 1.5 fusion.14
  96.8 0.3 copy.61
  97.0 0.2 reshape.39
  97.3 0.0 copy-done.4
  97.3 0.2 copy.73
  97.4 2.9 %convert_bitcast_fusion.p_ref = bf16[8,896,256]{2,1,0:T(8,128)(2,1)} fusion(bf16[176,8,256]{2,1,0:T(8,128)(2,1)S(1)} %bitcast.57, bf16[896,176]{1,0:T(8,128)(2,1)S(1)} %reshape.39), kind=kOutput, calls=%fused_computation | convolution fusion | flops 647757824 | bytes 4706304 | tf_op jit(solution)/shard_map/sf,fnd->nsd/dot_general | solution.py:448
  100.4 0.0 copy-start.5
  100.4 75.5 %shard_map.65 = bf16[64,14,256]{2,1,0:T(8,128)(2,1)} custom-call(bf16[8,896,256]{2,1,0:T(8,128)(2,1)} %convert_bitcast_fusion.p_ref), custom_call_target="tpu_custom_call" | custom-call | flops 3670016 | bytes 7340032 | tf_op jit(solution)/shard_map/pallas_call | solution.py:365
  175.9 0.0 copy-done.5
  175.9 0.3 select_reduce_fusion
  176.2 0.2 copy.53
  176.4 0.1 convert_element_type.33
  176.5 2.0 %fusion.17 = bf16[128,256]{1,0:T(8,128)(2,1)} fusion(bf16[64,14,256]{2,1,0:T(8,128)(2,1)} %shard_map.65, bf16[128,64,14]{0,2,1:T(8,128)(2,1)S(1)} %convert_element_type.33), kind=kOutput, calls=%fused_computation.14 | convolution fusion | flops 58753024 | bytes 753664 | tf_op jit(solution)/shard_map/tbc,bcd->td/dot_general | solution.py:452
  (4 shorter events, 0.0 us)
Async XLA Ops:
  0.0 5.1 %copy-start = (bf16[128,256]{1,0:T(8,128)(2,1)S(1)}, bf16[128,256]{1,0:T(8,128)(2,1)}, u32[]{:S(2)}) copy-start(bf16[128,256]{1,0:T(8,128)(2,1)} %param.6) | copy-start | bytes 196612
  3.1 88.0 %copy-start.2 = (bf16[1,176,2048]{2,1,0:T(8,128)(2,1)S(1)}, bf16[1,176,2048]{2,1,0:T(8,128)(2,1)}, u32[]{:S(2)}) copy-start(bf16[1,176,2048]{2,1,0:T(8,128)(2,1)} %param.9) | copy-start | bytes 2162692
  91.3 3.8 %copy-start.3 = (bf16[1,176,2048]{2,1,0:T(8,128)(2,1)S(1)}, bf16[1,176,2048]{2,1,0:T(8,128)(2,1)}, u32[]{:S(2)}) copy-start(bf16[1,176,2048]{2,1,0:T(8,128)(2,1)} %param.10) | copy-start | bytes 2162692
  91.3 3.9 %copy-start.1 = (bf16[8,64,14,256]{3,2,1,0:T(8,128)(2,1)S(1)}, bf16[8,64,14,256]{3,2,1,0:T(8,128)(2,1)}, u32[]{:S(2)}) copy-start(bf16[8,64,14,256]{3,2,1,0:T(8,128)(2,1)} %shard_map.64) | copy-start | bytes 11010052
  95.2 2.0 %copy-start.4 = (bf16[1,176,2048]{2,1,0:T(8,128)(2,1)S(1)}, bf16[1,176,2048]{2,1,0:T(8,128)(2,1)}, u32[]{:S(2)}) copy-start(bf16[1,176,2048]{2,1,0:T(8,128)(2,1)} %param.11) | copy-start | bytes 2162692
  100.4 75.5 %copy-start.5 = (bf16[128,6]{0,1:T(8,128)(2,1)S(1)}, bf16[128,6]{0,1:T(8,128)(2,1)}, u32[]{:S(2)}) copy-start(bf16[128,6]{0,1:T(8,128)(2,1)} %param.8) | copy-start | bytes 4612

commit v12 on v10

--- a/solution.py
+++ b/solution.py
@@ -52,7 +52,7 @@
     own.wait()
 
 
-def _gather_chain(x_ref, slot_of, sem_y, sem_x1, sem_x2, own_sem):
+def _gather_chain(x_ref, slot_of, sem_y, sem_x1, sem_x2, own_sem, after_start=None):
     me = lax.axis_index("narrow")
     w = lax.axis_index("wide")
     yh = me // 4
@@ -83,6 +83,8 @@
     ]
     for c in c1:
         c.start()
+    if after_start is not None:
+        after_start()
     remote(x_ref, partner, (sem_y.at[0], sem_y.at[1]), partner).wait_recv()
     c2 = [
         remote(y_ref.at[partner], partner, (sem_x1.at[2, 0], sem_x1.at[2, 1]), right),
@@ -190,10 +192,10 @@
     pending = []
     own0 = wide_start(0)
     wide_wait(0, own0)
-    own1 = wide_start(1)
+    owns = []
     for h in range(halves):
         if h == 1:
-            wide_wait(1, own1)
+            wide_wait(1, owns[0])
         cs = pl.ds(h * cw, cw)
         sends, own = _gather_chain(
             r_ref.at[:, :, cs],
@@ -202,6 +204,7 @@
             sem_x1.at[h],
             sem_x2.at[h],
             own_g.at[h],
+            (lambda: owns.append(wide_start(1))) if h == 0 else None,
         )
         pending.append((sends, own))
     for h in range(halves):

time: 177 us -> 176 us (level)
    pallas_call x1, Pallas kernels: 78.1 us -> 76.3 us  [_dispatch(): pl.pallas_call(_dispatch_kernel, out_shape=jax.ShapeDtypeStruct((n_narrow...]
where the time goes in v12:
time: 176 us; the launch traced here: 175 us
  Pallas kernels  157 us (89%)
  matrix products  10.4 us (6%)
  local copies, waits for them, and re-layouts  4.22 us (2%)
  other arithmetic  3.47 us (2%)
    pallas_call x1, Pallas kernels, _reduce(): pl.pallas_call(_reduce_kernel, out_shape=jax.ShapeDtypeStruct(blocks, p.d...  80.7 us
    pallas_call x1, Pallas kernels, _dispatch(): pl.pallas_call(_dispatch_kernel, out_shape=jax.ShapeDtypeStruct((n_narrow...  76.3 us
    dot_general x1, matrix products, local(): jnp.einsum('nbcd,fnd->bcf', slot_rows, wg, preferred_element_type=jnp.flo...  3.73 us

profile of v12, /device:TPU:1, one launch (start us, length us, event | category | flops | bytes accessed | tf_op | source)
XLA Modules:
  0.0 175.3 jit_solution(139600125770993883)
XLA Ops:
  0.0 0.0 copy-start
  0.0 0.8 copy.49
  0.8 0.1 eq.42
  1.0 1.8 %reduce-window.6 = s32[64,6,128]{2,0,1:T(8,128)S(1)} reduce-window(s32[64,6,128]{2,0,1:T(8,128)S(1)} %fusion.29, s32[]{:T(128)} %constant.7.clone.1), window={size=1x1x128 pad=0_0x0_0x127_0}, to_apply=%region_0.0 | reduce-window | flops 6242304 | bytes 393220 | tf_op jit(solution)/shard_map/reduce-window
  2.8 0.3 slice_reduce_fusion
  3.1 0.0 copy-start.2
  3.1 0.1 eq.38
  3.2 0.1 fusion.28
  3.4 0.1 sub.7
  3.5 0.1 copy.52
  3.6 0.7 multiply_add_fusion
  4.3 0.4 fusion.4
  4.7 0.3 copy.54
  5.0 0.1 reshape.38
  5.1 0.0 copy-done
  5.1 0.3 convolution_convert_fusion
  5.4 1.1 copy.56.x_ref
  6.4 76.3 %shard_map.64 = bf16[8,64,14,256]{3,2,1,0:T(8,128)(2,1)} custom-call(bf16[64,14,256]{2,1,0:T(8,128)(2,1)} %copy.56.x_ref), custom_call_target="tpu_custom_call" | custom-call | bytes 8257536 | tf_op jit(solution)/shard_map/pallas_call | solution.py:220
  82.7 0.0 copy-done.2
  82.7 0.2 copy.71
  82.9 0.0 copy-start.3
  82.9 0.0 copy-start.1
  82.9 3.7 %fusion.5 = f32[64,14,176]{2,0,1:T(8,128)S(1)} fusion(bf16[8,64,14,256]{3,2,1,0:T(8,128)(2,1)} %shard_map.64, bf16[176,8,256]{2,1,0:T(8,128)(2,1)S(1)} %bitcast.62), kind=kOutput, calls=%fused_computation.8 | convolution fusion | flops 645922816 | bytes 5021696 | tf_op jit(solution)/shard_map/nbcd,fnd->bcf/dot_general | solution.py:447
  86.7 0.0 copy-done.3
  86.7 0.2 copy.72
  86.8 0.0 copy-done.1
  86.9 0.0 copy-start.4
  86.9 1.5 fusion.14
  88.4 0.3 copy.61
  88.6 0.2 reshape.39
  88.9 0.0 copy-done.4
  88.9 0.2 copy.73
  89.1 2.9 %convert_bitcast_fusion.p_ref = bf16[8,896,256]{2,1,0:T(8,128)(2,1)} fusion(bf16[176,8,256]{2,1,0:T(8,128)(2,1)S(1)} %bitcast.57, bf16[896,176]{1,0:T(8,128)(2,1)S(1)} %reshape.39), kind=kOutput, calls=%fused_computation | convolution fusion | flops 647757824 | bytes 4706304 | tf_op jit(solution)/shard_map/sf,fnd->nsd/dot_general | solution.py:450
  92.0 0.0 copy-start.5
  92.0 80.7 %shard_map.65 = bf16[64,14,256]{2,1,0:T(8,128)(2,1)} custom-call(bf16[8,896,256]{2,1,0:T(8,128)(2,1)} %convert_bitcast_fusion.p_ref), custom_call_target="tpu_custom_call" | custom-call | flops 3670016 | bytes 7340032 | tf_op jit(solution)/shard_map/pallas_call | solution.py:367
  172.7 0.0 copy-done.5
  172.7 0.3 select_reduce_fusion
  173.0 0.2 copy.53
  173.2 0.1 convert_element_type.33
  173.3 2.0 %fusion.17 = bf16[128,256]{1,0:T(8,128)(2,1)} fusion(bf16[64,14,256]{2,1,0:T(8,128)(2,1)} %shard_map.65, bf16[128,64,14]{0,2,1:T(8,128)(2,1)S(1)} %convert_element_type.33), kind=kOutput, calls=%fused_computation.14 | convolution fusion | flops 58753024 | bytes 753664 | tf_op jit(solution)/shard_map/tbc,bcd->td/dot_general | solution.py:454
  (4 shorter events, 0.0 us)
Async XLA Ops:
  0.0 5.1 %copy-start = (bf16[128,256]{1,0:T(8,128)(2,1)S(1)}, bf16[128,256]{1,0:T(8,128)(2,1)}, u32[]{:S(2)}) copy-start(bf16[128,256]{1,0:T(8,128)(2,1)} %param.6) | copy-start | bytes 196612
  3.1 79.6 %copy-start.2 = (bf16[1,176,2048]{2,1,0:T(8,128)(2,1)S(1)}, bf16[1,176,2048]{2,1,0:T(8,128)(2,1)}, u32[]{:S(2)}) copy-start(bf16[1,176,2048]{2,1,0:T(8,128)(2,1)} %param.9) | copy-start | bytes 2162692
  82.9 3.8 %copy-start.3 = (bf16[1,176,2048]{2,1,0:T(8,128)(2,1)S(1)}, bf16[1,176,2048]{2,1,0:T(8,128)(2,1)}, u32[]{:S(2)}) copy-start(bf16[1,176,2048]{2,1,0:T(8,128)(2,1)} %param.10) | copy-start | bytes 2162692
  82.9 3.9 %copy-start.1 = (bf16[8,64,14,256]{3,2,1,0:T(8,128)(2,1)S(1)}, bf16[8,64,14,256]{3,2,1,0:T(8,128)(2,1)}, u32[]{:S(2)}) copy-start(bf16[8,64,14,256]{3,2,1,0:T(8,128)(2,1)} %shard_map.64) | copy-start | bytes 11010052
  86.9 2.0 %copy-start.4 = (bf16[1,176,2048]{2,1,0:T(8,128)(2,1)S(1)}, bf16[1,176,2048]{2,1,0:T(8,128)(2,1)}, u32[]{:S(2)}) copy-start(bf16[1,176,2048]{2,1,0:T(8,128)(2,1)} %param.11) | copy-start | bytes 2162692
  92.0 80.7 %copy-start.5 = (bf16[128,6]{0,1:T(8,128)(2,1)S(1)}, bf16[128,6]{0,1:T(8,128)(2,1)}, u32[]{:S(2)}) copy-start(bf16[128,6]{0,1:T(8,128)(2,1)} %param.8) | copy-start | bytes 4612

commit v13 on v12

--- a/solution.py
+++ b/solution.py
@@ -289,73 +289,72 @@
     peers = (right, left)
     froms = (left, right)
     offsets = ((3, 2, 1), (1, 2, 3))
-
-    def plane(h, rb, sb, sem):
-        sends = []
-        for d in (0, 1):
-            src = p_ref.at[h * 4 + (xi + offsets[d][0]) % 4, :, cols[d]]
-            c = remote(src, rb.at[d, 0], sem.at[d, 0], peers[d])
+    cap = o_ref.shape[1]
+    own_p = p_ref.at[yh * 4 + xi]
+
+    def wide_copy(hf, k, peer, origin):
+        return pltpu.make_async_remote_copy(
+            src_ref=o_ref.at[peer, :, cols[hf]],
+            dst_ref=r_ref.at[origin, :, cols[hf]],
+            send_sem=sem_w.at[hf, k, 0],
+            recv_sem=sem_w.at[hf, k, 1],
+            device_id=(peer, me),
+            device_id_type=MESH,
+        )
+
+    sends = []
+    owns = []
+    for hf in (0, 1):
+        jobs = ((other, 0), (yh, 1))
+        for j, (h, d) in enumerate(jobs):
+            src = p_ref.at[h * 4 + (xi + offsets[d][0]) % 4, :, cols[hf]]
+            c = remote(src, rp.at[hf, j, 0], sem_p.at[hf, j, 0], peers[d])
             c.start()
             sends.append(c)
         for step in (1, 2):
-            for d in (0, 1):
-                remote(sb.at[d, step - 1], rb.at[d, step - 1], sem.at[d, step - 1], froms[d]).wait_recv()
-                term = p_ref.at[h * 4 + (xi + offsets[d][step]) % 4, :, cols[d]]
-                _add_into(sb.at[d, step - 1], rb.at[d, step - 1], term)
-                c = remote(sb.at[d, step - 1], rb.at[d, step], sem.at[d, step], peers[d])
+            for j, (h, d) in enumerate(jobs):
+                remote(sp.at[hf, j, step - 1], rp.at[hf, j, step - 1], sem_p.at[hf, j, step - 1], froms[d]).wait_recv()
+                term = p_ref.at[h * 4 + (xi + offsets[d][step]) % 4, :, cols[hf]]
+                _add_into(sp.at[hf, j, step - 1], rp.at[hf, j, step - 1], term)
+                c = remote(sp.at[hf, j, step - 1], rp.at[hf, j, step], sem_p.at[hf, j, step], peers[d])
                 c.start()
                 sends.append(c)
-        for d in (0, 1):
-            remote(sb.at[d, 1], rb.at[d, 2], sem.at[d, 2], froms[d]).wait_recv()
-        return sends
-
-    sends = plane(other, rp, sp, sem_p)
-    for d in (0, 1):
-        _add_into(qy.at[:, cols[d]], rp.at[d, 2], p_ref.at[other * 4 + xi, :, cols[d]])
-    c = remote(qy, ry, sem_y, partner)
-    c.start()
-    sends.append(c)
-    sends += plane(yh, rm, sm, sem_m)
-    remote(qy, ry, sem_y, partner).wait_recv()
-    own_p = p_ref.at[yh * 4 + xi]
-    cap = o_ref.shape[1]
-    for b in range(nw):
-        rows = pl.ds(b * cap, cap)
-        for d in (0, 1):
-            total = rm[d, 2, rows, :].astype(jnp.float32) + own_p[rows, cols[d]].astype(jnp.float32)
-            o_ref[b, :, cols[d]] = (total + ry[rows, cols[d]].astype(jnp.float32)).astype(o_ref.dtype)
-    own = pltpu.make_async_copy(o_ref.at[w], r_ref.at[w], own_w)
-    own.start()
-
-    def wide_copy(k, peer, origin):
-        return pltpu.make_async_remote_copy(
-            src_ref=o_ref.at[peer],
-            dst_ref=r_ref.at[origin],
-            send_sem=sem_w.at[k, 0],
-            recv_sem=sem_w.at[k, 1],
-            device_id=(peer, me),
-            device_id_type=MESH,
-        )
-
-    def send_body(k, carry):
-        wide_copy(k, (w + k) % nw, w).start()
-        return carry
-
-    lax.fori_loop(1, nw, send_body, 0)
-
-    def recv_body(k, carry):
-        src = (w + nw - k) % nw
-        wide_copy(k, src, src).wait_recv()
-        return carry
-
-    lax.fori_loop(1, nw, recv_body, 0)
-
-    def sent_body(k, carry):
-        wide_copy(k, (w + k) % nw, w).wait_send()
-        return carry
-
-    lax.fori_loop(1, nw, sent_body, 0)
-    own.wait()
+        remote(sp.at[hf, 0, 1], rp.at[hf, 0, 2], sem_p.at[hf, 0, 2], froms[0]).wait_recv()
+        _add_into(qy.at[hf], rp.at[hf, 0, 2], p_ref.at[other * 4 + xi, :, cols[hf]])
+        c = remote(qy.at[hf], ry.at[hf], sem_y.at[hf], partner)
+        c.start()
+        sends.append(c)
+        remote(sp.at[hf, 1, 1], rp.at[hf, 1, 2], sem_p.at[hf, 1, 2], froms[1]).wait_recv()
+        remote(qy.at[hf], ry.at[hf], sem_y.at[hf], partner).wait_recv()
+        for b in range(nw):
+            rows = pl.ds(b * cap, cap)
+            total = rp[hf, 1, 2, rows, :].astype(jnp.float32) + own_p[rows, cols[hf]].astype(jnp.float32)
+            o_ref[b, :, cols[hf]] = (total + ry[hf, rows, :].astype(jnp.float32)).astype(o_ref.dtype)
+        own = pltpu.make_async_copy(o_ref.at[w, :, cols[hf]], r_ref.at[w, :, cols[hf]], own_w.at[hf])
+        own.start()
+        owns.append(own)
+
+        def send_body(k, carry, hf=hf):
+            wide_copy(hf, k, (w + k) % nw, w).start()
+            return carry
+
+        lax.fori_loop(1, nw, send_body, 0)
+
+    for hf in (0, 1):
+
+        def recv_body(k, carry, hf=hf):
+            src = (w + nw - k) % nw
+            wide_copy(hf, k, src, src).wait_recv()
+            return carry
+
+        lax.fori_loop(1, nw, recv_body, 0)
+
+        def sent_body(k, carry, hf=hf):
+            wide_copy(hf, k, (w + k) % nw, w).wait_send()
+            return carry
+
+        lax.fori_loop(1, nw, sent_body, 0)
+        owns[hf].wait()
     for c in sends:
         c.wait_send()
 
@@ -370,18 +369,18 @@
         in_specs=[pl.BlockSpec(memory_space=pltpu.VMEM)],
         out_specs=pl.BlockSpec(memory_space=pl.ANY),
         scratch_shapes=[
-            pltpu.VMEM((2, 3, one[0], one[1] // 2), p.dtype),
-            pltpu.VMEM((2, 3, one[0], one[1] // 2), p.dtype),
-            pltpu.VMEM((2, 2, one[0], one[1] // 2), p.dtype),
-            pltpu.VMEM((2, 2, one[0], one[1] // 2), p.dtype),
-            block,
-            block,
+            pltpu.VMEM((2, 2, 3, one[0], one[1] // 2), p.dtype),
+            pltpu.VMEM((1,), p.dtype),
+            pltpu.VMEM((2, 2, 2, one[0], one[1] // 2), p.dtype),
+            pltpu.VMEM((1,), p.dtype),
+            pltpu.VMEM((2, one[0], one[1] // 2), p.dtype),
+            pltpu.VMEM((2, one[0], one[1] // 2), p.dtype),
             pltpu.VMEM(blocks, p.dtype),
-            pltpu.SemaphoreType.DMA((2, 3, 2)),
-            pltpu.SemaphoreType.DMA((2, 3, 2)),
+            pltpu.SemaphoreType.DMA((2, 2, 3, 2)),
+            pltpu.SemaphoreType.DMA((1,)),
+            pltpu.SemaphoreType.DMA((2, 2)),
+            pltpu.SemaphoreType.DMA((2, nw, 2)),
             pltpu.SemaphoreType.DMA((2,)),
-            pltpu.SemaphoreType.DMA((nw, 2)),
-            pltpu.SemaphoreType.DMA(()),
         ],
         compiler_params=pltpu.CompilerParams(collective_id=collective_id, has_side_effects=True),
         cost_estimate=pl.CostEstimate(

time: 176 us -> 177 us (level)
  no operation moved by 1% of the time
where the time goes in v13:
time: 177 us; the launch traced here: 176 us
  Pallas kernels  158 us (89%)
  matrix products  10.4 us (6%)
  local copies, waits for them, and re-layouts  4.22 us (2%)
  other arithmetic  3.47 us (2%)
    pallas_call x1, Pallas kernels, _reduce(): pl.pallas_call(_reduce_kernel, out_shape=jax.ShapeDtypeStruct(blocks, p.d...  81.7 us
    pallas_call x1, Pallas kernels, _dispatch(): pl.pallas_call(_dispatch_kernel, out_shape=jax.ShapeDtypeStruct((n_narrow...  76.3 us
    dot_general x1, matrix products, local(): jnp.einsum('nbcd,fnd->bcf', slot_rows, wg, preferred_element_type=jnp.flo...  3.73 us

profile of v13, /device:TPU:1, one launch (start us, length us, event | category | flops | bytes accessed | tf_op | source)
XLA Modules:
  0.0 176.3 jit_solution(17318923855636403248)
XLA Ops:
  0.0 0.0 copy-start
  0.0 0.8 copy.49
  0.8 0.1 eq.42
  1.0 1.8 %reduce-window.6 = s32[64,6,128]{2,0,1:T(8,128)S(1)} reduce-window(s32[64,6,128]{2,0,1:T(8,128)S(1)} %fusion.29, s32[]{:T(128)} %constant.7.clone.1), window={size=1x1x128 pad=0_0x0_0x127_0}, to_apply=%region_0.0 | reduce-window | flops 6242304 | bytes 393220 | tf_op jit(solution)/shard_map/reduce-window
  2.8 0.3 slice_reduce_fusion
  3.1 0.0 copy-start.2
  3.1 0.1 eq.38
  3.2 0.1 fusion.28
  3.4 0.1 sub.7
  3.5 0.1 copy.52
  3.6 0.7 multiply_add_fusion
  4.3 0.4 fusion.4
  4.7 0.3 copy.54
  5.0 0.1 reshape.38
  5.1 0.0 copy-done
  5.1 0.3 convolution_convert_fusion
  5.4 1.1 copy.56.x_ref
  6.4 76.3 %shard_map.64 = bf16[8,64,14,256]{3,2,1,0:T(8,128)(2,1)} custom-call(bf16[64,14,256]{2,1,0:T(8,128)(2,1)} %copy.56.x_ref), custom_call_target="tpu_custom_call" | custom-call | bytes 8257536 | tf_op jit(solution)/shard_map/pallas_call | solution.py:220
  82.7 0.0 copy-done.2
  82.7 0.2 copy.71
  82.9 0.0 copy-start.3
  82.9 0.0 copy-start.1
  82.9 3.7 %fusion.5 = f32[64,14,176]{2,0,1:T(8,128)S(1)} fusion(bf16[8,64,14,256]{3,2,1,0:T(8,128)(2,1)} %shard_map.64, bf16[176,8,256]{2,1,0:T(8,128)(2,1)S(1)} %bitcast.62), kind=kOutput, calls=%fused_computation.8 | convolution fusion | flops 645922816 | bytes 5021696 | tf_op jit(solution)/shard_map/nbcd,fnd->bcf/dot_general | solution.py:446
  86.7 0.0 copy-done.3
  86.7 0.2 copy.72
  86.8 0.0 copy-done.1
  86.9 0.0 copy-start.4
  86.9 1.5 fusion.14
  88.4 0.3 copy.61
  88.6 0.2 reshape.39
  88.9 0.0 copy-done.4
  88.9 0.2 copy.73
  89.1 2.9 %convert_bitcast_fusion.p_ref = bf16[8,896,256]{2,1,0:T(8,128)(2,1)} fusion(bf16[176,8,256]{2,1,0:T(8,128)(2,1)S(1)} %bitcast.57, bf16[896,176]{1,0:T(8,128)(2,1)S(1)} %reshape.39), kind=kOutput, calls=%fused_computation | convolution fusion | flops 647757824 | bytes 4706304 | tf_op jit(solution)/shard_map/sf,fnd->nsd/dot_general | solution.py:449
  92.0 0.0 copy-start.5
  92.0 81.7 %shard_map.65 = bf16[64,14,256]{2,1,0:T(8,128)(2,1)} custom-call(bf16[8,896,256]{2,1,0:T(8,128)(2,1)} %convert_bitcast_fusion.p_ref), custom_call_target="tpu_custom_call" | custom-call | flops 3670016 | bytes 7340032 | tf_op jit(solution)/shard_map/pallas_call | solution.py:366
  173.7 0.0 copy-done.5
  173.7 0.3 select_reduce_fusion
  174.0 0.2 copy.53
  174.2 0.1 convert_element_type.33
  174.3 2.0 %fusion.17 = bf16[128,256]{1,0:T(8,128)(2,1)} fusion(bf16[64,14,256]{2,1,0:T(8,128)(2,1)} %shard_map.65, bf16[128,64,14]{0,2,1:T(8,128)(2,1)S(1)} %convert_element_type.33), kind=kOutput, calls=%fused_computation.14 | convolution fusion | flops 58753024 | bytes 753664 | tf_op jit(solution)/shard_map/tbc,bcd->td/dot_general | solution.py:453
  (4 shorter events, 0.0 us)
Async XLA Ops:
  0.0 5.1 %copy-start = (bf16[128,256]{1,0:T(8,128)(2,1)S(1)}, bf16[128,256]{1,0:T(8,128)(2,1)}, u32[]{:S(2)}) copy-start(bf16[128,256]{1,0:T(8,128)(2,1)} %param.6) | copy-start | bytes 196612
  3.1 79.6 %copy-start.2 = (bf16[1,176,2048]{2,1,0:T(8,128)(2,1)S(1)}, bf16[1,176,2048]{2,1,0:T(8,128)(2,1)}, u32[]{:S(2)}) copy-start(bf16[1,176,2048]{2,1,0:T(8,128)(2,1)} %param.9) | copy-start | bytes 2162692
  82.9 3.8 %copy-start.3 = (bf16[1,176,2048]{2,1,0:T(8,128)(2,1)S(1)}, bf16[1,176,2048]{2,1,0:T(8,128)(2,1)}, u32[]{:S(2)}) copy-start(bf16[1,176,2048]{2,1,0:T(8,128)(2,1)} %param.10) | copy-start | bytes 2162692
  82.9 3.9 %copy-start.1 = (bf16[8,64,14,256]{3,2,1,0:T(8,128)(2,1)S(1)}, bf16[8,64,14,256]{3,2,1,0:T(8,128)(2,1)}, u32[]{:S(2)}) copy-start(bf16[8,64,14,256]{3,2,1,0:T(8,128)(2,1)} %shard_map.64) | copy-start | bytes 11010052
  86.9 2.0 %copy-start.4 = (bf16[1,176,2048]{2,1,0:T(8,128)(2,1)S(1)}, bf16[1,176,2048]{2,1,0:T(8,128)(2,1)}, u32[]{:S(2)}) copy-start(bf16[1,176,2048]{2,1,0:T(8,128)(2,1)} %param.11) | copy-start | bytes 2162692
  92.0 81.7 %copy-start.5 = (bf16[128,6]{0,1:T(8,128)(2,1)S(1)}, bf16[128,6]{0,1:T(8,128)(2,1)}, u32[]{:S(2)}) copy-start(bf16[128,6]{0,1:T(8,128)(2,1)} %param.8) | copy-start | bytes 4612

commit v14 on v12

--- a/solution.py
+++ b/solution.py
@@ -83,8 +83,6 @@
     ]
     for c in c1:
         c.start()
-    if after_start is not None:
-        after_start()
     remote(x_ref, partner, (sem_y.at[0], sem_y.at[1]), partner).wait_recv()
     c2 = [
         remote(y_ref.at[partner], partner, (sem_x1.at[2, 0], sem_x1.at[2, 1]), right),
@@ -92,6 +90,8 @@
     ]
     for c in c2:
         c.start()
+    if after_start is not None:
+        after_start()
     lp = (1 - yh) * 4 + (xi + 3) % 4
     rp = (1 - yh) * 4 + (xi + 1) % 4
     remote(x_ref, left, (sem_x1.at[0, 0], sem_x1.at[0, 1]), left).wait_recv()

time: 176 us -> 176 us (level)
    pallas_call x1, Pallas kernels: 76.3 us -> 84.9 us  [_dispatch(): pl.pallas_call(_dispatch_kernel, out_shape=jax.ShapeDtypeStruct((n_narrow...]
    pallas_call x1, Pallas kernels: 80.7 us -> 72.5 us  [_reduce(): pl.pallas_call(_reduce_kernel, out_shape=jax.ShapeDtypeStruct(blocks, p.d...]
where the time goes in v14:
time: 176 us
  Pallas kernels  157 us (89%)
  matrix products  10.4 us (6%)
  local copies, waits for them, and re-layouts  4.22 us (2%)
  other arithmetic  3.47 us (2%)
    pallas_call x1, Pallas kernels, _dispatch(): pl.pallas_call(_dispatch_kernel, out_shape=jax.ShapeDtypeStruct((n_narrow...  84.9 us
    pallas_call x1, Pallas kernels, _reduce(): pl.pallas_call(_reduce_kernel, out_shape=jax.ShapeDtypeStruct(blocks, p.d...  72.5 us
    dot_general x1, matrix products, local(): jnp.einsum('nbcd,fnd->bcf', slot_rows, wg, preferred_element_type=jnp.flo...  3.73 us

profile of v14, /device:TPU:1, one launch (start us, length us, event | category | flops | bytes accessed | tf_op | source)
XLA Modules:
  0.0 175.7 jit_solution(911006946956640267)
XLA Ops:
  0.0 0.0 copy-start
  0.0 0.8 copy.49
  0.8 0.1 eq.42
  1.0 1.8 %reduce-window.6 = s32[64,6,128]{2,0,1:T(8,128)S(1)} reduce-window(s32[64,6,128]{2,0,1:T(8,128)S(1)} %fusion.29, s32[]{:T(128)} %constant.7.clone.1), window={size=1x1x128 pad=0_0x0_0x127_0}, to_apply=%region_0.0 | reduce-window | flops 6242304 | bytes 393220 | tf_op jit(solution)/shard_map/reduce-window
  2.8 0.3 slice_reduce_fusion
  3.1 0.0 copy-start.2
  3.1 0.1 eq.38
  3.2 0.1 fusion.28
  3.4 0.1 sub.7
  3.5 0.1 copy.52
  3.6 0.7 multiply_add_fusion
  4.3 0.4 fusion.4
  4.7 0.3 copy.54
  5.0 0.1 reshape.38
  5.1 0.0 copy-done
  5.1 0.3 convolution_convert_fusion
  5.4 1.1 copy.56.x_ref
  6.4 84.9 %shard_map.64 = bf16[8,64,14,256]{3,2,1,0:T(8,128)(2,1)} custom-call(bf16[64,14,256]{2,1,0:T(8,128)(2,1)} %copy.56.x_ref), custom_call_target="tpu_custom_call" | custom-call | bytes 8257536 | tf_op jit(solution)/shard_map/pallas_call | solution.py:220
  91.3 0.0 copy-done.2
  91.3 0.2 copy.71
  91.5 0.0 copy-start.3
  91.5 0.0 copy-start.1
  91.5 3.7 %fusion.5 = f32[64,14,176]{2,0,1:T(8,128)S(1)} fusion(bf16[8,64,14,256]{3,2,1,0:T(8,128)(2,1)} %shard_map.64, bf16[176,8,256]{2,1,0:T(8,128)(2,1)S(1)} %bitcast.62), kind=kOutput, calls=%fused_computation.8 | convolution fusion | flops 645922816 | bytes 5021696 | tf_op jit(solution)/shard_map/nbcd,fnd->bcf/dot_general | solution.py:447
  95.2 0.0 copy-done.3
  95.2 0.2 copy.72
  95.4 0.0 copy-done.1
  95.4 0.0 copy-start.4
  95.5 1.5 fusion.14
  97.0 0.3 copy.61
  97.2 0.2 reshape.39
  97.5 0.0 copy-done.4
  97.5 0.2 copy.73
  97.6 2.9 %convert_bitcast_fusion.p_ref = bf16[8,896,256]{2,1,0:T(8,128)(2,1)} fusion(bf16[176,8,256]{2,1,0:T(8,128)(2,1)S(1)} %bitcast.57, bf16[896,176]{1,0:T(8,128)(2,1)S(1)} %reshape.39), kind=kOutput, calls=%fused_computation | convolution fusion | flops 647757824 | bytes 4706304 | tf_op jit(solution)/shard_map/sf,fnd->nsd/dot_general | solution.py:450
  100.6 0.0 copy-start.5
  100.6 72.5 %shard_map.65 = bf16[64,14,256]{2,1,0:T(8,128)(2,1)} custom-call(bf16[8,896,256]{2,1,0:T(8,128)(2,1)} %convert_bitcast_fusion.p_ref), custom_call_target="tpu_custom_call" | custom-call | flops 3670016 | bytes 7340032 | tf_op jit(solution)/shard_map/pallas_call | solution.py:367
  173.1 0.0 copy-done.5
  173.1 0.3 select_reduce_fusion
  173.5 0.2 copy.53
  173.6 0.1 convert_element_type.33
  173.7 2.0 %fusion.17 = bf16[128,256]{1,0:T(8,128)(2,1)} fusion(bf16[64,14,256]{2,1,0:T(8,128)(2,1)} %shard_map.65, bf16[128,64,14]{0,2,1:T(8,128)(2,1)S(1)} %convert_element_type.33), kind=kOutput, calls=%fused_computation.14 | convolution fusion | flops 58753024 | bytes 753664 | tf_op jit(solution)/shard_map/tbc,bcd->td/dot_general | solution.py:454
  (4 shorter events, 0.0 us)
Async XLA Ops:
  0.0 5.1 %copy-start = (bf16[128,256]{1,0:T(8,128)(2,1)S(1)}, bf16[128,256]{1,0:T(8,128)(2,1)}, u32[]{:S(2)}) copy-start(bf16[128,256]{1,0:T(8,128)(2,1)} %param.6) | copy-start | bytes 196612
  3.1 88.2 %copy-start.2 = (bf16[1,176,2048]{2,1,0:T(8,128)(2,1)S(1)}, bf16[1,176,2048]{2,1,0:T(8,128)(2,1)}, u32[]{:S(2)}) copy-start(bf16[1,176,2048]{2,1,0:T(8,128)(2,1)} %param.9) | copy-start | bytes 2162692
  91.5 3.8 %copy-start.3 = (bf16[1,176,2048]{2,1,0:T(8,128)(2,1)S(1)}, bf16[1,176,2048]{2,1,0:T(8,128)(2,1)}, u32[]{:S(2)}) copy-start(bf16[1,176,2048]{2,1,0:T(8,128)(2,1)} %param.10) | copy-start | bytes 2162692
  91.5 3.9 %copy-start.1 = (bf16[8,64,14,256]{3,2,1,0:T(8,128)(2,1)S(1)}, bf16[8,64,14,256]{3,2,1,0:T(8,128)(2,1)}, u32[]{:S(2)}) copy-start(bf16[8,64,14,256]{3,2,1,0:T(8,128)(2,1)} %shard_map.64) | copy-start | bytes 11010052
  95.4 2.0 %copy-start.4 = (bf16[1,176,2048]{2,1,0:T(8,128)(2,1)S(1)}, bf16[1,176,2048]{2,1,0:T(8,128)(2,1)}, u32[]{:S(2)}) copy-start(bf16[1,176,2048]{2,1,0:T(8,128)(2,1)} %param.11) | copy-start | bytes 2162692
  100.6 72.5 %copy-start.5 = (bf16[128,6]{0,1:T(8,128)(2,1)S(1)}, bf16[128,6]{0,1:T(8,128)(2,1)}, u32[]{:S(2)}) copy-start(bf16[128,6]{0,1:T(8,128)(2,1)} %param.8) | copy-start | bytes 4612

commit v15 on v12

--- a/solution.py
+++ b/solution.py
@@ -425,8 +425,11 @@
     onehot = (flat_ids[:, None] == jnp.arange(experts_all, dtype=jnp.int32)[None, :]).astype(
         jnp.int32
     )
-    running = jnp.cumsum(onehot, axis=0)
-    slot_index = jnp.sum(running * onehot, axis=1) - 1
+    pairs = flat_ids.shape[0]
+    order = jnp.arange(pairs, dtype=jnp.int32)
+    lower = (order[:, None] >= order[None, :]).astype(jnp.bfloat16)
+    running = jnp.dot(lower, onehot.astype(jnp.bfloat16), preferred_element_type=jnp.float32)
+    slot_index = jnp.sum(running * onehot, axis=1).astype(jnp.int32) - 1
     destination = (flat_ids * capacity + slot_index).reshape(tok_rows, top_count)
     hit = destination[:, :, None] == jnp.arange(slots_all, dtype=jnp.int32)[None, None, :]
     dispatch = jnp.any(hit, axis=1).astype(jnp.bfloat16)

time: 176 us -> 173 us (0.983)
  other arithmetic: 3.47 us -> 1.5 us
    another operation x2 -> x0, other arithmetic: 1.82 us -> none
where the time goes in v15:
time: 173 us
  Pallas kernels  157 us (91%)
  matrix products  10.8 us (6%)
  local copies, waits for them, and re-layouts  3.81 us (2%)
    pallas_call x1, Pallas kernels, _reduce(): pl.pallas_call(_reduce_kernel, out_shape=jax.ShapeDtypeStruct(blocks, p.d...  80.4 us
    pallas_call x1, Pallas kernels, _dispatch(): pl.pallas_call(_dispatch_kernel, out_shape=jax.ShapeDtypeStruct((n_narrow...  76.5 us
    dot_general x1, matrix products, local(): jnp.einsum('nbcd,fnd->bcf', slot_rows, wg, preferred_element_type=jnp.flo...  3.73 us

profile of v15, /device:TPU:1, one launch (start us, length us, event | category | flops | bytes accessed | tf_op | source)
XLA Modules:
  0.0 173.2 jit_solution(18293481998110171520)
XLA Ops:
  0.0 0.0 copy-start
  0.0 0.8 copy.45
  0.8 0.1 eq.28
  1.0 0.4 fusion.19
  1.4 0.0 copy-start.2
  1.4 0.1 sub.7
  1.5 0.1 copy.46
  1.6 0.7 multiply_add_fusion
  2.3 0.4 fusion.4
  2.7 0.3 copy.48
  3.0 0.1 reshape.23
  3.1 0.0 copy-done
  3.1 0.3 convolution_convert_fusion
  3.4 1.1 copy.50.x_ref
  4.4 76.5 %shard_map.64 = bf16[8,64,14,256]{3,2,1,0:T(8,128)(2,1)} custom-call(bf16[64,14,256]{2,1,0:T(8,128)(2,1)} %copy.50.x_ref), custom_call_target="tpu_custom_call" | custom-call | bytes 8257536 | tf_op jit(solution)/shard_map/pallas_call | solution.py:220
  80.9 0.0 copy-done.2
  80.9 0.2 copy.64
  81.1 0.0 copy-start.3
  81.1 0.0 copy-start.1
  81.1 3.7 %fusion.6 = f32[64,14,176]{2,0,1:T(8,128)S(1)} fusion(bf16[8,64,14,256]{3,2,1,0:T(8,128)(2,1)} %shard_map.64, bf16[176,8,256]{2,1,0:T(8,128)(2,1)S(1)} %bitcast.46), kind=kOutput, calls=%fused_computation.10 | convolution fusion | flops 645922816 | bytes 5021696 | tf_op jit(solution)/shard_map/nbcd,fnd->bcf/dot_general | solution.py:450
  84.9 0.0 copy-done.3
  84.9 0.2 copy.65
  85.1 0.0 copy-done.1
  85.1 0.0 copy-start.4
  85.1 1.5 fusion.15
  86.6 0.3 copy.55
  86.9 0.2 reshape.24
  87.1 0.0 copy-done.4
  87.1 0.2 copy.66
  87.3 2.9 %convert_bitcast_fusion.p_ref = bf16[8,896,256]{2,1,0:T(8,128)(2,1)} fusion(bf16[176,8,256]{2,1,0:T(8,128)(2,1)S(1)} %bitcast.41, bf16[896,176]{1,0:T(8,128)(2,1)S(1)} %reshape.24), kind=kOutput, calls=%fused_computation | convolution fusion | flops 647757824 | bytes 4706304 | tf_op jit(solution)/shard_map/sf,fnd->nsd/dot_general | solution.py:453
  90.2 0.0 copy-start.5
  90.2 80.4 %shard_map.65 = bf16[64,14,256]{2,1,0:T(8,128)(2,1)} custom-call(bf16[8,896,256]{2,1,0:T(8,128)(2,1)} %convert_bitcast_fusion.p_ref), custom_call_target="tpu_custom_call" | custom-call | flops 3670016 | bytes 7340032 | tf_op jit(solution)/shard_map/pallas_call | solution.py:367
  170.6 0.0 copy-done.5
  170.6 0.3 select_reduce_fusion
  170.9 0.2 copy.47
  171.1 0.1 convert_element_type.47
  171.2 2.0 %fusion.20 = bf16[128,256]{1,0:T(8,128)(2,1)} fusion(bf16[64,14,256]{2,1,0:T(8,128)(2,1)} %shard_map.65, bf16[128,64,14]{0,2,1:T(8,128)(2,1)S(1)} %convert_element_type.47), kind=kOutput, calls=%fused_computation.18 | convolution fusion | flops 58753024 | bytes 753664 | tf_op jit(solution)/shard_map/tbc,bcd->td/dot_general | solution.py:457
  (2 shorter events, 0.0 us)
Async XLA Ops:
  0.0 3.1 %copy-start = (bf16[128,256]{1,0:T(8,128)(2,1)S(1)}, bf16[128,256]{1,0:T(8,128)(2,1)}, u32[]{:S(2)}) copy-start(bf16[128,256]{1,0:T(8,128)(2,1)} %param.6) | copy-start | bytes 196612
  1.4 79.6 %copy-start.2 = (bf16[1,176,2048]{2,1,0:T(8,128)(2,1)S(1)}, bf16[1,176,2048]{2,1,0:T(8,128)(2,1)}, u32[]{:S(2)}) copy-start(bf16[1,176,2048]{2,1,0:T(8,128)(2,1)} %param.9) | copy-start | bytes 2162692
  81.1 3.8 %copy-start.3 = (bf16[1,176,2048]{2,1,0:T(8,128)(2,1)S(1)}, bf16[1,176,2048]{2,1,0:T(8,128)(2,1)}, u32[]{:S(2)}) copy-start(bf16[1,176,2048]{2,1,0:T(8,128)(2,1)} %param.10) | copy-start | bytes 2162692
  81.1 3.9 %copy-start.1 = (bf16[8,64,14,256]{3,2,1,0:T(8,128)(2,1)S(1)}, bf16[8,64,14,256]{3,2,1,0:T(8,128)(2,1)}, u32[]{:S(2)}) copy-start(bf16[8,64,14,256]{3,2,1,0:T(8,128)(2,1)} %shard_map.64) | copy-start | bytes 11010052
  85.1 2.0 %copy-start.4 = (bf16[1,176,2048]{2,1,0:T(8,128)(2,1)S(1)}, bf16[1,176,2048]{2,1,0:T(8,128)(2,1)}, u32[]{:S(2)}) copy-start(bf16[1,176,2048]{2,1,0:T(8,128)(2,1)} %param.11) | copy-start | bytes 2162692
  90.2 80.4 %copy-start.5 = (bf16[128,6]{0,1:T(8,128)(2,1)S(1)}, bf16[128,6]{0,1:T(8,128)(2,1)}, u32[]{:S(2)}) copy-start(bf16[128,6]{0,1:T(8,128)(2,1)} %param.8) | copy-start | bytes 4612

commit v16 on v15

--- a/solution.py
+++ b/solution.py
@@ -290,13 +290,17 @@
     froms = (left, right)
     offsets = ((3, 2, 1), (1, 2, 3))
 
-    def plane(h, rb, sb, sem):
+    def first(h, rb, sem):
         sends = []
         for d in (0, 1):
             src = p_ref.at[h * 4 + (xi + offsets[d][0]) % 4, :, cols[d]]
             c = remote(src, rb.at[d, 0], sem.at[d, 0], peers[d])
             c.start()
             sends.append(c)
+        return sends
+
+    def plane(h, rb, sb, sem):
+        sends = []
         for step in (1, 2):
             for d in (0, 1):
                 remote(sb.at[d, step - 1], rb.at[d, step - 1], sem.at[d, step - 1], froms[d]).wait_recv()
@@ -309,7 +313,8 @@
             remote(sb.at[d, 1], rb.at[d, 2], sem.at[d, 2], froms[d]).wait_recv()
         return sends
 
-    sends = plane(other, rp, sp, sem_p)
+    sends = first(other, rp, sem_p) + first(yh, rm, sem_m)
+    sends += plane(other, rp, sp, sem_p)
     for d in (0, 1):
         _add_into(qy.at[:, cols[d]], rp.at[d, 2], p_ref.at[other * 4 + xi, :, cols[d]])
     c = remote(qy, ry, sem_y, partner)

time: 173 us -> 172 us (level)
  Pallas kernels: 157 us -> 155 us
    pallas_call x1, Pallas kernels: 80.4 us -> 78.5 us  [_reduce(): pl.pallas_call(_reduce_kernel, out_shape=jax.ShapeDtypeStruct(blocks, p.d...]
where the time goes in v16:
time: 172 us; the launch traced here: 171 us
  Pallas kernels  155 us (90%)
  matrix products  10.8 us (6%)
  local copies, waits for them, and re-layouts  3.81 us (2%)
    pallas_call x1, Pallas kernels, _reduce(): pl.pallas_call(_reduce_kernel, out_shape=jax.ShapeDtypeStruct(blocks, p.d...  78.5 us
    pallas_call x1, Pallas kernels, _dispatch(): pl.pallas_call(_dispatch_kernel, out_shape=jax.ShapeDtypeStruct((n_narrow...  76.5 us
    dot_general x1, matrix products, local(): jnp.einsum('nbcd,fnd->bcf', slot_rows, wg, preferred_element_type=jnp.flo...  3.73 us

profile of v16, /device:TPU:1, one launch (start us, length us, event | category | flops | bytes accessed | tf_op | source)
XLA Modules:
  0.0 171.3 jit_solution(8406987331053597535)
XLA Ops:
  0.0 0.0 copy-start
  0.0 0.8 copy.45
  0.8 0.1 eq.28
  1.0 0.4 fusion.19
  1.4 0.0 copy-start.2
  1.4 0.1 sub.7
  1.5 0.1 copy.46
  1.6 0.7 multiply_add_fusion
  2.3 0.4 fusion.4
  2.7 0.3 copy.48
  3.0 0.1 reshape.23
  3.1 0.0 copy-done
  3.1 0.3 convolution_convert_fusion
  3.4 1.1 copy.50.x_ref
  4.4 76.5 %shard_map.64 = bf16[8,64,14,256]{3,2,1,0:T(8,128)(2,1)} custom-call(bf16[64,14,256]{2,1,0:T(8,128)(2,1)} %copy.50.x_ref), custom_call_target="tpu_custom_call" | custom-call | bytes 8257536 | tf_op jit(solution)/shard_map/pallas_call | solution.py:220
  80.9 0.0 copy-done.2
  80.9 0.2 copy.64
  81.1 0.0 copy-start.3
  81.1 0.0 copy-start.1
  81.1 3.7 %fusion.6 = f32[64,14,176]{2,0,1:T(8,128)S(1)} fusion(bf16[8,64,14,256]{3,2,1,0:T(8,128)(2,1)} %shard_map.64, bf16[176,8,256]{2,1,0:T(8,128)(2,1)S(1)} %bitcast.46), kind=kOutput, calls=%fused_computation.10 | convolution fusion | flops 645922816 | bytes 5021696 | tf_op jit(solution)/shard_map/nbcd,fnd->bcf/dot_general | solution.py:455
  84.9 0.0 copy-done.3
  84.9 0.2 copy.65
  85.1 0.0 copy-done.1
  85.1 0.0 copy-start.4
  85.1 1.5 fusion.15
  86.6 0.3 copy.55
  86.9 0.2 reshape.24
  87.1 0.0 copy-done.4
  87.1 0.2 copy.66
  87.3 2.9 %convert_bitcast_fusion.p_ref = bf16[8,896,256]{2,1,0:T(8,128)(2,1)} fusion(bf16[176,8,256]{2,1,0:T(8,128)(2,1)S(1)} %bitcast.41, bf16[896,176]{1,0:T(8,128)(2,1)S(1)} %reshape.24), kind=kOutput, calls=%fused_computation | convolution fusion | flops 647757824 | bytes 4706304 | tf_op jit(solution)/shard_map/sf,fnd->nsd/dot_general | solution.py:458
  90.2 0.0 copy-start.5
  90.2 78.5 %shard_map.65 = bf16[64,14,256]{2,1,0:T(8,128)(2,1)} custom-call(bf16[8,896,256]{2,1,0:T(8,128)(2,1)} %convert_bitcast_fusion.p_ref), custom_call_target="tpu_custom_call" | custom-call | flops 3670016 | bytes 7340032 | tf_op jit(solution)/shard_map/pallas_call | solution.py:372
  168.7 0.0 copy-done.5
  168.7 0.3 select_reduce_fusion
  169.1 0.2 copy.47
  169.3 0.1 convert_element_type.47
  169.3 2.0 %fusion.20 = bf16[128,256]{1,0:T(8,128)(2,1)} fusion(bf16[64,14,256]{2,1,0:T(8,128)(2,1)} %shard_map.65, bf16[128,64,14]{0,2,1:T(8,128)(2,1)S(1)} %convert_element_type.47), kind=kOutput, calls=%fused_computation.18 | convolution fusion | flops 58753024 | bytes 753664 | tf_op jit(solution)/shard_map/tbc,bcd->td/dot_general | solution.py:462
  (2 shorter events, 0.0 us)
Async XLA Ops:
  0.0 3.1 %copy-start = (bf16[128,256]{1,0:T(8,128)(2,1)S(1)}, bf16[128,256]{1,0:T(8,128)(2,1)}, u32[]{:S(2)}) copy-start(bf16[128,256]{1,0:T(8,128)(2,1)} %param.6) | copy-start | bytes 196612
  1.4 79.6 %copy-start.2 = (bf16[1,176,2048]{2,1,0:T(8,128)(2,1)S(1)}, bf16[1,176,2048]{2,1,0:T(8,128)(2,1)}, u32[]{:S(2)}) copy-start(bf16[1,176,2048]{2,1,0:T(8,128)(2,1)} %param.9) | copy-start | bytes 2162692
  81.1 3.8 %copy-start.3 = (bf16[1,176,2048]{2,1,0:T(8,128)(2,1)S(1)}, bf16[1,176,2048]{2,1,0:T(8,128)(2,1)}, u32[]{:S(2)}) copy-start(bf16[1,176,2048]{2,1,0:T(8,128)(2,1)} %param.10) | copy-start | bytes 2162692
  81.1 3.9 %copy-start.1 = (bf16[8,64,14,256]{3,2,1,0:T(8,128)(2,1)S(1)}, bf16[8,64,14,256]{3,2,1,0:T(8,128)(2,1)}, u32[]{:S(2)}) copy-start(bf16[8,64,14,256]{3,2,1,0:T(8,128)(2,1)} %shard_map.64) | copy-start | bytes 11010052
  85.1 2.0 %copy-start.4 = (bf16[1,176,2048]{2,1,0:T(8,128)(2,1)S(1)}, bf16[1,176,2048]{2,1,0:T(8,128)(2,1)}, u32[]{:S(2)}) copy-start(bf16[1,176,2048]{2,1,0:T(8,128)(2,1)} %param.11) | copy-start | bytes 2162692
  90.2 78.5 %copy-start.5 = (bf16[128,6]{0,1:T(8,128)(2,1)S(1)}, bf16[128,6]{0,1:T(8,128)(2,1)}, u32[]{:S(2)}) copy-start(bf16[128,6]{0,1:T(8,128)(2,1)} %param.8) | copy-start | bytes 4612

commit v17 on v16

--- a/solution.py
+++ b/solution.py
@@ -324,13 +324,6 @@
     remote(qy, ry, sem_y, partner).wait_recv()
     own_p = p_ref.at[yh * 4 + xi]
     cap = o_ref.shape[1]
-    for b in range(nw):
-        rows = pl.ds(b * cap, cap)
-        for d in (0, 1):
-            total = rm[d, 2, rows, :].astype(jnp.float32) + own_p[rows, cols[d]].astype(jnp.float32)
-            o_ref[b, :, cols[d]] = (total + ry[rows, cols[d]].astype(jnp.float32)).astype(o_ref.dtype)
-    own = pltpu.make_async_copy(o_ref.at[w], r_ref.at[w], own_w)
-    own.start()
 
     def wide_copy(k, peer, origin):
         return pltpu.make_async_remote_copy(
@@ -342,11 +335,18 @@
             device_id_type=MESH,
         )
 
-    def send_body(k, carry):
-        wide_copy(k, (w + k) % nw, w).start()
-        return carry
-
-    lax.fori_loop(1, nw, send_body, 0)
+    for b in range(nw):
+        rows = pl.ds(b * cap, cap)
+        for d in (0, 1):
+            total = rm[d, 2, rows, :].astype(jnp.float32) + own_p[rows, cols[d]].astype(jnp.float32)
+            o_ref[b, :, cols[d]] = (total + ry[rows, cols[d]].astype(jnp.float32)).astype(o_ref.dtype)
+
+        @pl.when(w != b)
+        def _(b=b):
+            wide_copy((b + nw - w) % nw, b, w).start()
+
+    own = pltpu.make_async_copy(o_ref.at[w], r_ref.at[w], own_w)
+    own.start()
 
     def recv_body(k, carry):
         src = (w + nw - k) % nw

time: 172 us -> 168 us (0.977)
  the two profiles are of different devices: /device:TPU:1 before, /device:TPU:137 now
where the time goes in v17:
time: 168 us
  Pallas kernels  151 us (90%)
  matrix products  10.8 us (6%)
  local copies, waits for them, and re-layouts  3.81 us (2%)
    pallas_call x1, Pallas kernels, _reduce(): pl.pallas_call(_reduce_kernel, out_shape=jax.ShapeDtypeStruct(blocks, p.d...  81 us
    pallas_call x1, Pallas kernels, _dispatch(): pl.pallas_call(_dispatch_kernel, out_shape=jax.ShapeDtypeStruct((n_narrow...  70.1 us
    dot_general x1, matrix products, local(): jnp.einsum('nbcd,fnd->bcf', slot_rows, wg, preferred_element_type=jnp.flo...  3.73 us

profile of v17, /device:TPU:137, one launch (start us, length us, event | category | flops | bytes accessed | tf_op | source)
XLA Modules:
  0.0 167.5 jit_solution(15023979591001051684)
XLA Ops:
  0.0 0.0 copy-start
  0.0 0.8 copy.45
  0.8 0.1 eq.28
  1.0 0.4 fusion.19
  1.4 0.0 copy-start.2
  1.4 0.1 sub.7
  1.5 0.1 copy.46
  1.6 0.7 multiply_add_fusion
  2.3 0.4 fusion.4
  2.7 0.3 copy.48
  3.0 0.1 reshape.23
  3.1 0.0 copy-done
  3.1 0.3 convolution_convert_fusion
  3.4 1.1 copy.50.x_ref
  4.4 70.1 %shard_map.64 = bf16[8,64,14,256]{3,2,1,0:T(8,128)(2,1)} custom-call(bf16[64,14,256]{2,1,0:T(8,128)(2,1)} %copy.50.x_ref), custom_call_target="tpu_custom_call" | custom-call | bytes 8257536 | tf_op jit(solution)/shard_map/pallas_call | solution.py:220
  74.6 0.0 copy-done.2
  74.6 0.2 copy.64
  74.7 0.0 copy-start.3
  74.8 0.0 copy-start.1
  74.8 3.7 %fusion.6 = f32[64,14,176]{2,0,1:T(8,128)S(1)} fusion(bf16[8,64,14,256]{3,2,1,0:T(8,128)(2,1)} %shard_map.64, bf16[176,8,256]{2,1,0:T(8,128)(2,1)S(1)} %bitcast.46), kind=kOutput, calls=%fused_computation.10 | convolution fusion | flops 645922816 | bytes 5021696 | tf_op jit(solution)/shard_map/nbcd,fnd->bcf/dot_general | solution.py:455
  78.5 0.0 copy-done.3
  78.5 0.2 copy.65
  78.7 0.0 copy-done.1
  78.7 0.0 copy-start.4
  78.7 1.5 fusion.15
  80.2 0.3 copy.55
  80.5 0.2 reshape.24
  80.7 0.0 copy-done.4
  80.7 0.2 copy.66
  80.9 2.9 %convert_bitcast_fusion.p_ref = bf16[8,896,256]{2,1,0:T(8,128)(2,1)} fusion(bf16[176,8,256]{2,1,0:T(8,128)(2,1)S(1)} %bitcast.41, bf16[896,176]{1,0:T(8,128)(2,1)S(1)} %reshape.24), kind=kOutput, calls=%fused_computation | convolution fusion | flops 647757824 | bytes 4706304 | tf_op jit(solution)/shard_map/sf,fnd->nsd/dot_general | solution.py:458
  83.8 0.0 copy-start.5
  83.8 81.0 %shard_map.65 = bf16[64,14,256]{2,1,0:T(8,128)(2,1)} custom-call(bf16[8,896,256]{2,1,0:T(8,128)(2,1)} %convert_bitcast_fusion.p_ref), custom_call_target="tpu_custom_call" | custom-call | flops 3670016 | bytes 7340032 | tf_op jit(solution)/shard_map/pallas_call | solution.py:372
  164.9 0.0 copy-done.5
  164.9 0.3 select_reduce_fusion
  165.2 0.2 copy.47
  165.4 0.1 convert_element_type.47
  165.5 2.0 %fusion.20 = bf16[128,256]{1,0:T(8,128)(2,1)} fusion(bf16[64,14,256]{2,1,0:T(8,128)(2,1)} %shard_map.65, bf16[128,64,14]{0,2,1:T(8,128)(2,1)S(1)} %convert_element_type.47), kind=kOutput, calls=%fused_computation.18 | convolution fusion | flops 58753024 | bytes 753664 | tf_op jit(solution)/shard_map/tbc,bcd->td/dot_general | solution.py:462
  (2 shorter events, 0.0 us)
Async XLA Ops:
  0.0 3.1 %copy-start = (bf16[128,256]{1,0:T(8,128)(2,1)S(1)}, bf16[128,256]{1,0:T(8,128)(2,1)}, u32[]{:S(2)}) copy-start(bf16[128,256]{1,0:T(8,128)(2,1)} %param.6) | copy-start | bytes 196612
  1.4 73.2 %copy-start.2 = (bf16[1,176,2048]{2,1,0:T(8,128)(2,1)S(1)}, bf16[1,176,2048]{2,1,0:T(8,128)(2,1)}, u32[]{:S(2)}) copy-start(bf16[1,176,2048]{2,1,0:T(8,128)(2,1)} %param.9) | copy-start | bytes 2162692
  74.7 3.8 %copy-start.3 = (bf16[1,176,2048]{2,1,0:T(8,128)(2,1)S(1)}, bf16[1,176,2048]{2,1,0:T(8,128)(2,1)}, u32[]{:S(2)}) copy-start(bf16[1,176,2048]{2,1,0:T(8,128)(2,1)} %param.10) | copy-start | bytes 2162692
  74.8 3.9 %copy-start.1 = (bf16[8,64,14,256]{3,2,1,0:T(8,128)(2,1)S(1)}, bf16[8,64,14,256]{3,2,1,0:T(8,128)(2,1)}, u32[]{:S(2)}) copy-start(bf16[8,64,14,256]{3,2,1,0:T(8,128)(2,1)} %shard_map.64) | copy-start | bytes 11010052
  78.7 2.0 %copy-start.4 = (bf16[1,176,2048]{2,1,0:T(8,128)(2,1)S(1)}, bf16[1,176,2048]{2,1,0:T(8,128)(2,1)}, u32[]{:S(2)}) copy-start(bf16[1,176,2048]{2,1,0:T(8,128)(2,1)} %param.11) | copy-start | bytes 2162692
  83.8 81.0 %copy-start.5 = (bf16[128,6]{0,1:T(8,128)(2,1)S(1)}, bf16[128,6]{0,1:T(8,128)(2,1)}, u32[]{:S(2)}) copy-start(bf16[128,6]{0,1:T(8,128)(2,1)} %param.8) | copy-start | bytes 4612
